TPU v7x, 128 devices: a whole 4x4x4 slice. The times are simulated.
128 devices in a mesh: grp: 4 (over y), ffn: 32 (over x, z, core).
Axes of the slice: x: 4, y: 4, z: 4, core: 2. Of those that a mesh axis runs over, the one named last changes fastest.
Arguments:
- layer_input: bfloat16 [288, 5120], P(None, 'ffn')
- norm_gain: float32 [5120], P('ffn'), may hold values from 0.1 to 1.9
- qkv_weight: bfloat16 [3, 5120, 2560], P(None, 'ffn', 'grp'), may hold values from -0.078125 to 0.078125
- key_cache: bfloat16 [896, 128, 2560], P('ffn', None, 'grp'), may hold values from -256 to 256
- value_cache: bfloat16 [896, 128, 2560], P('ffn', None, 'grp'), may hold values from -4 to 4
- out_weight: bfloat16 [2560, 5120], P('grp', 'ffn'), may hold values from -0.125 to 0.125
- ffn_gain: float32 [5120], replicated, may hold values from 0.1 to 1.9
- gate_up_weight: bfloat16 [2, 5120, 13824], P(None, None, 'ffn'), may hold values from -0.078125 to 0.078125
- down_weight: bfloat16 [13824, 5120], P('ffn'), may hold values from -0.09375 to 0.09375
- span_offsets: int32 [2], replicated, may hold values from 0 to 16256, as said below
- decode_lengths: int32 [32], replicated, may hold values from 1 to 16383, as said below
- page_table: int32 [34, 128], replicated, may hold values from -1 to 895, as said below
Outputs:
- layer_output: bfloat16 [288, 5120], P('grp', 'ffn')
Inputs may be any that keep to these rules, and one draw needn't show every extreme that they name: `span_offsets`: the largest offset equals 16256. `decode_lengths`: one length equals 16383, the others are under 2048. `page_table`: row r holds page ids in its first ceil(n / 128) slots, where n is its prefix length plus its new tokens (128 for prefill, 1 for decode), and -1 in the others; no page id appears twice in the table.
All inputs are finite; a program needn't handle non-finite values.
Results may differ from a plain program's by a relative error of at most 0.025.
Values may be sent and summed in bfloat16 or wider, within the bound.
No kernel may reach another device: no remote copies, remote signals or barrier semaphores. Data moves between devices by JAX's collectives and lax.ppermute only.
A program may use at most 128 MiB of HBM per device.

v0:
```python
import functools
import math

import jax
import jax.numpy as jnp
from jax import lax
from jax.experimental import pallas as pl
from jax.experimental.pallas import tpu as pltpu
from jax.sharding import PartitionSpec as P

D = 5120
HD = 128
PAGE = 128
SPAN = 128
PRE = 2
DEC = 32
MAXP = 128
TOKENS = 288
GH = 5
HALF = 144
ROWS = 48
QUARTER = 72
COLS = 160
MSG = 96

EPS = 1e-05
NEG = -1e30
SCALE2 = HD ** (-0.5) * math.log2(math.e)
F32 = jnp.float32
BF16 = jnp.bfloat16
LIMIT = 48 << 20
GROUP = 4
CHUNKS = 4
FCHUNK = 512

vmem = pl.BlockSpec(memory_space=pltpu.VMEM)
smem = pl.BlockSpec(memory_space=pltpu.SMEM)
hbm = pl.BlockSpec(memory_space=pl.ANY)


def params():
    return pltpu.CompilerParams(vmem_limit_bytes=LIMIT)


def lanes(shape):
    return lax.broadcasted_iota(jnp.int32, shape, len(shape) - 1)


def rows_of(shape):
    return lax.broadcasted_iota(jnp.int32, shape, len(shape) - 2)


def split3(value):
    high = value.astype(BF16).astype(F32)
    rest = value - high
    middle = rest.astype(BF16).astype(F32)
    return high, middle, rest - middle


def project_kernel(x_ref, gain_ref, w_ref, out_ref):
    x = x_ref[...].astype(F32)
    scaled = (x * gain_ref[...]).astype(BF16)
    for k in range(3):
        product = jnp.dot(scaled, w_ref[k], preferred_element_type=F32)
        for h in range(GH):
            out_ref[k * GH + h] = product[:, h * HD : (h + 1) * HD].astype(BF16)
    squares = jnp.sum(x * x, axis=1, keepdims=True)
    high, middle, low = split3(squares)
    lane = lanes((TOKENS, HD))
    block = jnp.where(lane == 0, high, jnp.where(lane == 1, middle, jnp.where(lane == 2, low, 0.0)))
    out_ref[3 * GH] = block.astype(BF16)


def rotate_kernel(f_ref, in_ref, cos_ref, sin_ref, out_ref):
    total = in_ref[0].astype(F32)
    for s in range(1, in_ref.shape[0]):
        total = total + in_ref[s].astype(F32)
    turned = jnp.concatenate([total[:, HD // 2 :], total[:, : HD // 2]], axis=1)
    rotated = total * cos_ref[...] + turned * sin_ref[...]
    squares = total[:, 0:1] + total[:, 1:2] + total[:, 2:3]
    high, middle, low = split3(squares)
    lane = lanes((HALF, HD))
    block = jnp.where(lane == 0, high, jnp.where(lane == 1, middle, jnp.where(lane == 2, low, 0.0)))
    result = jnp.where(f_ref[0] >= 6 * GH, block, rotated).astype(BF16)
    for s in range(out_ref.shape[0]):
        out_ref[s] = result


def attention_kernel(
    code_ref,
    prefix_ref,
    f_ref,
    fresh_ref,
    key_hbm,
    value_hbm,
    out_ref,
    keys,
    values,
    sems,
    lists,
    scores,
    self_scores,
    peak,
    summed,
    factor,
    new_keys,
    new_values,
    dec_query,
    dec_peak,
    dec_total,
    dec_sum,
    final,
    lse,
):
    pages = key_hbm.shape[0]
    step = pages // CHUNKS
    copies = []
    for c in range(CHUNKS):
        part = pl.ds(c * step, step)
        copies.append(pltpu.make_async_copy(key_hbm.at[part], keys.at[part], sems.at[0, c]))
        copies.append(pltpu.make_async_copy(value_hbm.at[part], values.at[part], sems.at[1, c]))
    for copy in copies:
        copy.start()

    peak[...] = jnp.full(peak.shape, NEG, F32)
    summed[...] = jnp.zeros(summed.shape, F32)
    dec_peak[...] = jnp.full(dec_peak.shape, NEG, F32)
    dec_total[...] = jnp.zeros(dec_total.shape, F32)
    dec_sum[...] = jnp.zeros(dec_sum.shape, F32)

    squares = fresh_ref[3 * GH].astype(F32)
    squares = squares[:, 0:1] + squares[:, 1:2] + squares[:, 2:3]
    inverse = jnp.broadcast_to(lax.rsqrt(squares / D + EPS), (TOKENS, HD))
    factor[...] = inverse * SCALE2
    for h in range(GH):
        new_keys[h] = (fresh_ref[GH + h].astype(F32) * inverse).astype(BF16)
        new_values[h] = (fresh_ref[2 * GH + h].astype(F32) * inverse).astype(BF16)
        dec_query[h] = fresh_ref[h, PRE * SPAN :, :].astype(F32)

    def classify(p, counts):
        n_pre, n_dec = counts
        code = code_ref[p]
        owner = (code - 1) >> 7
        slot = (code - 1) & 127
        live = (code > 0) & (slot * PAGE < prefix_ref[jnp.maximum(owner, 0)])
        is_pre = live & (owner < PRE)
        is_dec = live & (owner >= PRE)

        @pl.when(is_pre)
        def _():
            lists[0, n_pre] = p

        @pl.when(is_dec)
        def _():
            lists[1, n_dec] = p

        return n_pre + is_pre.astype(jnp.int32), n_dec + is_dec.astype(jnp.int32)

    n_pre, n_dec = lax.fori_loop(0, pages, classify, (0, 0))

    f = f_ref[0]
    has_self = f < PRE * GH
    self_request = jnp.where(f >= GH, 1, 0)
    self_head = jnp.where(has_self, f - GH * self_request, 0)

    def span_rows(request):
        return pl.ds(pl.multiple_of(request * SPAN, SPAN), SPAN)

    def scored(query, key, scale):
        product = lax.dot_general(
            query, key, (((1,), (1,)), ((), ())), preferred_element_type=F32
        )
        return product * scale

    @pl.when(has_self)
    def _():
        part = span_rows(self_request)
        result = scored(fresh_ref[self_head, part, :], new_keys[self_head, part, :], factor[part, :])
        result = jnp.where(lanes((SPAN, SPAN)) <= rows_of((SPAN, SPAN)), result, NEG)
        self_scores[...] = result
        unit = self_request * GH + self_head
        peak[unit] = jnp.maximum(peak[unit], result)

    for copy in copies:
        copy.wait()

    def first_pass(i, _):
        p = lists[0, i]
        code = code_ref[p] - 1
        request = code >> 7
        left = prefix_ref[request] - (code & 127) * PAGE
        part = span_rows(request)
        scale = factor[part, :]
        visible = lanes((SPAN, PAGE)) < left
        for h in range(GH):
            result = scored(fresh_ref[h, part, :], keys[p, :, h * HD : (h + 1) * HD], scale)
            result = jnp.where(visible, result, NEG)
            scores[i, h] = result
            unit = request * GH + h
            peak[unit] = jnp.maximum(peak[unit], result)
        return 0

    lax.fori_loop(0, n_pre, first_pass, 0)

    for unit in range(PRE * GH):
        peak[unit] = jnp.broadcast_to(
            jnp.max(peak[unit], axis=1, keepdims=True), (SPAN, SPAN)
        )

    ones = jnp.ones((PAGE, HD), BF16)

    def weigh(unit, result, value):
        weights = jnp.exp2(result - peak[unit]).astype(BF16)
        both = jnp.concatenate([value, ones], axis=1)
        summed[unit] += jnp.dot(weights, both, preferred_element_type=F32)

    def second_pass(i, _):
        p = lists[0, i]
        request = (code_ref[p] - 1) >> 7
        for h in range(GH):
            weigh(request * GH + h, scores[i, h], values[p, :, h * HD : (h + 1) * HD])
        return 0

    lax.fori_loop(0, n_pre, second_pass, 0)

    @pl.when(has_self)
    def _():
        part = span_rows(self_request)
        weigh(self_request * GH + self_head, self_scores[...], new_values[self_head, part, :])

    def decode_pass(step_index, _):
        found = []
        for j in range(GROUP):
            position = step_index * GROUP + j
            p = lists[1, jnp.minimum(position, n_dec - 1)]
            code = code_ref[p] - 1
            owner = code >> 7
            token = owner - PRE
            left = jnp.where(position < n_dec, prefix_ref[owner] - (code & 127) * PAGE, 0)
            row = rows_of((8, HD))
            query = jnp.concatenate(
                [
                    jnp.where(row == h, jnp.broadcast_to(dec_query[h, pl.ds(token, 1), :], (8, HD)), 0.0)
                    for h in range(GH)
                ],
                axis=1,
            ).astype(BF16)
            result = scored(query, keys[p], factor[pl.ds(PRE * SPAN + token, 1), :])
            visible = lanes((8, PAGE)) < left
            result = jnp.where(visible, result, NEG)
            top = jnp.max(result, axis=1, keepdims=True)
            weights = jnp.where(visible, jnp.exp2(result - top), 0.0)
            total = jnp.sum(weights, axis=1, keepdims=True)
            product = jnp.dot(weights.astype(BF16), values[p], preferred_element_type=F32)
            found.append((token, top, total, product))
        for token, top, total, product in found:
            before = dec_peak[token]
            after = jnp.maximum(before, top)
            keep = jnp.exp2(before - after)
            take = jnp.exp2(top - after)
            dec_peak[token] = after
            dec_total[token] = dec_total[token] * keep + total * take
            wide = jnp.concatenate([keep] * GH, axis=1)
            wide_take = jnp.concatenate([take] * GH, axis=1)
            dec_sum[token] = dec_sum[token] * wide + product * wide_take
        return 0

    lax.fori_loop(0, (n_dec + GROUP - 1) // GROUP, decode_pass, 0)

    for request in range(PRE):
        for h in range(GH):
            unit = request * GH + h
            total = summed[unit, :, HD:]
            some = total > 0.0
            safe = jnp.where(some, total, 1.0)
            part = pl.ds(request * SPAN, SPAN)
            final[h, part, :] = summed[unit, :, :HD] / safe
            lse[h, part, :] = jnp.where(some, peak[unit] + jnp.log2(safe), NEG)

    dec_factor = factor[PRE * SPAN :, :]
    dec_rows = pl.ds(PRE * SPAN, DEC)
    for h in range(GH):
        own = jnp.sum(
            dec_query[h] * new_keys[h, dec_rows, :].astype(F32), axis=1, keepdims=True
        )
        own = jnp.where(f == PRE * GH, jnp.broadcast_to(own, (DEC, HD)) * dec_factor, NEG)
        before = dec_peak[:, h, :]
        after = jnp.maximum(before, own)
        keep = jnp.exp2(before - after)
        take = jnp.where(f == PRE * GH, jnp.exp2(own - after), 0.0)
        total = dec_total[:, h, :] * keep + take
        value = dec_sum[:, h, h * HD : (h + 1) * HD] * keep
        value = value + take * new_values[h, dec_rows, :].astype(F32)
        some = total > 0.0
        safe = jnp.where(some, total, 1.0)
        final[h, dec_rows, :] = value / safe
        lse[h, dec_rows, :] = jnp.where(some, after + jnp.log2(safe), NEG)

    diagonal = rows_of((ROWS, HD)) == lanes((ROWS, HD))
    row = rows_of((16, HD))
    for h in range(GH):
        for b in range(TOKENS // ROWS):
            part = pl.ds(b * ROWS, ROWS)
            target = h * (TOKENS // ROWS) + b
            out_ref[target, :ROWS, :] = final[h, part, :].astype(BF16)
            stat = jnp.sum(jnp.where(diagonal, lse[h, part, :], 0.0), axis=0, keepdims=True)
            high, middle, low = split3(stat)
            block = jnp.where(
                row == 0, high, jnp.where(row == 1, middle, jnp.where(row == 2, low, 0.0))
            )
            out_ref[target, ROWS:, :] = block.astype(BF16)
    for target in range(GH * (TOKENS // ROWS), out_ref.shape[0]):
        out_ref[target] = jnp.zeros(out_ref.shape[1:], BF16)


def merge_kernel(in_ref, out_ref):
    sources = in_ref.shape[0]
    stats = jnp.concatenate(
        [
            jnp.sum(in_ref[s, ROWS:, :].astype(F32), axis=0, keepdims=True)
            for s in range(sources)
        ],
        axis=0,
    )
    top = jnp.max(stats, axis=0, keepdims=True)
    weights = jnp.exp2(stats - top)
    weights = weights / jnp.sum(weights, axis=0, keepdims=True)
    padded = jnp.concatenate([weights, jnp.zeros((HD - sources, HD), F32)], axis=0)
    turned = jnp.transpose(padded)
    total = jnp.zeros((ROWS, HD), F32)
    for s in range(sources):
        total = total + turned[:ROWS, s : s + 1] * in_ref[s, :ROWS, :].astype(F32)
    result = total.astype(BF16)
    for s in range(sources):
        out_ref[s] = result


def output_kernel(in_ref, w_ref, out_ref):
    blocks = TOKENS // ROWS
    heads = jnp.concatenate(
        [
            jnp.concatenate([in_ref[h * blocks + b] for b in range(blocks)], axis=0)
            for h in range(GH)
        ],
        axis=1,
    )
    product = jnp.dot(heads, w_ref[...], preferred_element_type=F32)
    for i in range(out_ref.shape[0]):
        out_ref[i] = product[i * QUARTER : (i + 1) * QUARTER].astype(BF16)


def packed(value):
    third = QUARTER // 3
    tail = value[:, HD:]
    extra = jnp.concatenate(
        [tail[i * third : (i + 1) * third] for i in range(3)]
        + [jnp.zeros((third, HD - 3 * (COLS - HD)), F32)],
        axis=1,
    )
    return jnp.concatenate([value[:, :HD], extra], axis=0).astype(BF16)


def unpacked(message):
    third = QUARTER // 3
    wide = COLS - HD
    extra = message[QUARTER:]
    tail = jnp.concatenate([extra[:, i * wide : (i + 1) * wide] for i in range(3)], axis=0)
    assert tail.shape == (3 * third, wide)
    return jnp.concatenate([message[:QUARTER], tail], axis=1)


def residual_kernel(g_ref, in_ref, x_ref, own_ref, out_ref):
    attended = in_ref[0].astype(F32)
    for i in range(1, in_ref.shape[0]):
        attended = attended + in_ref[i].astype(F32)
    x = x_ref[...].astype(F32)
    own = jnp.zeros((QUARTER, COLS), F32)
    for i in range(in_ref.shape[0]):
        own = jnp.where(g_ref[0] == i, x[i * QUARTER : (i + 1) * QUARTER], own)
    own = (own + attended).astype(BF16)
    own_ref[...] = own
    message = packed(own.astype(F32))
    for s in range(out_ref.shape[0]):
        out_ref[s] = message


def ffn_kernel(
    in_ref, gain_ref, gate_hbm, down_hbm, out_ref, rows, normed, gates, down, sems
):
    copies = []
    for c in range(D // FCHUNK):
        part = pl.ds(c * FCHUNK, FCHUNK)
        copies.append(
            pltpu.make_async_copy(gate_hbm.at[:, part, :], gates.at[:, part, :], sems.at[c])
        )
    copies.append(pltpu.make_async_copy(down_hbm, down, sems.at[D // FCHUNK]))
    for copy in copies:
        copy.start()
    for s in range(in_ref.shape[0]):
        rows[:, s * COLS : (s + 1) * COLS] = unpacked(in_ref[s].astype(F32))
    full = rows[...]
    inverse = lax.rsqrt(jnp.sum(full * full, axis=1, keepdims=True) / D + EPS)
    normed[...] = (full * inverse * gain_ref[...]).astype(BF16)
    hidden_units = down.shape[0]
    gate = jnp.zeros((QUARTER, hidden_units), F32)
    up = jnp.zeros((QUARTER, hidden_units), F32)
    for c in range(D // FCHUNK):
        copies[c].wait()
        part = pl.ds(c * FCHUNK, FCHUNK)
        block = normed[:, part]
        gate = gate + jnp.dot(block, gates[0, part, :], preferred_element_type=F32)
        up = up + jnp.dot(block, gates[1, part, :], preferred_element_type=F32)
    hidden = (gate / (1.0 + jnp.exp(-gate)) * up).astype(BF16)
    copies[-1].wait()
    wide = 4 * COLS
    for s in range(in_ref.shape[0] // 4):
        product = jnp.dot(
            hidden, down[:, s * wide : (s + 1) * wide], preferred_element_type=F32
        )
        for j in range(4):
            out_ref[4 * s + j] = packed(product[:, j * COLS : (j + 1) * COLS])


def finish_kernel(in_ref, own_ref, out_ref):
    total = in_ref[0].astype(F32)
    for s in range(1, in_ref.shape[0]):
        total = total + in_ref[s].astype(F32)
    out_ref[...] = (own_ref[...].astype(F32) + unpacked(total)).astype(BF16)


def call(kernel, out, specs, scratch=(), out_specs=None):
    return pl.pallas_call(
        kernel,
        out_shape=out,
        in_specs=specs,
        out_specs=out_specs if out_specs is not None else vmem,
        scratch_shapes=list(scratch),
        compiler_params=params(),
    )


def shape(*dims, kind=BF16):
    return jax.ShapeDtypeStruct(dims, kind)


def swap(value, axis):
    return lax.all_to_all(value, axis, 0, 0)


def tables(f, span_offsets, decode_lengths):
    within = jnp.arange(SPAN, dtype=jnp.int32)
    prefill = (span_offsets[:, None] + within[None, :]).reshape(PRE * SPAN)
    positions = jnp.concatenate([prefill, decode_lengths])
    positions = jnp.where(f % 2 == 0, positions[:HALF], positions[HALF:])
    half_width = HD // 2
    lane = jnp.arange(HD, dtype=jnp.int32)
    frequency = jnp.exp(
        (lane % half_width).astype(F32) * (-2.0 * math.log(10000.0) / HD)
    )
    angles = positions.astype(F32)[:, None] * frequency[None, :]
    turning = f < 4 * GH
    cosine = jnp.where(turning, jnp.cos(angles), 1.0)
    sine = jnp.where(
        turning, jnp.sin(angles) * jnp.where(lane < half_width, -1.0, 1.0)[None, :], 0.0
    )
    return cosine, sine


def shards(
    layer_input,
    norm_gain,
    qkv_weight,
    key_cache,
    value_cache,
    out_weight,
    ffn_gain,
    gate_up_weight,
    down_weight,
    span_offsets,
    decode_lengths,
    page_table,
):
    ffn = lax.axis_size("ffn")
    grp = lax.axis_size("grp")
    f = lax.axis_index("ffn")
    g = lax.axis_index("grp")
    f1 = f.astype(jnp.int32).reshape(1)
    g1 = g.astype(jnp.int32).reshape(1)
    pages = key_cache.shape[0]
    hidden_units = down_weight.shape[0]

    cosine, sine = tables(f, span_offsets, decode_lengths)
    local_ids = f * pages + jnp.arange(pages, dtype=jnp.int32)
    requests = PRE + DEC
    numbers = jnp.arange(requests * MAXP, dtype=jnp.int32).reshape(requests, MAXP) + 1
    codes = jnp.sum(
        jnp.where(page_table[None] == local_ids[:, None, None], numbers[None], 0), axis=(1, 2)
    )
    prefixes = jnp.concatenate([span_offsets, decode_lengths])

    partial = call(project_kernel, shape(3 * GH + 1, TOKENS, HD), [vmem] * 3)(
        layer_input, norm_gain.reshape(1, -1), qkv_weight
    )
    partial = swap(partial.reshape(ffn, HALF, HD), "ffn")
    fresh = call(rotate_kernel, shape(ffn, HALF, HD), [smem] + [vmem] * 3)(
        f1, partial, cosine, sine
    )
    fresh = swap(fresh, "ffn").reshape(3 * GH + 1, TOKENS, HD)

    units = PRE * GH
    message = call(
        attention_kernel,
        shape(ffn, ROWS + 16, HD),
        [smem] * 3 + [vmem] + [hbm] * 2,
        [
            pltpu.VMEM((pages, PAGE, GH * HD), BF16),
            pltpu.VMEM((pages, PAGE, GH * HD), BF16),
            pltpu.SemaphoreType.DMA((2, CHUNKS)),
            pltpu.SMEM((2, pages), jnp.int32),
            pltpu.VMEM((pages, GH, SPAN, PAGE), F32),
            pltpu.VMEM((SPAN, SPAN), F32),
            pltpu.VMEM((units, SPAN, PAGE), F32),
            pltpu.VMEM((units, SPAN, 2 * HD), F32),
            pltpu.VMEM((TOKENS, HD), F32),
            pltpu.VMEM((GH, TOKENS, HD), BF16),
            pltpu.VMEM((GH, TOKENS, HD), BF16),
            pltpu.VMEM((GH, DEC, HD), F32),
            pltpu.VMEM((DEC, 8, HD), F32),
            pltpu.VMEM((DEC, 8, HD), F32),
            pltpu.VMEM((DEC, 8, GH * HD), F32),
            pltpu.VMEM((GH, TOKENS, HD), F32),
            pltpu.VMEM((GH, TOKENS, HD), F32),
        ],
    )(codes, prefixes, f1, fresh, key_cache, value_cache)
    message = swap(message, "ffn")
    heads = call(merge_kernel, shape(ffn, ROWS, HD), [vmem])(message)
    heads = swap(heads, "ffn")

    product = call(output_kernel, shape(grp, QUARTER, COLS), [vmem] * 2)(heads, out_weight)
    product = swap(product, "grp")
    own, rows = call(
        residual_kernel,
        (shape(QUARTER, COLS), shape(ffn, MSG, HD)),
        [smem] + [vmem] * 2,
        out_specs=(vmem, vmem),
    )(g1, product, layer_input)
    rows = swap(rows, "ffn")

    down_terms = call(
        ffn_kernel,
        shape(ffn, MSG, HD),
        [vmem] * 2 + [hbm] * 2,
        [
            pltpu.VMEM((QUARTER, D), F32),
            pltpu.VMEM((QUARTER, D), BF16),
            pltpu.VMEM((2, D, hidden_units), BF16),
            pltpu.VMEM((hidden_units, D), BF16),
            pltpu.SemaphoreType.DMA((D // FCHUNK + 1,)),
        ],
    )(rows, ffn_gain.reshape(1, -1), gate_up_weight, down_weight)
    down_terms = swap(down_terms, "ffn")
    return call(finish_kernel, shape(QUARTER, COLS), [vmem] * 2)(down_terms, own)


def solution(mesh):
    in_specs = (
        P(None, "ffn"),
        P("ffn"),
        P(None, "ffn", "grp"),
        P("ffn", None, "grp"),
        P("ffn", None, "grp"),
        P("grp", "ffn"),
        P(),
        P(None, None, "ffn"),
        P("ffn", None),
        P(),
        P(),
        P(),
    )
    out_specs = P("grp", "ffn")
    return jax.shard_map(shards, mesh=mesh, in_specs=in_specs, out_specs=out_specs, check_vma=False)
```

profile of v0, /device:TPU:1, one launch (start us, length us, event | category | flops | bytes accessed | tf_op | source)
XLA Modules:
  0.0 159.6 jit_solution(9326976030973607889)
XLA Ops:
  0.0 1.0 copy.17.x_ref
  1.1 1.1 copy-done.1
  2.8 1.6 shard_map.118
  4.4 9.4 %all-to-all-start = ((bf16[32,144,128]{2,1,0:T(8,128)(2,1)}), bf16[32,144,128]{2,1,0:T(8,128)(2,1)S(1)}, u32[]{:S(2)}, u32[]{:S(2)}) async-start(bf16[32,144,128]{2,1,0:T(8,128)(2,1)} %bitcast.3), calls=%async_computation | async-start | bytes 2359296 | tf_op jit(solution)/shard_map/all_to_all | solution.py:447
  14.4 17.8 %all-to-all-done.in_ref = bf16[32,144,128]{2,1,0:T(8,128)(2,1)S(1)} async-done(((bf16[32,144,128]{2,1,0:T(8,128)(2,1)}), bf16[32,144,128]{2,1,0:T(8,128)(2,1)S(1)}, u32[]{:S(2)}, u32[]{:S(2)}) %all-to-all-start) | async-done | bytes 1179680 | tf_op jit(solution)/shard_map/all_to_all | solution.py:447
  32.2 1.5 shard_map.119
  33.7 3.9 %all-to-all-start.1 = ((bf16[32,144,128]{2,1,0:T(8,128)(2,1)}), bf16[32,144,128]{2,1,0:T(8,128)(2,1)S(1)}, u32[]{:S(2)}, u32[]{:S(2)}) async-start(bf16[32,144,128]{2,1,0:T(8,128)(2,1)} %shard_map.119), calls=%async_computation.1 | async-start | bytes 2359296 | tf_op jit(solution)/shard_map/all_to_all | solution.py:447
  37.9 18.0 %all-to-all-done.1 = bf16[32,144,128]{2,1,0:T(8,128)(2,1)S(1)} async-done(((bf16[32,144,128]{2,1,0:T(8,128)(2,1)}), bf16[32,144,128]{2,1,0:T(8,128)(2,1)S(1)}, u32[]{:S(2)}, u32[]{:S(2)}) %all-to-all-start.1) | async-done | bytes 1179680 | tf_op jit(solution)/shard_map/all_to_all | solution.py:447
  56.0 12.5 %shard_map.120 = bf16[32,64,128]{2,1,0:T(8,128)(2,1)S(1)} custom-call(s32[28]{0:T(128)S(1)} %select_reduce_fusion.code_ref, s32[34]{0:T(128)S(1)} %pad_add_fusion.1.prefix_ref, s32[1]{0:T(128)} %bitcast.1.f_ref, bf16[16,288,128]{2,1,0:T(8,128)(2,1)S(1)} %bitcast.8, bf16[28,128,640]{2,1,0:T(8,128)(2,1)} %key_hbm.1, bf16[28,128,640]{2,1,0:T(8,128)(2,1)} %value_hbm.1), custom_call_target="tpu_custom_call" | custom-call | tf_op jit(solution)/shard_map/pallas_call | solution.py:511
  68.5 15.9 %all_to_all.35.in_ref = bf16[32,64,128]{2,1,0:T(8,128)(2,1)S(1)} all-to-all(bf16[32,64,128]{2,1,0:T(8,128)(2,1)S(1)} %shard_map.120), channel_id=1, replica_groups=mesh['grp'=4,'ffn'=32] {'ffn'}, dimensions={0} | all-to-all | bytes 1048576 | tf_op jit(solution)/shard_map/all_to_all | solution.py:447
  84.4 1.3 shard_map.121
  85.7 3.7 %all-to-all-start.3 = ((bf16[32,48,128]{2,1,0:T(8,128)(2,1)}), bf16[32,48,128]{2,1,0:T(8,128)(2,1)S(1)}, u32[]{:S(2)}, u32[]{:S(2)}) async-start(bf16[32,48,128]{2,1,0:T(8,128)(2,1)} %shard_map.121), calls=%async_computation.3 | async-start | bytes 786432 | tf_op jit(solution)/shard_map/all_to_all | solution.py:447
  89.5 10.1 %all-to-all-done.3.in_ref = bf16[32,48,128]{2,1,0:T(8,128)(2,1)S(1)} async-done(((bf16[32,48,128]{2,1,0:T(8,128)(2,1)}), bf16[32,48,128]{2,1,0:T(8,128)(2,1)S(1)}, u32[]{:S(2)}, u32[]{:S(2)}) %all-to-all-start.3) | async-done | bytes 393248 | tf_op jit(solution)/shard_map/all_to_all | solution.py:447
  99.6 1.0 shard_map.122
  100.5 4.2 %all-to-all-start.4 = ((bf16[4,72,160]{2,1,0:T(8,128)(2,1)}), bf16[4,72,160]{2,1,0:T(8,128)(2,1)S(1)}, u32[]{:S(2)}, u32[]{:S(2)}) async-start(bf16[4,72,160]{2,1,0:T(8,128)(2,1)} %shard_map.122), calls=%async_computation.4 | async-start | bytes 294912 | tf_op jit(solution)/shard_map/all_to_all | solution.py:447
  104.7 5.1 %all-to-all-done.4.in_ref = bf16[4,72,160]{2,1,0:T(8,128)(2,1)S(1)} async-done(((bf16[4,72,160]{2,1,0:T(8,128)(2,1)}), bf16[4,72,160]{2,1,0:T(8,128)(2,1)S(1)}, u32[]{:S(2)}, u32[]{:S(2)}) %all-to-all-start.4) | async-done | bytes 92192 | tf_op jit(solution)/shard_map/all_to_all | solution.py:447
  109.9 1.0 shard_map.123
  110.9 4.8 %all-to-all-start.5 = ((bf16[32,96,128]{2,1,0:T(8,128)(2,1)}), bf16[32,96,128]{2,1,0:T(8,128)(2,1)S(1)}, u32[]{:S(2)}, u32[]{:S(2)}) async-start(bf16[32,96,128]{2,1,0:T(8,128)(2,1)} %get-tuple-element.7), calls=%async_computation.5 | async-start | bytes 1572864 | tf_op jit(solution)/shard_map/all_to_all | solution.py:447
  115.7 13.2 %copy.20.gate_hbm = bf16[2,5120,432]{2,1,0:T(8,128)(2,1)} copy(bf16[2,5120,432]{1,2,0:T(8,128)(2,1)} %param.19) | data formatting | bytes 17694720 | tf_op args[7]
  129.0 1.1 all-to-all-done.5.in_ref
  130.0 2.3 %copy-done = bf16[432,5120]{1,0:T(8,128)(2,1)S(1)} copy-done((bf16[432,5120]{1,0:T(8,128)(2,1)S(1)}, bf16[432,5120]{1,0:T(8,128)(2,1)}, u32[]{:S(2)}) %copy-start) | copy-done | bytes 4423704
  132.3 6.1 %shard_map.124 = bf16[32,96,128]{2,1,0:T(8,128)(2,1)S(1)} custom-call(bf16[32,96,128]{2,1,0:T(8,128)(2,1)S(1)} %all-to-all-done.5.in_ref, f32[1,5120]{1,0:T(1,128)S(1)} %bitcast.9, bf16[2,5120,432]{2,1,0:T(8,128)(2,1)} %copy.20.gate_hbm, bf16[432,5120]{1,0:T(8,128)(2,1)S(1)} %copy-done), custom_call_target="tpu_custom_call" | custom-call | tf_op jit(solution)/shard_map/pallas_call | solution.py:549
  138.4 20.4 %all_to_all.36.in_ref = bf16[32,96,128]{2,1,0:T(8,128)(2,1)S(1)} all-to-all(bf16[32,96,128]{2,1,0:T(8,128)(2,1)S(1)} %shard_map.124), channel_id=1, replica_groups=mesh['grp'=4,'ffn'=32] {'ffn'}, dimensions={0} | all-to-all | bytes 1572864 | tf_op jit(solution)/shard_map/all_to_all | solution.py:447
  158.8 0.7 shard_map.125
  (24 shorter events, 1.7 us)
Async XLA Ops:
  0.0 13.8 %copy-start.7 = (s32[2]{0:T(128)S(1)}, s32[2]{0:T(128)}, u32[]{:S(2)}) copy-start(s32[2]{0:T(128)} %param.21) | copy-start | bytes 28
  0.0 13.9 %copy-start.6 = (s32[32]{0:T(128)S(1)}, s32[32]{0:T(128)}, u32[]{:S(2)}) copy-start(s32[32]{0:T(128)} %param.22) | copy-start | bytes 388
  1.0 1.1 copy-start.1
  2.1 0.7 copy-start.3
  2.8 34.9 %copy-start.5 = (s32[34,128]{1,0:T(8,128)S(1)}, s32[34,128]{1,0:T(8,128)}, u32[]{:S(2)}) copy-start(s32[34,128]{1,0:T(8,128)} %param.23) | copy-start | bytes 52228
  4.4 27.8 %all-to-all-start = ((bf16[32,144,128]{2,1,0:T(8,128)(2,1)}), bf16[32,144,128]{2,1,0:T(8,128)(2,1)S(1)}, u32[]{:S(2)}, u32[]{:S(2)}) async-start(bf16[32,144,128]{2,1,0:T(8,128)(2,1)} %bitcast.3), calls=%async_computation | async-start | bytes 2359296 | tf_op jit(solution)/shard_map/all_to_all | solution.py:447
  33.7 22.3 %all-to-all-start.1 = ((bf16[32,144,128]{2,1,0:T(8,128)(2,1)}), bf16[32,144,128]{2,1,0:T(8,128)(2,1)S(1)}, u32[]{:S(2)}, u32[]{:S(2)}) async-start(bf16[32,144,128]{2,1,0:T(8,128)(2,1)} %shard_map.119), calls=%async_computation.1 | async-start | bytes 2359296 | tf_op jit(solution)/shard_map/all_to_all | solution.py:447
  56.0 33.4 %copy-start.4 = (bf16[640,160]{0,1:T(8,128)(2,1)S(1)}, bf16[640,160]{0,1:T(8,128)(2,1)}, u32[]{:S(2)}) copy-start(bf16[640,160]{0,1:T(8,128)(2,1)} %param.17) | copy-start | bytes 614404
  85.7 13.9 %all-to-all-start.3 = ((bf16[32,48,128]{2,1,0:T(8,128)(2,1)}), bf16[32,48,128]{2,1,0:T(8,128)(2,1)S(1)}, u32[]{:S(2)}, u32[]{:S(2)}) async-start(bf16[32,48,128]{2,1,0:T(8,128)(2,1)} %shard_map.121), calls=%async_computation.3 | async-start | bytes 786432 | tf_op jit(solution)/shard_map/all_to_all | solution.py:447
  100.5 9.3 %all-to-all-start.4 = ((bf16[4,72,160]{2,1,0:T(8,128)(2,1)}), bf16[4,72,160]{2,1,0:T(8,128)(2,1)S(1)}, u32[]{:S(2)}, u32[]{:S(2)}) async-start(bf16[4,72,160]{2,1,0:T(8,128)(2,1)} %shard_map.122), calls=%async_computation.4 | async-start | bytes 294912 | tf_op jit(solution)/shard_map/all_to_all | solution.py:447
  110.9 19.2 %all-to-all-start.5 = ((bf16[32,96,128]{2,1,0:T(8,128)(2,1)}), bf16[32,96,128]{2,1,0:T(8,128)(2,1)S(1)}, u32[]{:S(2)}, u32[]{:S(2)}) async-start(bf16[32,96,128]{2,1,0:T(8,128)(2,1)} %get-tuple-element.7), calls=%async_computation.5 | async-start | bytes 1572864 | tf_op jit(solution)/shard_map/all_to_all | solution.py:447
  115.7 14.3 %copy-start.2 = (f32[5120]{0:T(1024)S(1)}, f32[5120]{0:T(1024)}, u32[]{:S(2)}) copy-start(f32[5120]{0:T(1024)} %param.18) | copy-start | bytes 61444
  130.0 2.3 %copy-start = (bf16[432,5120]{1,0:T(8,128)(2,1)S(1)}, bf16[432,5120]{1,0:T(8,128)(2,1)}, u32[]{:S(2)}) copy-start(bf16[432,5120]{1,0:T(8,128)(2,1)} %down_hbm.1) | copy-start | bytes 13271044
where the time goes:
time: 162 us; the launch traced here: 160 us
  waiting for transfers between devices  52.1 us (32%)
  blocking collectives  36.3 us (22%)
  starting transfers between devices  26 us (16%)
  Pallas kernels  25.6 us (16%)
  local copies, waits for them, and re-layouts  18.5 us (11%)
    all_to_all x5, waiting for transfers between devices, swap(): return lax.all_to_all(value, axis, 0, 0)  52.1 us
    all_to_all x2, blocking collectives, swap(): return lax.all_to_all(value, axis, 0, 0)  36.3 us
    all_to_all x5, starting transfers between devices, swap(): return lax.all_to_all(value, axis, 0, 0)  26 us
    unnamed x19, local copies, waits for them, and re-layouts  18.5 us
    pallas_call x1, Pallas kernels, shards(): call(attention_kernel, shape(ffn, ROWS + 16, HD), [smem] * 3 + [vmem] + [...  12.5 us
    pallas_call x1, Pallas kernels, shards(): call(ffn_kernel, shape(ffn, MSG, HD), [vmem] * 2 + [hbm] * 2, [pltpu.VMEM...  6.08 us
  transfers between devices with their start and end apart: 5, of which 5 were waited for; matrix products, arithmetic and copies ran while one was open for 9% of the time, Pallas kernels for 0%

commit v1 on v0

v1 whole, which is shorter than its diff:
```python
import functools
import math

import jax
import jax.numpy as jnp
from jax import lax
from jax.experimental import pallas as pl
from jax.experimental.pallas import tpu as pltpu
from jax.sharding import PartitionSpec as P

D = 5120
HD = 128
PAGE = 128
SPAN = 128
PRE = 2
DEC = 32
MAXP = 128
TOKENS = 288
GH = 5
ROWS = 48
QUARTER = 72
COLS = 160
MSG = 96
FEW = 12
STATS = 8

EPS = 1e-05
NEG = -1e30
SCALE2 = HD ** (-0.5) * math.log2(math.e)
F32 = jnp.float32
BF16 = jnp.bfloat16
LIMIT = 32 << 20
GROUP = 4
CHUNKS = 4
FCHUNK = 512

vmem = pl.BlockSpec(memory_space=pltpu.VMEM)
smem = pl.BlockSpec(memory_space=pltpu.SMEM)
hbm = pl.BlockSpec(memory_space=pl.ANY)


def params():
    return pltpu.CompilerParams(vmem_limit_bytes=LIMIT)


def lanes(shape):
    return lax.broadcasted_iota(jnp.int32, shape, len(shape) - 1)


def rows_of(shape):
    return lax.broadcasted_iota(jnp.int32, shape, len(shape) - 2)


def split3(value):
    high = value.astype(BF16).astype(F32)
    rest = value - high
    middle = rest.astype(BF16).astype(F32)
    return high, middle, rest - middle


def project_kernel(x_hbm, gain_hbm, w_hbm, out_ref, x_vmem, gain_ref, w_vmem, sems):
    copies = [pltpu.make_async_copy(x_hbm, x_vmem, sems.at[3])]
    gain_copy = pltpu.make_async_copy(gain_hbm, gain_ref, sems.at[4])
    gain_copy.start()
    for k in range(3):
        copies.append(pltpu.make_async_copy(w_hbm.at[k], w_vmem.at[k], sems.at[k]))
    for copy in copies:
        copy.start()
    copies[0].wait()
    gain_copy.wait()
    x = jnp.transpose(x_vmem[...].astype(F32))
    scaled = (x * gain_ref[...]).astype(BF16)
    squares = jnp.sum(x * x, axis=1, keepdims=True)
    blocks = TOKENS // ROWS
    diagonal = rows_of((ROWS, HD)) == lanes((ROWS, HD))
    row = rows_of((STATS, HD))
    for b in range(blocks):
        part = jnp.broadcast_to(squares[b * ROWS : (b + 1) * ROWS], (ROWS, HD))
        stat = jnp.sum(jnp.where(diagonal, part, 0.0), axis=0, keepdims=True)
        high, middle, low = split3(stat)
        block = jnp.where(
            row == 0, high, jnp.where(row == 1, middle, jnp.where(row == 2, low, 0.0))
        ).astype(BF16)
        for h in range(GH):
            out_ref[h * blocks + b, 3 * ROWS :, :] = block
    for k in range(3):
        copies[1 + k].wait()
        product = jnp.dot(scaled, w_vmem[k], preferred_element_type=F32).astype(BF16)
        for h in range(GH):
            for b in range(blocks):
                out_ref[h * blocks + b, k * ROWS : (k + 1) * ROWS, :] = product[
                    b * ROWS : (b + 1) * ROWS, h * HD : (h + 1) * HD
                ]
    for target in range(GH * blocks, out_ref.shape[0]):
        out_ref[target] = jnp.zeros(out_ref.shape[1:], BF16)


def rotate_kernel(in_ref, cos_ref, sin_ref, out_ref, own_ref):
    total = in_ref[0].astype(F32)
    for s in range(1, in_ref.shape[0]):
        total = total + in_ref[s].astype(F32)
    diagonal = rows_of((ROWS, HD)) == lanes((ROWS, HD))
    stat = jnp.sum(total[3 * ROWS :], axis=0, keepdims=True)
    squares = jnp.sum(
        jnp.where(diagonal, jnp.broadcast_to(stat, (ROWS, HD)), 0.0), axis=1, keepdims=True
    )
    inverse = lax.rsqrt(squares / D + EPS)

    def rotated(value):
        value = value * inverse
        turned = jnp.concatenate([value[:, HD // 2 :], value[:, : HD // 2]], axis=1)
        return (value * cos_ref[...] + turned * sin_ref[...]).astype(BF16)

    own_ref[0] = rotated(total[ROWS : 2 * ROWS])
    own_ref[1] = (total[2 * ROWS : 3 * ROWS] * inverse).astype(BF16)
    query = rotated(total[:ROWS])
    for s in range(out_ref.shape[0]):
        out_ref[s] = query


def attention_kernel(
    code_ref,
    prefix_ref,
    f_ref,
    fresh_ref,
    own_ref,
    key_hbm,
    value_hbm,
    out_ref,
    keys,
    values,
    sems,
    lists,
    scores,
    peak,
    summed,
    dec_query,
    dec_peak,
    dec_total,
    dec_sum,
    final,
    lse,
):
    pages = key_hbm.shape[0]
    step = pages // CHUNKS
    parts = [pl.ds(c * step, step) for c in range(CHUNKS)]
    copies = [
        pltpu.make_async_copy(key_hbm.at[part], keys.at[part], sems.at[0, c])
        for c, part in enumerate(parts)
    ] + [
        pltpu.make_async_copy(value_hbm.at[part], values.at[part], sems.at[1, c])
        for c, part in enumerate(parts)
    ]
    for copy in copies:
        copy.start()

    peak[...] = jnp.full(peak.shape, NEG, F32)
    summed[...] = jnp.zeros(summed.shape, F32)
    dec_peak[...] = jnp.full(dec_peak.shape, NEG, F32)
    dec_total[...] = jnp.zeros(dec_total.shape, F32)
    dec_sum[...] = jnp.zeros(dec_sum.shape, F32)
    final[:, TOKENS:, :] = jnp.zeros((GH, 16, HD), F32)
    lse[:, TOKENS:, :] = jnp.zeros((GH, 16, HD), F32)
    for h in range(GH):
        dec_query[h] = fresh_ref[h * TOKENS + PRE * SPAN : (h + 1) * TOKENS, :].astype(F32)

    def classify(p, counts):
        n_pre, n_dec = counts
        code = code_ref[p]
        owner = (code - 1) >> 7
        slot = (code - 1) & 127
        live = (code > 0) & (slot * PAGE < prefix_ref[jnp.maximum(owner, 0)])
        is_pre = live & (owner < PRE)
        is_dec = live & (owner >= PRE)

        @pl.when(is_pre)
        def _():
            lists[0, n_pre] = p

        @pl.when(is_dec)
        def _():
            lists[1, n_dec] = p

        return n_pre + is_pre.astype(jnp.int32), n_dec + is_dec.astype(jnp.int32)

    n_pre, n_dec = lax.fori_loop(0, pages, classify, (0, 0))

    f = f_ref[0]
    blocks = TOKENS // ROWS
    has_own = f < GH * blocks
    own_head = jnp.where(has_own, f // blocks, 0)
    own_block = jnp.where(has_own, f - own_head * blocks, 0)
    filler = jnp.zeros((PAGE - ROWS, HD), BF16)
    own_keys = jnp.concatenate([own_ref[0], filler], axis=0)
    own_values = jnp.concatenate([own_ref[1], filler], axis=0)
    own_token = own_block * ROWS + lanes((SPAN, PAGE))
    in_block = lanes((SPAN, PAGE)) < ROWS

    def query_rows(request, h):
        return fresh_ref[pl.ds(pl.multiple_of(h * TOKENS + request * SPAN, 16), SPAN), :]

    def scored(query, key):
        product = lax.dot_general(
            query, key, (((1,), (1,)), ((), ())), preferred_element_type=F32
        )
        return product * SCALE2

    def own_scores(request):
        within = own_token - request * SPAN
        visible = in_block & (within >= 0) & (within <= rows_of((SPAN, PAGE)))
        return jnp.where(visible, scored(query_rows(request, own_head), own_keys), NEG), visible

    @pl.when(has_own)
    def _():
        for request in range(PRE):
            unit = request * GH + own_head
            peak[unit] = jnp.maximum(peak[unit], own_scores(request)[0])

    for copy in copies[:CHUNKS]:
        copy.wait()

    def first_pass(i, _):
        p = lists[0, i]
        code = code_ref[p] - 1
        request = code >> 7
        left = prefix_ref[request] - (code & 127) * PAGE
        visible = lanes((SPAN, PAGE)) < left
        for h in range(GH):
            result = scored(query_rows(request, h), keys[p, :, h * HD : (h + 1) * HD])
            result = jnp.where(visible, result, NEG)
            scores[i, h] = result
            unit = request * GH + h
            peak[unit] = jnp.maximum(peak[unit], result)
        return 0

    lax.fori_loop(0, n_pre, first_pass, 0)

    for unit in range(PRE * GH):
        peak[unit] = jnp.broadcast_to(
            jnp.max(peak[unit], axis=1, keepdims=True), (SPAN, SPAN)
        )

    for copy in copies[CHUNKS:]:
        copy.wait()

    ones = jnp.ones((PAGE, HD), BF16)

    def weigh(unit, weights, value):
        both = jnp.concatenate([value, ones], axis=1)
        summed[unit] += jnp.dot(weights.astype(BF16), both, preferred_element_type=F32)

    def second_pass(i, _):
        p = lists[0, i]
        request = (code_ref[p] - 1) >> 7
        for h in range(GH):
            unit = request * GH + h
            weights = jnp.exp2(scores[i, h] - peak[unit])
            weigh(unit, weights, values[p, :, h * HD : (h + 1) * HD])
        return 0

    lax.fori_loop(0, n_pre, second_pass, 0)

    @pl.when(has_own)
    def _():
        for request in range(PRE):
            unit = request * GH + own_head
            result, visible = own_scores(request)
            weigh(unit, jnp.where(visible, jnp.exp2(result - peak[unit]), 0.0), own_values)

    def decode_pass(step_index, _):
        found = []
        for j in range(GROUP):
            position = step_index * GROUP + j
            p = lists[1, jnp.minimum(position, n_dec - 1)]
            code = code_ref[p] - 1
            owner = code >> 7
            token = owner - PRE
            left = jnp.where(position < n_dec, prefix_ref[owner] - (code & 127) * PAGE, 0)
            row = rows_of((8, HD))
            query = jnp.concatenate(
                [
                    jnp.where(row == h, jnp.broadcast_to(dec_query[h, pl.ds(token, 1), :], (8, HD)), 0.0)
                    for h in range(GH)
                ],
                axis=1,
            ).astype(BF16)
            visible = lanes((8, PAGE)) < left
            result = jnp.where(visible, scored(query, keys[p]), NEG)
            top = jnp.max(result, axis=1, keepdims=True)
            weights = jnp.where(visible, jnp.exp2(result - top), 0.0)
            total = jnp.sum(weights, axis=1, keepdims=True)
            product = jnp.dot(weights.astype(BF16), values[p], preferred_element_type=F32)
            found.append((token, top, total, product))
        for token, top, total, product in found:
            before = dec_peak[token]
            after = jnp.maximum(before, top)
            keep = jnp.exp2(before - after)
            take = jnp.exp2(top - after)
            dec_peak[token] = after
            dec_total[token] = dec_total[token] * keep + total * take
            wide = jnp.concatenate([keep] * GH, axis=1)
            wide_take = jnp.concatenate([take] * GH, axis=1)
            dec_sum[token] = dec_sum[token] * wide + product * wide_take
        return 0

    lax.fori_loop(0, (n_dec + GROUP - 1) // GROUP, decode_pass, 0)

    for request in range(PRE):
        for h in range(GH):
            unit = request * GH + h
            total = summed[unit, :, HD:]
            some = total > 0.0
            safe = jnp.where(some, total, 1.0)
            part = pl.ds(request * SPAN, SPAN)
            final[h, part, :] = summed[unit, :, :HD] / safe
            lse[h, part, :] = jnp.where(some, peak[unit] + jnp.log2(safe), NEG)

    first = ROWS - DEC
    dec_rows = pl.ds(PRE * SPAN, DEC)
    for h in range(GH):
        mine = f == h * blocks + blocks - 1
        own = jnp.sum(dec_query[h] * own_ref[0].astype(F32)[first:], axis=1, keepdims=True)
        own = jnp.where(mine, jnp.broadcast_to(own, (DEC, HD)) * SCALE2, NEG)
        before = dec_peak[:, h, :]
        after = jnp.maximum(before, own)
        keep = jnp.exp2(before - after)
        take = jnp.where(mine, jnp.exp2(own - after), 0.0)
        total = dec_total[:, h, :] * keep + take
        value = dec_sum[:, h, h * HD : (h + 1) * HD] * keep
        value = value + take * own_ref[1].astype(F32)[first:]
        some = total > 0.0
        safe = jnp.where(some, total, 1.0)
        final[h, dec_rows, :] = value / safe
        lse[h, dec_rows, :] = jnp.where(some, after + jnp.log2(safe), NEG)

    row = rows_of((16, HD))
    diagonal = (row == lanes((16, HD))) & (row < FEW)
    ffn = out_ref.shape[0] // (TOKENS // QUARTER)
    for q in range(TOKENS // QUARTER):
        for h in range(GH):
            for b in range(QUARTER // FEW):
                part = pl.ds(q * QUARTER + b * FEW, 16)
                stat = jnp.sum(jnp.where(diagonal, lse[h, part, :], 0.0), axis=0, keepdims=True)
                high, middle, low = split3(stat)
                block = jnp.where(row < FEW, final[h, part, :], 0.0)
                block = jnp.where(row == FEW, high, block)
                block = jnp.where(row == FEW + 1, middle, block)
                block = jnp.where(row == FEW + 2, low, block)
                out_ref[q * ffn + h * (QUARTER // FEW) + b] = block.astype(BF16)
        for target in range(GH * (QUARTER // FEW), ffn):
            out_ref[q * ffn + target] = jnp.zeros((16, HD), BF16)


def merge_kernel(in_ref, out_ref):
    sources = out_ref.shape[0]
    groups = in_ref.shape[0] // sources
    row = rows_of((16, HD))
    all_weights = []
    for g in range(groups):
        stats = jnp.concatenate(
            [
                jnp.sum(
                    jnp.where(row >= FEW, in_ref[g * sources + s].astype(F32), 0.0),
                    axis=0,
                    keepdims=True,
                )
                for s in range(sources)
            ],
            axis=0,
        )
        weights = jnp.exp2(stats - jnp.max(stats, axis=0, keepdims=True))
        all_weights.append(weights / jnp.sum(weights, axis=0, keepdims=True))
    turned = jnp.transpose(jnp.concatenate(all_weights, axis=0))
    pieces = []
    for g in range(groups):
        total = jnp.zeros((16, HD), F32)
        for s in range(sources):
            source = g * sources + s
            total = total + turned[:16, source : source + 1] * in_ref[source].astype(F32)
        pieces.append(total[:FEW])
    result = jnp.concatenate(pieces, axis=0).astype(BF16)
    for s in range(sources):
        out_ref[s] = result


def output_kernel(g_ref, in_ref, x_ref, *refs):
    *w_refs, own_ref, out_ref, spread, heads, product = refs
    blocks = QUARTER // FEW
    groups = len(w_refs)
    for source in range(GH * blocks):
        spread[source, :ROWS, :] = in_ref[source].astype(F32)
        spread[source, ROWS:, :] = jnp.zeros((16, HD), F32)
    for g in range(groups):
        for h in range(GH):
            for b in range(blocks):
                heads[g, b * 16 : (b + 1) * 16, h * HD : (h + 1) * HD] = spread[
                    h * blocks + b, g * FEW : g * FEW + 16, :
                ].astype(BF16)
    attended = jnp.zeros((16 * blocks, COLS), F32)
    for s in range(groups):
        source = lax.rem(g_ref[0] + groups - s, groups)
        attended = attended + turned_dot(heads[source], w_refs[s][...])
    for b in range(blocks):
        product[b * FEW : (b + 1) * FEW, :] = attended[b * 16 : b * 16 + FEW]
    x = x_ref[...].astype(F32)
    own = jnp.zeros((QUARTER, COLS), F32)
    for i in range(groups):
        own = jnp.where(g_ref[0] == i, x[i * QUARTER : (i + 1) * QUARTER], own)
    own = (own + product[...]).astype(BF16)
    own_ref[...] = own
    message = packed(own.astype(F32))
    for s in range(out_ref.shape[0]):
        out_ref[s] = message


def packed(value):
    third = QUARTER // 3
    tail = value[:, HD:]
    extra = jnp.concatenate(
        [tail[i * third : (i + 1) * third] for i in range(3)]
        + [jnp.zeros((third, HD - 3 * (COLS - HD)), F32)],
        axis=1,
    )
    return jnp.concatenate([value[:, :HD], extra], axis=0).astype(BF16)


def unpacked(message):
    third = QUARTER // 3
    wide = COLS - HD
    extra = message[QUARTER:]
    tail = jnp.concatenate([extra[:, i * wide : (i + 1) * wide] for i in range(3)], axis=0)
    assert tail.shape == (3 * third, wide)
    return jnp.concatenate([message[:QUARTER], tail], axis=1)


def turned_dot(left, right):
    return lax.dot_general(left, right, (((1,), (1,)), ((), ())), preferred_element_type=F32)


def ffn_kernel(
    in_ref, gain_ref, gate_hbm, down_hbm, out_ref, rows, normed, gates, down, sems
):
    copies = []
    for c in range(D // FCHUNK):
        part = pl.ds(c * FCHUNK, FCHUNK)
        copies.append(
            pltpu.make_async_copy(gate_hbm.at[:, :, part], gates.at[:, :, part], sems.at[c])
        )
    copies.append(pltpu.make_async_copy(down_hbm, down, sems.at[D // FCHUNK]))
    for copy in copies:
        copy.start()
    for s in range(in_ref.shape[0]):
        rows[:, s * COLS : (s + 1) * COLS] = unpacked(in_ref[s].astype(F32))
    full = rows[...]
    inverse = lax.rsqrt(jnp.sum(full * full, axis=1, keepdims=True) / D + EPS)
    normed[...] = (full * inverse * gain_ref[...]).astype(BF16)
    hidden_units = down.shape[0]
    gate = jnp.zeros((QUARTER, hidden_units), F32)
    up = jnp.zeros((QUARTER, hidden_units), F32)
    for c in range(D // FCHUNK):
        copies[c].wait()
        part = pl.ds(c * FCHUNK, FCHUNK)
        block = normed[:, part]
        gate = gate + turned_dot(block, gates[0, :, part])
        up = up + turned_dot(block, gates[1, :, part])
    hidden = (gate / (1.0 + jnp.exp(-gate)) * up).astype(BF16)
    copies[-1].wait()
    wide = 4 * COLS
    for s in range(in_ref.shape[0] // 4):
        product = jnp.dot(
            hidden, down[:, s * wide : (s + 1) * wide], preferred_element_type=F32
        )
        for j in range(4):
            out_ref[4 * s + j] = packed(product[:, j * COLS : (j + 1) * COLS])


def finish_kernel(in_ref, own_ref, out_ref):
    total = in_ref[0].astype(F32)
    for s in range(1, in_ref.shape[0]):
        total = total + in_ref[s].astype(F32)
    out_ref[...] = (own_ref[...].astype(F32) + unpacked(total)).astype(BF16)


def call(kernel, out, specs, scratch=(), out_specs=None):
    function = pl.pallas_call(
        kernel,
        out_shape=out,
        in_specs=specs,
        out_specs=out_specs if out_specs is not None else vmem,
        scratch_shapes=list(scratch),
        compiler_params=params(),
    )

    def placed(*args):
        return function(
            *[
                pltpu.with_memory_space_constraint(a, pltpu.HBM) if spec is hbm else a
                for a, spec in zip(args, specs)
            ]
        )

    return placed


def shape(*dims, kind=BF16):
    return jax.ShapeDtypeStruct(dims, kind)


def swap(value, axis):
    return lax.all_to_all(value, axis, 0, 0)


def tables(f, span_offsets, decode_lengths):
    within = jnp.arange(SPAN, dtype=jnp.int32)
    prefill = (span_offsets[:, None] + within[None, :]).reshape(PRE * SPAN)
    positions = jnp.concatenate([prefill, decode_lengths])
    block = lax.rem(f, TOKENS // ROWS)
    positions = lax.dynamic_slice_in_dim(positions, block * ROWS, ROWS)
    half_width = HD // 2
    lane = jnp.arange(HD, dtype=jnp.int32)
    frequency = jnp.exp((lane % half_width).astype(F32) * (-2.0 * math.log(10000.0) / HD))
    angles = positions.astype(F32)[:, None] * frequency[None, :]
    sine = jnp.sin(angles) * jnp.where(lane < half_width, -1.0, 1.0)[None, :]
    return jnp.cos(angles), sine


def shards(
    layer_input,
    norm_gain,
    qkv_weight,
    key_cache,
    value_cache,
    out_weight,
    ffn_gain,
    gate_up_weight,
    down_weight,
    span_offsets,
    decode_lengths,
    page_table,
):
    ffn = lax.axis_size("ffn")
    grp = lax.axis_size("grp")
    f = lax.axis_index("ffn")
    g = lax.axis_index("grp")
    f1 = f.astype(jnp.int32).reshape(1)
    g1 = g.astype(jnp.int32).reshape(1)
    pages = key_cache.shape[0]
    hidden_units = down_weight.shape[0]

    cosine, sine = tables(f, span_offsets, decode_lengths)
    local_ids = f * pages + jnp.arange(pages, dtype=jnp.int32)
    requests = PRE + DEC
    numbers = jnp.arange(requests * MAXP, dtype=jnp.int32).reshape(requests, MAXP) + 1
    codes = jnp.sum(
        jnp.where(page_table[None] == local_ids[:, None, None], numbers[None], 0), axis=(1, 2)
    )
    prefixes = jnp.concatenate([span_offsets, decode_lengths])

    partial = call(
        project_kernel,
        shape(ffn, 3 * ROWS + STATS, HD),
        [hbm, hbm, hbm],
        [
            pltpu.VMEM((COLS, TOKENS), BF16),
            pltpu.VMEM((1, COLS), F32),
            pltpu.VMEM(qkv_weight.shape, BF16),
            pltpu.SemaphoreType.DMA((5,)),
        ],
    )(layer_input.T, norm_gain.reshape(1, -1), qkv_weight)
    turned_weight, partial = lax.optimization_barrier((out_weight.T, partial))
    out_weights = [turned_weight] + [
        lax.ppermute(turned_weight, "grp", [(i, (i + s) % grp) for i in range(grp)])
        for s in range(1, grp)
    ]
    partial, *out_weights = lax.optimization_barrier((swap(partial, "ffn"), *out_weights))
    fresh, own_block = call(
        rotate_kernel,
        (shape(ffn, ROWS, HD), shape(2, ROWS, HD)),
        [vmem] * 3,
        out_specs=(vmem, vmem),
    )(partial, cosine, sine)
    fresh = swap(fresh, "ffn").reshape(ffn * ROWS, HD)
    units = PRE * GH
    message = call(
        attention_kernel,
        shape(grp * ffn, 16, HD),
        [smem] * 3 + [vmem] * 2 + [hbm] * 2,
        [
            pltpu.VMEM((pages, PAGE, GH * HD), BF16),
            pltpu.VMEM((pages, PAGE, GH * HD), BF16),
            pltpu.SemaphoreType.DMA((2, CHUNKS)),
            pltpu.SMEM((2, pages), jnp.int32),
            pltpu.VMEM((pages, GH, SPAN, PAGE), F32),
            pltpu.VMEM((units, SPAN, PAGE), F32),
            pltpu.VMEM((units, SPAN, 2 * HD), F32),
            pltpu.VMEM((GH, DEC, HD), F32),
            pltpu.VMEM((DEC, 8, HD), F32),
            pltpu.VMEM((DEC, 8, HD), F32),
            pltpu.VMEM((DEC, 8, GH * HD), F32),
            pltpu.VMEM((GH, TOKENS + 16, HD), F32),
            pltpu.VMEM((GH, TOKENS + 16, HD), F32),
        ],
    )(codes, prefixes, f1, fresh, own_block, key_cache, value_cache)
    message = swap(message, ("grp", "ffn"))
    heads = call(merge_kernel, shape(ffn, ROWS, HD), [vmem])(message)
    heads = swap(heads, "ffn")
    own, rows = call(
        output_kernel,
        (shape(QUARTER, COLS), shape(ffn, MSG, HD)),
        [smem] + [vmem] * (2 + grp),
        [
            pltpu.VMEM((GH * (QUARTER // FEW), ROWS + 16, HD), F32),
            pltpu.VMEM((grp, 16 * (QUARTER // FEW), GH * HD), BF16),
            pltpu.VMEM((QUARTER, COLS), F32),
        ],
        out_specs=(vmem, vmem),
    )(g1, heads, layer_input, *out_weights)
    rows = swap(rows, "ffn")

    down_terms = call(
        ffn_kernel,
        shape(ffn, MSG, HD),
        [vmem] * 2 + [hbm] * 2,
        [
            pltpu.VMEM((QUARTER, D), F32),
            pltpu.VMEM((QUARTER, D), BF16),
            pltpu.VMEM((2, hidden_units, D), BF16),
            pltpu.VMEM((hidden_units, D), BF16),
            pltpu.SemaphoreType.DMA((D // FCHUNK + 1,)),
        ],
    )(rows, ffn_gain.reshape(1, -1), jnp.swapaxes(gate_up_weight, 1, 2), down_weight)
    down_terms = swap(down_terms, "ffn")
    return call(finish_kernel, shape(QUARTER, COLS), [vmem] * 2)(down_terms, own)


def solution(mesh):
    in_specs = (
        P(None, "ffn"),
        P("ffn"),
        P(None, "ffn", "grp"),
        P("ffn", None, "grp"),
        P("ffn", None, "grp"),
        P("grp", "ffn"),
        P(),
        P(None, None, "ffn"),
        P("ffn", None),
        P(),
        P(),
        P(),
    )
    out_specs = P("grp", "ffn")
    return jax.shard_map(shards, mesh=mesh, in_specs=in_specs, out_specs=out_specs, check_vma=False)
```

time: 162 us -> 141 us (0.87)
  waiting for transfers between devices: 52.1 us -> 32.6 us
  local copies, waits for them, and re-layouts: 18.5 us -> 0.14 us
  blocking collectives: 36.3 us -> 54 us
  starting transfers between devices: 26 us -> 23.1 us
  Pallas kernels: 25.6 us -> 28.1 us
    all_to_all x5 -> x3, waiting for transfers between devices: 52.1 us -> 25.8 us  [swap(): return lax.all_to_all(value, axis, 0, 0)]
    unnamed x19 -> x13, local copies, waits for them, and re-layouts: 18.5 us -> 0.14 us
    all_to_all x2 -> x3, blocking collectives: 36.3 us -> 54 us  [swap(): return lax.all_to_all(value, axis, 0, 0)]
    all_to_all x5 -> x3, starting transfers between devices: 26 us -> 18.1 us  [swap(): return lax.all_to_all(value, axis, 0, 0)]
    ppermute x0 -> x3, waiting for transfers between devices: none -> 6.86 us  [shards(): lax.ppermute(turned_weight, 'grp', [(i, (i + s) % grp) for i in range(grp)])]
    ppermute x0 -> x3, starting transfers between devices: none -> 5.06 us  [shards(): lax.ppermute(turned_weight, 'grp', [(i, (i + s) % grp) for i in range(grp)])]
    pallas_call x8 -> x7, Pallas kernels: 25.6 us -> 28.1 us  [placed(): function(*[pltpu.with_memory_space_constraint(a, pltpu.HBM) if spec is hb...]
  transfers between devices with their start and end apart: 5 -> 6, of which waited for: 5 -> 5; matrix products, arithmetic and copies ran while one was open for 9% -> 1% of each run, Pallas kernels for 0% -> 0%
where the time goes in v1:
time: 141 us; the launch traced here: 140 us
  blocking collectives  54 us (38%)
  waiting for transfers between devices  32.6 us (23%)
  Pallas kernels  28.1 us (20%)
  starting transfers between devices  23.1 us (16%)
  other arithmetic  1.98 us (1%)
    all_to_all x3, blocking collectives, swap(): return lax.all_to_all(value, axis, 0, 0)  54 us
    pallas_call x7, Pallas kernels, placed(): function(*[pltpu.with_memory_space_constraint(a, pltpu.HBM) if spec is hb...  28.1 us
    all_to_all x3, waiting for transfers between devices, swap(): return lax.all_to_all(value, axis, 0, 0)  25.8 us
    all_to_all x3, starting transfers between devices, swap(): return lax.all_to_all(value, axis, 0, 0)  18.1 us
    ppermute x3, waiting for transfers between devices, shards(): lax.ppermute(turned_weight, 'grp', [(i, (i + s) % grp) for i in range(grp)])  6.86 us
    ppermute x3, starting transfers between devices, shards(): lax.ppermute(turned_weight, 'grp', [(i, (i + s) % grp) for i in range(grp)])  5.06 us
  transfers between devices with their start and end apart: 6, of which 5 were waited for; matrix products, arithmetic and copies ran while one was open for 1% of the time, Pallas kernels for 0%

profile of v1, /device:TPU:1, one launch (start us, length us, event | category | flops | bytes accessed | tf_op | source)
XLA Modules:
  0.0 140.1 jit_solution(611649912446548053)
XLA Ops:
  0.0 3.2 %shard_map.118 = bf16[32,152,128]{2,1,0:T(8,128)(2,1)} custom-call(bf16[160,288]{1,0:T(8,128)(2,1)} %bitcast.17, f32[1,160]{1,0:T(1,128)} %bitcast.18, bf16[3,160,640]{2,1,0:T(8,128)(2,1)} %w_hbm.1), custom_call_target="tpu_custom_call" | custom-call | tf_op jit(solution)/shard_map/pallas_call | solution.py:495
  3.2 9.4 %all-to-all-start = ((bf16[32,152,128]{2,1,0:T(8,128)(2,1)}), bf16[32,152,128]{2,1,0:T(8,128)(2,1)S(1)}, u32[]{:S(2)}, u32[]{:S(2)}) async-start(bf16[32,152,128]{2,1,0:T(8,128)(2,1)} %shard_map.118), calls=%async_computation | async-start | bytes 2490368 | tf_op jit(solution)/shard_map/all_to_all | solution.py:510
  12.7 1.4 collective-permute-start
  14.0 2.6 %collective-permute-start.1 = (bf16[160,640]{1,0:T(8,128)(2,1)}, bf16[160,640]{1,0:T(8,128)(2,1)S(1)}, u32[]{:S(2)}, u32[]{:S(2)}) collective-permute-start(bf16[160,640]{1,0:T(8,128)(2,1)} %bitcast.12), channel_id=1, source_target_pairs={{0,64},{32,96},{64,0},{96,32},{1,65},{33,97},{65,1},{97,33},{2,66}... | collective-permute-start | bytes 614408 | tf_op jit(solution)/shard_map/ppermute | solution.py:572
  16.6 1.1 collective-permute-start.2
  17.7 0.7 add_bitcast_fusion
  18.4 0.7 pad_add_fusion
  19.4 1.4 collective-permute-done.refs_1_
  20.7 5.5 %collective-permute-done.1.refs_2_ = bf16[160,640]{1,0:T(8,128)(2,1)S(1)} collective-permute-done((bf16[160,640]{1,0:T(8,128)(2,1)}, bf16[160,640]{1,0:T(8,128)(2,1)S(1)}, u32[]{:S(2)}, u32[]{:S(2)}) %collective-permute-start.1) | collective-permute-done | bytes 204832 | tf_op jit(solution)/shard_map/ppermute | solution.py:572
  26.2 5.5 %all-to-all-done.in_ref = bf16[32,152,128]{2,1,0:T(8,128)(2,1)S(1)} async-done(((bf16[32,152,128]{2,1,0:T(8,128)(2,1)}), bf16[32,152,128]{2,1,0:T(8,128)(2,1)S(1)}, u32[]{:S(2)}, u32[]{:S(2)}) %all-to-all-start) | async-done | bytes 1245216 | tf_op jit(solution)/shard_map/all_to_all | solution.py:510
  31.7 1.0 shard_map.119
  32.7 3.9 %all-to-all-start.1 = ((bf16[32,48,128]{2,1,0:T(8,128)(2,1)}), bf16[32,48,128]{2,1,0:T(8,128)(2,1)S(1)}, u32[]{:S(2)}, u32[]{:S(2)}) async-start(bf16[32,48,128]{2,1,0:T(8,128)(2,1)} %get-tuple-element.19), calls=%async_computation.1 | async-start | bytes 786432 | tf_op jit(solution)/shard_map/all_to_all | solution.py:510
  36.7 0.2 select_reduce_fusion.code_ref
  37.0 10.0 %all-to-all-done.1 = bf16[32,48,128]{2,1,0:T(8,128)(2,1)S(1)} async-done(((bf16[32,48,128]{2,1,0:T(8,128)(2,1)}), bf16[32,48,128]{2,1,0:T(8,128)(2,1)S(1)}, u32[]{:S(2)}, u32[]{:S(2)}) %all-to-all-start.1) | async-done | bytes 393248 | tf_op jit(solution)/shard_map/all_to_all | solution.py:510
  47.0 13.6 %shard_map.120 = bf16[128,16,128]{2,1,0:T(8,128)(2,1)S(1)} custom-call(s32[28]{0:T(128)S(1)} %select_reduce_fusion.code_ref, s32[34]{0:T(128)S(1)} %pad_add_fusion.1.prefix_ref, s32[1]{0:T(128)} %bitcast.1.f_ref, bf16[1536,128]{1,0:T(8,128)(2,1)S(1)} %bitcast.10, bf16[2,48,128]{2,1,0:T(8,128)(2,1)S(1)} %get-tuple-element.20.own_ref, ...), custom_call_target="tpu_custom_call" | custom-call | tf_op jit(solution)/shard_map/pallas_call | solution.py:495
  60.6 18.6 %all_to_all.30.in_ref = bf16[128,16,128]{2,1,0:T(8,128)(2,1)S(1)} all-to-all(bf16[128,16,128]{2,1,0:T(8,128)(2,1)S(1)} %shard_map.120), channel_id=1, replica_groups=mesh['grp'=4,'ffn'=32] {'grp','ffn'}, dimensions={0} | all-to-all | bytes 1048576 | tf_op jit(solution)/shard_map/all_to_all | solution.py:510
  79.2 1.5 %shard_map.121 = bf16[32,48,128]{2,1,0:T(8,128)(2,1)} custom-call(bf16[128,16,128]{2,1,0:T(8,128)(2,1)S(1)} %all_to_all.30.in_ref), custom_call_target="tpu_custom_call" | custom-call | tf_op jit(solution)/shard_map/pallas_call | solution.py:495
  80.7 4.7 %all-to-all-start.3 = ((bf16[32,48,128]{2,1,0:T(8,128)(2,1)}), bf16[32,48,128]{2,1,0:T(8,128)(2,1)S(1)}, u32[]{:S(2)}, u32[]{:S(2)}) async-start(bf16[32,48,128]{2,1,0:T(8,128)(2,1)} %shard_map.121), calls=%async_computation.3 | async-start | bytes 786432 | tf_op jit(solution)/shard_map/all_to_all | solution.py:510
  85.6 10.3 %all-to-all-done.3.in_ref = bf16[32,48,128]{2,1,0:T(8,128)(2,1)S(1)} async-done(((bf16[32,48,128]{2,1,0:T(8,128)(2,1)}), bf16[32,48,128]{2,1,0:T(8,128)(2,1)S(1)}, u32[]{:S(2)}, u32[]{:S(2)}) %all-to-all-start.3) | async-done | bytes 393248 | tf_op jit(solution)/shard_map/all_to_all | solution.py:510
  95.9 0.6 shard_map.122
  96.5 17.5 %all_to_all.31.in_ref = bf16[32,96,128]{2,1,0:T(8,128)(2,1)S(1)} all-to-all(bf16[32,96,128]{2,1,0:T(8,128)(2,1)S(1)} %get-tuple-element.25), channel_id=1, replica_groups=mesh['grp'=4,'ffn'=32] {'ffn'}, dimensions={0} | all-to-all | bytes 1572864 | tf_op jit(solution)/shard_map/all_to_all | solution.py:510
  114.1 7.5 %shard_map.123 = bf16[32,96,128]{2,1,0:T(8,128)(2,1)S(1)} custom-call(bf16[32,96,128]{2,1,0:T(8,128)(2,1)S(1)} %all_to_all.31.in_ref, f32[1,5120]{1,0:T(1,128)S(1)} %bitcast.15, bf16[2,432,5120]{2,1,0:T(8,128)(2,1)} %bitcast.16, bf16[432,5120]{1,0:T(8,128)(2,1)} %down_hbm.1), custom_call_target="tpu_custom_call" | custom-call | tf_op jit(solution)/shard_map/pallas_call | solution.py:495
  121.5 17.9 %all_to_all.32.in_ref = bf16[32,96,128]{2,1,0:T(8,128)(2,1)S(1)} all-to-all(bf16[32,96,128]{2,1,0:T(8,128)(2,1)S(1)} %shard_map.123), channel_id=1, replica_groups=mesh['grp'=4,'ffn'=32] {'ffn'}, dimensions={0} | all-to-all | bytes 1572864 | tf_op jit(solution)/shard_map/all_to_all | solution.py:510
  139.4 0.7 shard_map.124
  (20 shorter events, 0.5 us)
Async XLA Ops:
  0.0 36.6 %copy-start.5 = (s32[2]{0:T(128)S(1)}, s32[2]{0:T(128)}, u32[]{:S(2)}) copy-start(s32[2]{0:T(128)} %param.21) | copy-start | bytes 28
  0.0 36.6 %copy-start.4 = (s32[32]{0:T(128)S(1)}, s32[32]{0:T(128)}, u32[]{:S(2)}) copy-start(s32[32]{0:T(128)} %param.22) | copy-start | bytes 388
  0.0 36.7 %copy-start.3 = (s32[34,128]{1,0:T(8,128)S(1)}, s32[34,128]{1,0:T(8,128)}, u32[]{:S(2)}) copy-start(s32[34,128]{1,0:T(8,128)} %param.23) | copy-start | bytes 52228
  3.2 28.5 %all-to-all-start = ((bf16[32,152,128]{2,1,0:T(8,128)(2,1)}), bf16[32,152,128]{2,1,0:T(8,128)(2,1)S(1)}, u32[]{:S(2)}, u32[]{:S(2)}) async-start(bf16[32,152,128]{2,1,0:T(8,128)(2,1)} %shard_map.118), calls=%async_computation | async-start | bytes 2490368 | tf_op jit(solution)/shard_map/all_to_all | solution.py:510
  12.7 8.1 %collective-permute-start = (bf16[160,640]{1,0:T(8,128)(2,1)}, bf16[160,640]{1,0:T(8,128)(2,1)S(1)}, u32[]{:S(2)}, u32[]{:S(2)}) collective-permute-start(bf16[160,640]{1,0:T(8,128)(2,1)} %bitcast.11), channel_id=1, source_target_pairs={{0,32},{32,64},{64,96},{96,0},{1,33},{33,65},{65,97},{97,1},{2,34}... | collective-permute-start | bytes 614408 | tf_op jit(solution)/shard_map/ppermute | solution.py:572
  14.0 12.2 %collective-permute-start.1 = (bf16[160,640]{1,0:T(8,128)(2,1)}, bf16[160,640]{1,0:T(8,128)(2,1)S(1)}, u32[]{:S(2)}, u32[]{:S(2)}) collective-permute-start(bf16[160,640]{1,0:T(8,128)(2,1)} %bitcast.12), channel_id=1, source_target_pairs={{0,64},{32,96},{64,0},{96,32},{1,65},{33,97},{65,1},{97,33},{2,66}... | collective-permute-start | bytes 614408 | tf_op jit(solution)/shard_map/ppermute | solution.py:572
  16.6 9.6 %collective-permute-start.2 = (bf16[160,640]{1,0:T(8,128)(2,1)}, bf16[160,640]{1,0:T(8,128)(2,1)S(1)}, u32[]{:S(2)}, u32[]{:S(2)}) collective-permute-start(bf16[160,640]{1,0:T(8,128)(2,1)} %bitcast.13), channel_id=1, source_target_pairs={{0,96},{32,0},{64,32},{96,64},{1,97},{33,1},{65,33},{97,65},{2,98}... | collective-permute-start | bytes 614408 | tf_op jit(solution)/shard_map/ppermute | solution.py:572
  32.7 14.3 %all-to-all-start.1 = ((bf16[32,48,128]{2,1,0:T(8,128)(2,1)}), bf16[32,48,128]{2,1,0:T(8,128)(2,1)S(1)}, u32[]{:S(2)}, u32[]{:S(2)}) async-start(bf16[32,48,128]{2,1,0:T(8,128)(2,1)} %get-tuple-element.19), calls=%async_computation.1 | async-start | bytes 786432 | tf_op jit(solution)/shard_map/all_to_all | solution.py:510
  47.0 38.5 %copy-start.2 = (bf16[288,160]{0,1:T(8,128)(2,1)S(1)}, bf16[288,160]{0,1:T(8,128)(2,1)}, u32[]{:S(2)}) copy-start(bf16[288,160]{0,1:T(8,128)(2,1)} %param.12) | copy-start | bytes 276484
  47.0 48.9 %copy-start = (bf16[640,160]{0,1:T(8,128)(2,1)S(1)}, bf16[640,160]{0,1:T(8,128)(2,1)}, u32[]{:S(2)}) copy-start(bf16[640,160]{0,1:T(8,128)(2,1)} %param.17) | copy-start | bytes 614404
  60.6 53.5 %copy-start.1 = (f32[5120]{0:T(1024)S(1)}, f32[5120]{0:T(1024)}, u32[]{:S(2)}) copy-start(f32[5120]{0:T(1024)} %param.18) | copy-start | bytes 61444
  80.7 15.2 %all-to-all-start.3 = ((bf16[32,48,128]{2,1,0:T(8,128)(2,1)}), bf16[32,48,128]{2,1,0:T(8,128)(2,1)S(1)}, u32[]{:S(2)}, u32[]{:S(2)}) async-start(bf16[32,48,128]{2,1,0:T(8,128)(2,1)} %shard_map.121), calls=%async_computation.3 | async-start | bytes 786432 | tf_op jit(solution)/shard_map/all_to_all | solution.py:510

commit v2 on v1

--- a/solution.py
+++ b/solution.py
@@ -32,7 +32,7 @@
 LIMIT = 32 << 20
 GROUP = 4
 CHUNKS = 4
-FCHUNK = 512
+FCHUNK = 640
 
 vmem = pl.BlockSpec(memory_space=pltpu.VMEM)
 smem = pl.BlockSpec(memory_space=pltpu.SMEM)
@@ -119,8 +119,9 @@
 
 
 def attention_kernel(
-    code_ref,
-    prefix_ref,
+    lists,
+    left_ref,
+    token_ref,
     f_ref,
     fresh_ref,
     own_ref,
@@ -130,7 +131,6 @@
     keys,
     values,
     sems,
-    lists,
     scores,
     peak,
     summed,
@@ -164,26 +164,8 @@
     for h in range(GH):
         dec_query[h] = fresh_ref[h * TOKENS + PRE * SPAN : (h + 1) * TOKENS, :].astype(F32)
 
-    def classify(p, counts):
-        n_pre, n_dec = counts
-        code = code_ref[p]
-        owner = (code - 1) >> 7
-        slot = (code - 1) & 127
-        live = (code > 0) & (slot * PAGE < prefix_ref[jnp.maximum(owner, 0)])
-        is_pre = live & (owner < PRE)
-        is_dec = live & (owner >= PRE)
-
-        @pl.when(is_pre)
-        def _():
-            lists[0, n_pre] = p
-
-        @pl.when(is_dec)
-        def _():
-            lists[1, n_dec] = p
-
-        return n_pre + is_pre.astype(jnp.int32), n_dec + is_dec.astype(jnp.int32)
-
-    n_pre, n_dec = lax.fori_loop(0, pages, classify, (0, 0))
+    n_pre = [lists[k, pages] for k in range(PRE)]
+    n_dec = lists[PRE, pages]
 
     f = f_ref[0]
     blocks = TOKENS // ROWS
@@ -219,21 +201,35 @@
     for copy in copies[:CHUNKS]:
         copy.wait()
 
-    def first_pass(i, _):
-        p = lists[0, i]
-        code = code_ref[p] - 1
-        request = code >> 7
-        left = prefix_ref[request] - (code & 127) * PAGE
-        visible = lanes((SPAN, PAGE)) < left
-        for h in range(GH):
-            result = scored(query_rows(request, h), keys[p, :, h * HD : (h + 1) * HD])
-            result = jnp.where(visible, result, NEG)
-            scores[i, h] = result
-            unit = request * GH + h
-            peak[unit] = jnp.maximum(peak[unit], result)
-        return 0
-
-    lax.fori_loop(0, n_pre, first_pass, 0)
+    def pair(request, i):
+        last = n_pre[request] - 1
+        first_page = lists[request, 2 * i]
+        second_page = lists[request, jnp.minimum(2 * i + 1, last)]
+        return first_page, second_page
+
+    def joined(ref, pages_of, h):
+        return jnp.concatenate([ref[p, :, h * HD : (h + 1) * HD] for p in pages_of], axis=0)
+
+    wide_lane = lanes((SPAN, 2 * PAGE))
+    pairs = [(n + 1) >> 1 for n in n_pre]
+    for request in range(PRE):
+
+        def first_pass(i, _, request=request):
+            both = pair(request, i)
+            left = left_ref[both[0]]
+            other = jnp.where(2 * i + 1 < n_pre[request], left_ref[both[1]], 0) + PAGE
+            visible = wide_lane < jnp.where(wide_lane < PAGE, left, other)
+            for h in range(GH):
+                result = scored(query_rows(request, h), joined(keys, both, h))
+                result = jnp.where(visible, result, NEG)
+                scores[i + request * pairs[0], h] = result
+                unit = request * GH + h
+                peak[unit] = jnp.maximum(
+                    peak[unit], jnp.maximum(result[:, :PAGE], result[:, PAGE:])
+                )
+            return 0
+
+        lax.fori_loop(0, pairs[request], first_pass, 0)
 
     for unit in range(PRE * GH):
         peak[unit] = jnp.broadcast_to(
@@ -243,22 +239,24 @@
     for copy in copies[CHUNKS:]:
         copy.wait()
 
-    ones = jnp.ones((PAGE, HD), BF16)
-
     def weigh(unit, weights, value):
+        ones = jnp.ones((value.shape[0], HD), BF16)
         both = jnp.concatenate([value, ones], axis=1)
         summed[unit] += jnp.dot(weights.astype(BF16), both, preferred_element_type=F32)
 
-    def second_pass(i, _):
-        p = lists[0, i]
-        request = (code_ref[p] - 1) >> 7
-        for h in range(GH):
-            unit = request * GH + h
-            weights = jnp.exp2(scores[i, h] - peak[unit])
-            weigh(unit, weights, values[p, :, h * HD : (h + 1) * HD])
-        return 0
-
-    lax.fori_loop(0, n_pre, second_pass, 0)
+    for request in range(PRE):
+
+        def second_pass(i, _, request=request):
+            both = pair(request, i)
+            for h in range(GH):
+                unit = request * GH + h
+                top = peak[unit]
+                top = jnp.concatenate([top, top], axis=1)
+                weights = jnp.exp2(scores[i + request * pairs[0], h] - top)
+                weigh(unit, weights, joined(values, both, h))
+            return 0
+
+        lax.fori_loop(0, pairs[request], second_pass, 0)
 
     @pl.when(has_own)
     def _():
@@ -267,30 +265,52 @@
             result, visible = own_scores(request)
             weigh(unit, jnp.where(visible, jnp.exp2(result - peak[unit]), 0.0), own_values)
 
+    tall = (8 * GROUP, GROUP * PAGE)
+    owner_row = rows_of(tall) >> 3
+
     def decode_pass(step_index, _):
-        found = []
+        tokens, picked, queries = [], [], []
+        limit = jnp.zeros(tall, jnp.int32)
+        row = rows_of((8, HD))
         for j in range(GROUP):
             position = step_index * GROUP + j
-            p = lists[1, jnp.minimum(position, n_dec - 1)]
-            code = code_ref[p] - 1
-            owner = code >> 7
-            token = owner - PRE
-            left = jnp.where(position < n_dec, prefix_ref[owner] - (code & 127) * PAGE, 0)
-            row = rows_of((8, HD))
-            query = jnp.concatenate(
-                [
-                    jnp.where(row == h, jnp.broadcast_to(dec_query[h, pl.ds(token, 1), :], (8, HD)), 0.0)
-                    for h in range(GH)
-                ],
-                axis=1,
-            ).astype(BF16)
-            visible = lanes((8, PAGE)) < left
-            result = jnp.where(visible, scored(query, keys[p]), NEG)
-            top = jnp.max(result, axis=1, keepdims=True)
-            weights = jnp.where(visible, jnp.exp2(result - top), 0.0)
-            total = jnp.sum(weights, axis=1, keepdims=True)
-            product = jnp.dot(weights.astype(BF16), values[p], preferred_element_type=F32)
-            found.append((token, top, total, product))
+            p = lists[PRE, jnp.minimum(position, n_dec - 1)]
+            token = token_ref[p]
+            left = jnp.where(position < n_dec, left_ref[p], 0)
+            limit = jnp.where(owner_row == j, j * PAGE + left, limit)
+            tokens.append(token)
+            picked.append(p)
+            queries.append(
+                jnp.concatenate(
+                    [
+                        jnp.where(
+                            row == h,
+                            jnp.broadcast_to(dec_query[h, pl.ds(token, 1), :], (8, HD)),
+                            0.0,
+                        )
+                        for h in range(GH)
+                    ],
+                    axis=1,
+                )
+            )
+        query = jnp.concatenate(queries, axis=0).astype(BF16)
+        many_keys = jnp.concatenate([keys[p] for p in picked], axis=0)
+        many_values = jnp.concatenate([values[p] for p in picked], axis=0)
+        visible = (lanes(tall) >= owner_row * PAGE) & (lanes(tall) < limit)
+        result = jnp.where(visible, scored(query, many_keys), NEG)
+        tops = jnp.max(result, axis=1, keepdims=True)
+        weights = jnp.where(visible, jnp.exp2(result - tops), 0.0)
+        totals = jnp.sum(weights, axis=1, keepdims=True)
+        products = jnp.dot(weights.astype(BF16), many_values, preferred_element_type=F32)
+        found = [
+            (
+                tokens[j],
+                tops[8 * j : 8 * j + 8],
+                totals[8 * j : 8 * j + 8],
+                products[8 * j : 8 * j + 8],
+            )
+            for j in range(GROUP)
+        ]
         for token, top, total, product in found:
             before = dec_peak[token]
             after = jnp.maximum(before, top)
@@ -383,7 +403,7 @@
         out_ref[s] = result
 
 
-def output_kernel(g_ref, in_ref, x_ref, *refs):
+def output_kernel(g_ref, f_ref, in_ref, x_ref, *refs):
     *w_refs, own_ref, out_ref, spread, heads, product = refs
     blocks = QUARTER // FEW
     groups = len(w_refs)
@@ -408,7 +428,7 @@
         own = jnp.where(g_ref[0] == i, x[i * QUARTER : (i + 1) * QUARTER], own)
     own = (own + product[...]).astype(BF16)
     own_ref[...] = own
-    message = packed(own.astype(F32))
+    message = turned_lanes(packed(own.astype(F32)), lax.rem(f_ref[0], 4)).astype(BF16)
     for s in range(out_ref.shape[0]):
         out_ref[s] = message
 
@@ -421,7 +441,7 @@
         + [jnp.zeros((third, HD - 3 * (COLS - HD)), F32)],
         axis=1,
     )
-    return jnp.concatenate([value[:, :HD], extra], axis=0).astype(BF16)
+    return jnp.concatenate([value[:, :HD], extra], axis=0)
 
 
 def unpacked(message):
@@ -437,8 +457,50 @@
     return lax.dot_general(left, right, (((1,), (1,)), ((), ())), preferred_element_type=F32)
 
 
+def turned_lanes(message, amount):
+    result = message
+    for j in range(1, 4):
+        result = jnp.where(amount == j, pltpu.roll(message, 32 * j, 1), result)
+    return result
+
+
+def tiles_of(messages):
+    third = QUARTER // 3
+    lane = lanes((QUARTER, HD))
+    heads = [m[:QUARTER] for m in messages]
+    tails = [
+        jnp.concatenate(
+            [m[QUARTER:]] + [pltpu.roll(m[QUARTER:], HD - 32 * i, 1) for i in (1, 2)], axis=0
+        )
+        for m in messages
+    ]
+    assert tails[0].shape == (3 * third, HD)
+    result = [heads[0]]
+    for k in range(1, 5):
+        tile = jnp.where(lane >= 32 * (k - 1), tails[k - 1], heads[k - 1])
+        result.append(jnp.where(lane >= 32 * k, heads[k], tile) if k < 4 else tile)
+    return result
+
+
+def messages_of(product):
+    third = QUARTER // 3
+    lane = lanes((QUARTER, HD))
+    slot = lanes((third, HD)) >> 5
+    tiles = [product[:, k * HD : (k + 1) * HD] for k in range(5)]
+    result = []
+    for j in range(4):
+        head = jnp.where(lane >= 32 * j, tiles[j], tiles[j + 1]) if j else tiles[0]
+        extra = jnp.zeros((third, HD), F32)
+        for i in range(3):
+            piece = tiles[j + 1][i * third : (i + 1) * third]
+            piece = pltpu.roll(piece, 32 * i, 1) if i else piece
+            extra = jnp.where(slot == (i + j) % 4, piece, extra)
+        result.append(jnp.concatenate([head, extra], axis=0).astype(BF16))
+    return result
+
+
 def ffn_kernel(
-    in_ref, gain_ref, gate_hbm, down_hbm, out_ref, rows, normed, gates, down, sems
+    in_ref, gain_ref, gate_hbm, down_hbm, out_ref, rows, normed, gates, down, hidden, sems
 ):
     copies = []
     for c in range(D // FCHUNK):
@@ -449,35 +511,38 @@
     copies.append(pltpu.make_async_copy(down_hbm, down, sems.at[D // FCHUNK]))
     for copy in copies:
         copy.start()
-    for s in range(in_ref.shape[0]):
-        rows[:, s * COLS : (s + 1) * COLS] = unpacked(in_ref[s].astype(F32))
+    for s in range(0, in_ref.shape[0], 4):
+        tiles = tiles_of([in_ref[s + j].astype(F32) for j in range(4)])
+        for k, tile in enumerate(tiles):
+            at = s * COLS + k * HD
+            rows[:, at : at + HD] = tile
     full = rows[...]
     inverse = lax.rsqrt(jnp.sum(full * full, axis=1, keepdims=True) / D + EPS)
     normed[...] = (full * inverse * gain_ref[...]).astype(BF16)
-    hidden_units = down.shape[0]
-    gate = jnp.zeros((QUARTER, hidden_units), F32)
-    up = jnp.zeros((QUARTER, hidden_units), F32)
+    gate = jnp.zeros((QUARTER, down.shape[0]), F32)
+    up = jnp.zeros((QUARTER, down.shape[0]), F32)
     for c in range(D // FCHUNK):
         copies[c].wait()
         part = pl.ds(c * FCHUNK, FCHUNK)
         block = normed[:, part]
         gate = gate + turned_dot(block, gates[0, :, part])
         up = up + turned_dot(block, gates[1, :, part])
-    hidden = (gate / (1.0 + jnp.exp(-gate)) * up).astype(BF16)
+    hidden[...] = (gate / (1.0 + jnp.exp(-gate)) * up).astype(BF16)
     copies[-1].wait()
     wide = 4 * COLS
     for s in range(in_ref.shape[0] // 4):
         product = jnp.dot(
-            hidden, down[:, s * wide : (s + 1) * wide], preferred_element_type=F32
+            hidden[...], down[:, s * wide : (s + 1) * wide], preferred_element_type=F32
         )
-        for j in range(4):
-            out_ref[4 * s + j] = packed(product[:, j * COLS : (j + 1) * COLS])
-
-
-def finish_kernel(in_ref, own_ref, out_ref):
+        for j, message in enumerate(messages_of(product)):
+            out_ref[4 * s + j] = message
+
+
+def finish_kernel(f_ref, in_ref, own_ref, out_ref):
     total = in_ref[0].astype(F32)
     for s in range(1, in_ref.shape[0]):
         total = total + in_ref[s].astype(F32)
+    total = turned_lanes(total, lax.rem(4 - lax.rem(f_ref[0], 4), 4))
     out_ref[...] = (own_ref[...].astype(F32) + unpacked(total)).astype(BF16)
 
 
@@ -522,6 +587,49 @@
     angles = positions.astype(F32)[:, None] * frequency[None, :]
     sine = jnp.sin(angles) * jnp.where(lane < half_width, -1.0, 1.0)[None, :]
     return jnp.cos(angles), sine
+
+
+def run_attention(
+    lists, lefts, tokens, f1, fresh, own_block, key_cache, value_cache, grp, ffn
+):
+    pages = key_cache.shape[0]
+    units = PRE * GH
+    return call(
+        attention_kernel,
+        shape(grp * ffn, 16, HD),
+        [smem] * 4 + [vmem] * 2 + [hbm] * 2,
+        [
+            pltpu.VMEM((pages, PAGE, GH * HD), BF16),
+            pltpu.VMEM((pages, PAGE, GH * HD), BF16),
+            pltpu.SemaphoreType.DMA((2, CHUNKS)),
+            pltpu.VMEM((pages // 2 + 1, GH, SPAN, 2 * PAGE), F32),
+            pltpu.VMEM((units, SPAN, PAGE), F32),
+            pltpu.VMEM((units, SPAN, 2 * HD), F32),
+            pltpu.VMEM((GH, DEC, HD), F32),
+            pltpu.VMEM((DEC, 8, HD), F32),
+            pltpu.VMEM((DEC, 8, HD), F32),
+            pltpu.VMEM((DEC, 8, GH * HD), F32),
+            pltpu.VMEM((GH, TOKENS + 16, HD), F32),
+            pltpu.VMEM((GH, TOKENS + 16, HD), F32),
+        ],
+    )(lists, lefts, tokens, f1, fresh, own_block, key_cache, value_cache)
+
+
+def run_ffn(rows, gain, gate_up, down):
+    hidden_units = down.shape[0]
+    return call(
+        ffn_kernel,
+        shape(rows.shape[0], MSG, HD),
+        [vmem] * 2 + [hbm] * 2,
+        [
+            pltpu.VMEM((QUARTER, D), F32),
+            pltpu.VMEM((QUARTER, D), BF16),
+            pltpu.VMEM((2, hidden_units, D), BF16),
+            pltpu.VMEM((hidden_units, D), BF16),
+            pltpu.VMEM((QUARTER, hidden_units), BF16),
+            pltpu.SemaphoreType.DMA((D // FCHUNK + 1,)),
+        ],
+    )(rows, gain, gate_up, down)
 
 
 def shards(
@@ -545,17 +653,8 @@
     f1 = f.astype(jnp.int32).reshape(1)
     g1 = g.astype(jnp.int32).reshape(1)
     pages = key_cache.shape[0]
-    hidden_units = down_weight.shape[0]
 
     cosine, sine = tables(f, span_offsets, decode_lengths)
-    local_ids = f * pages + jnp.arange(pages, dtype=jnp.int32)
-    requests = PRE + DEC
-    numbers = jnp.arange(requests * MAXP, dtype=jnp.int32).reshape(requests, MAXP) + 1
-    codes = jnp.sum(
-        jnp.where(page_table[None] == local_ids[:, None, None], numbers[None], 0), axis=(1, 2)
-    )
-    prefixes = jnp.concatenate([span_offsets, decode_lengths])
-
     partial = call(
         project_kernel,
         shape(ffn, 3 * ROWS + STATS, HD),
@@ -567,7 +666,33 @@
             pltpu.SemaphoreType.DMA((5,)),
         ],
     )(layer_input.T, norm_gain.reshape(1, -1), qkv_weight)
-    turned_weight, partial = lax.optimization_barrier((out_weight.T, partial))
+    page_table, partial = lax.optimization_barrier((page_table, partial))
+    local_ids = f * pages + jnp.arange(pages, dtype=jnp.int32)
+    requests = PRE + DEC
+    numbers = jnp.arange(requests * MAXP, dtype=jnp.int32).reshape(requests, MAXP) + 1
+    codes = jnp.sum(
+        jnp.where(page_table[None] == local_ids[:, None, None], numbers[None], 0), axis=(1, 2)
+    )
+    prefixes = jnp.concatenate([span_offsets, decode_lengths])
+    owners = (codes - 1) >> 7
+    lefts = jnp.sum(
+        jnp.where(owners[:, None] == jnp.arange(requests)[None], prefixes[None], 0), axis=1
+    )
+    lefts = jnp.clip(lefts - ((codes - 1) & 127) * PAGE, 0, PAGE)
+    kinds = jnp.where((codes > 0) & (lefts > 0), jnp.minimum(owners, PRE), PRE + 1)
+    order = jnp.arange(pages, dtype=jnp.int32)
+    same = kinds[:, None] == kinds[None, :]
+    rank = jnp.sum(jnp.where(same & (order[None, :] < order[:, None]), 1, 0), axis=1)
+    of_kind = kinds[None, :] == jnp.arange(PRE + 1, dtype=jnp.int32)[:, None]
+    place = jnp.where(of_kind, rank[None, :], -1)
+    lists = jnp.sum(
+        jnp.where(place[:, None, :] == order[None, :, None], order[None, None, :], 0), axis=2
+    )
+    counts = jnp.sum(of_kind.astype(jnp.int32), axis=1, keepdims=True)
+    lists = jnp.concatenate([lists, counts], axis=1)
+    tokens = jnp.clip(owners - PRE, 0, DEC - 1)
+
+    turned_weight, lists = lax.optimization_barrier((out_weight.T, lists))
     out_weights = [turned_weight] + [
         lax.ppermute(turned_weight, "grp", [(i, (i + s) % grp) for i in range(grp)])
         for s in range(1, grp)
@@ -580,57 +705,30 @@
         out_specs=(vmem, vmem),
     )(partial, cosine, sine)
     fresh = swap(fresh, "ffn").reshape(ffn * ROWS, HD)
-    units = PRE * GH
-    message = call(
-        attention_kernel,
-        shape(grp * ffn, 16, HD),
-        [smem] * 3 + [vmem] * 2 + [hbm] * 2,
-        [
-            pltpu.VMEM((pages, PAGE, GH * HD), BF16),
-            pltpu.VMEM((pages, PAGE, GH * HD), BF16),
-            pltpu.SemaphoreType.DMA((2, CHUNKS)),
-            pltpu.SMEM((2, pages), jnp.int32),
-            pltpu.VMEM((pages, GH, SPAN, PAGE), F32),
-            pltpu.VMEM((units, SPAN, PAGE), F32),
-            pltpu.VMEM((units, SPAN, 2 * HD), F32),
-            pltpu.VMEM((GH, DEC, HD), F32),
-            pltpu.VMEM((DEC, 8, HD), F32),
-            pltpu.VMEM((DEC, 8, HD), F32),
-            pltpu.VMEM((DEC, 8, GH * HD), F32),
-            pltpu.VMEM((GH, TOKENS + 16, HD), F32),
-            pltpu.VMEM((GH, TOKENS + 16, HD), F32),
-        ],
-    )(codes, prefixes, f1, fresh, own_block, key_cache, value_cache)
+    message = run_attention(
+        lists, lefts, tokens, f1, fresh, own_block, key_cache, value_cache, grp, ffn
+    )
     message = swap(message, ("grp", "ffn"))
     heads = call(merge_kernel, shape(ffn, ROWS, HD), [vmem])(message)
     heads = swap(heads, "ffn")
     own, rows = call(
         output_kernel,
         (shape(QUARTER, COLS), shape(ffn, MSG, HD)),
-        [smem] + [vmem] * (2 + grp),
+        [smem] * 2 + [vmem] * (2 + grp),
         [
             pltpu.VMEM((GH * (QUARTER // FEW), ROWS + 16, HD), F32),
             pltpu.VMEM((grp, 16 * (QUARTER // FEW), GH * HD), BF16),
             pltpu.VMEM((QUARTER, COLS), F32),
         ],
         out_specs=(vmem, vmem),
-    )(g1, heads, layer_input, *out_weights)
+    )(g1, f1, heads, layer_input, *out_weights)
     rows = swap(rows, "ffn")
 
-    down_terms = call(
-        ffn_kernel,
-        shape(ffn, MSG, HD),
-        [vmem] * 2 + [hbm] * 2,
-        [
-            pltpu.VMEM((QUARTER, D), F32),
-            pltpu.VMEM((QUARTER, D), BF16),
-            pltpu.VMEM((2, hidden_units, D), BF16),
-            pltpu.VMEM((hidden_units, D), BF16),
-            pltpu.SemaphoreType.DMA((D // FCHUNK + 1,)),
-        ],
-    )(rows, ffn_gain.reshape(1, -1), jnp.swapaxes(gate_up_weight, 1, 2), down_weight)
+    down_terms = run_ffn(
+        rows, ffn_gain.reshape(1, -1), jnp.swapaxes(gate_up_weight, 1, 2), down_weight
+    )
     down_terms = swap(down_terms, "ffn")
-    return call(finish_kernel, shape(QUARTER, COLS), [vmem] * 2)(down_terms, own)
+    return call(finish_kernel, shape(QUARTER, COLS), [smem] + [vmem] * 2)(f1, down_terms, own)
 
 
 def solution(mesh):

time: 141 us -> 135 us (0.957)
  blocking collectives: 54 us -> 69.4 us
  waiting for transfers between devices: 32.6 us -> 21.4 us
  Pallas kernels: 28.1 us -> 20.8 us
  starting transfers between devices: 23.1 us -> 19.2 us
    all_to_all x3 -> x4, blocking collectives: 54 us -> 69.4 us  [swap(): return lax.all_to_all(value, axis, 0, 0)]
    all_to_all x3 -> x2, waiting for transfers between devices: 25.8 us -> 13.2 us  [swap(): return lax.all_to_all(value, axis, 0, 0)]
    pallas_call x7, Pallas kernels: 28.1 us -> 20.8 us  [placed(): function(*[pltpu.with_memory_space_constraint(a, pltpu.HBM) if spec is hb...]
    all_to_all x3 -> x2, starting transfers between devices: 18.1 us -> 14.2 us  [swap(): return lax.all_to_all(value, axis, 0, 0)]
  transfers between devices with their start and end apart: 6 -> 5, of which waited for: 5 -> 4; matrix products, arithmetic and copies ran while one was open for 1% -> 2% of each run, Pallas kernels for 0% -> 0%
where the time goes in v2:
time: 135 us; the launch traced here: 134 us
  blocking collectives  69.4 us (51%)
  waiting for transfers between devices  21.4 us (16%)
  Pallas kernels  20.8 us (15%)
  starting transfers between devices  19.2 us (14%)
  other arithmetic  2.81 us (2%)
    all_to_all x4, blocking collectives, swap(): return lax.all_to_all(value, axis, 0, 0)  69.4 us
    pallas_call x7, Pallas kernels, placed(): function(*[pltpu.with_memory_space_constraint(a, pltpu.HBM) if spec is hb...  20.8 us
    all_to_all x2, starting transfers between devices, swap(): return lax.all_to_all(value, axis, 0, 0)  14.2 us
    all_to_all x2, waiting for transfers between devices, swap(): return lax.all_to_all(value, axis, 0, 0)  13.2 us
    ppermute x3, waiting for transfers between devices, shards(): lax.ppermute(turned_weight, 'grp', [(i, (i + s) % grp) for i in range(grp)])  8.16 us
    ppermute x3, starting transfers between devices, shards(): lax.ppermute(turned_weight, 'grp', [(i, (i + s) % grp) for i in range(grp)])  4.99 us
  transfers between devices with their start and end apart: 5, of which 4 were waited for; matrix products, arithmetic and copies ran while one was open for 2% of the time, Pallas kernels for 0%

profile of v2, /device:TPU:1, one launch (start us, length us, event | category | flops | bytes accessed | tf_op | source)
XLA Modules:
  0.0 133.9 jit_solution(132283054908255582)
XLA Ops:
  0.0 3.2 %shard_map.118 = bf16[32,152,128]{2,1,0:T(8,128)(2,1)} custom-call(bf16[160,288]{1,0:T(8,128)(2,1)} %bitcast.18, f32[1,160]{1,0:T(1,128)} %bitcast.20, bf16[3,160,640]{2,1,0:T(8,128)(2,1)} %w_hbm.1), custom_call_target="tpu_custom_call" | custom-call | tf_op jit(solution)/shard_map/pallas_call | solution.py:560
  3.2 9.4 %all-to-all-start = ((bf16[32,152,128]{2,1,0:T(8,128)(2,1)}), bf16[32,152,128]{2,1,0:T(8,128)(2,1)S(1)}, u32[]{:S(2)}, u32[]{:S(2)}) async-start(bf16[32,152,128]{2,1,0:T(8,128)(2,1)} %shard_map.118), calls=%async_computation | async-start | bytes 2490368 | tf_op jit(solution)/shard_map/all_to_all | solution.py:575
  12.6 1.0 select_reduce_fusion
  13.6 0.8 pad_add_fusion.2
  14.4 0.2 select_reduce_fusion.3
  14.6 0.2 select_reduce_fusion.2
  15.2 1.3 collective-permute-start
  16.5 2.6 %collective-permute-start.1 = (bf16[160,640]{1,0:T(8,128)(2,1)}, bf16[160,640]{1,0:T(8,128)(2,1)S(1)}, u32[]{:S(2)}, u32[]{:S(2)}) collective-permute-start(bf16[160,640]{1,0:T(8,128)(2,1)} %bitcast.13), channel_id=1, source_target_pairs={{0,64},{32,96},{64,0},{96,32},{1,65},{33,97},{65,1},{97,33},{2,66}... | collective-permute-start | bytes 614408 | tf_op jit(solution)/shard_map/ppermute | solution.py:697
  19.1 1.1 collective-permute-start.2
  20.6 2.7 %collective-permute-done.refs_1_ = bf16[160,640]{1,0:T(8,128)(2,1)S(1)} collective-permute-done((bf16[160,640]{1,0:T(8,128)(2,1)}, bf16[160,640]{1,0:T(8,128)(2,1)S(1)}, u32[]{:S(2)}, u32[]{:S(2)}) %collective-permute-start) | collective-permute-done | bytes 204832 | tf_op jit(solution)/shard_map/ppermute | solution.py:697
  23.2 5.5 %collective-permute-done.1.refs_2_ = bf16[160,640]{1,0:T(8,128)(2,1)S(1)} collective-permute-done((bf16[160,640]{1,0:T(8,128)(2,1)}, bf16[160,640]{1,0:T(8,128)(2,1)S(1)}, u32[]{:S(2)}, u32[]{:S(2)}) %collective-permute-start.1) | collective-permute-done | bytes 204832 | tf_op jit(solution)/shard_map/ppermute | solution.py:697
  28.7 3.0 %all-to-all-done.in_ref = bf16[32,152,128]{2,1,0:T(8,128)(2,1)S(1)} async-done(((bf16[32,152,128]{2,1,0:T(8,128)(2,1)}), bf16[32,152,128]{2,1,0:T(8,128)(2,1)S(1)}, u32[]{:S(2)}, u32[]{:S(2)}) %all-to-all-start) | async-done | bytes 1245216 | tf_op jit(solution)/shard_map/all_to_all | solution.py:575
  31.7 0.3 shard_map.119
  32.0 15.2 %all_to_all.30 = bf16[32,48,128]{2,1,0:T(8,128)(2,1)S(1)} all-to-all(bf16[32,48,128]{2,1,0:T(8,128)(2,1)S(1)} %get-tuple-element.23), channel_id=1, replica_groups=mesh['grp'=4,'ffn'=32] {'ffn'}, dimensions={0} | all-to-all | bytes 786432 | tf_op jit(solution)/shard_map/all_to_all | solution.py:575
  47.2 8.3 %shard_map.120 = bf16[128,16,128]{2,1,0:T(8,128)(2,1)S(1)} custom-call(s32[3,29]{1,0:T(4,128)S(1)} %pad_add_fusion.lists, s32[28]{0:T(128)S(1)} %get-tuple-element.33.left_ref, s32[28]{0:T(128)S(1)} %get-tuple-element.35.token_ref, s32[1]{0:T(128)} %bitcast.f_ref, bf16[1536,128]{1,0:T(8,128)(2,1)S(1)} %bitcast.11, ...), custom_call_target="tpu_custom_call" | custom-call | tf_op jit(solution)/shard_map/pallas_call | solution.py:560
  55.5 18.8 %all_to_all.31.in_ref = bf16[128,16,128]{2,1,0:T(8,128)(2,1)S(1)} all-to-all(bf16[128,16,128]{2,1,0:T(8,128)(2,1)S(1)} %shard_map.120), channel_id=1, replica_groups=mesh['grp'=4,'ffn'=32] {'grp','ffn'}, dimensions={0} | all-to-all | bytes 1048576 | tf_op jit(solution)/shard_map/all_to_all | solution.py:575
  74.3 1.5 %shard_map.121 = bf16[32,48,128]{2,1,0:T(8,128)(2,1)} custom-call(bf16[128,16,128]{2,1,0:T(8,128)(2,1)S(1)} %all_to_all.31.in_ref), custom_call_target="tpu_custom_call" | custom-call | tf_op jit(solution)/shard_map/pallas_call | solution.py:560
  75.8 4.7 %all-to-all-start.3 = ((bf16[32,48,128]{2,1,0:T(8,128)(2,1)}), bf16[32,48,128]{2,1,0:T(8,128)(2,1)S(1)}, u32[]{:S(2)}, u32[]{:S(2)}) async-start(bf16[32,48,128]{2,1,0:T(8,128)(2,1)} %shard_map.121), calls=%async_computation.3 | async-start | bytes 786432 | tf_op jit(solution)/shard_map/all_to_all | solution.py:575
  80.7 10.3 %all-to-all-done.3.in_ref = bf16[32,48,128]{2,1,0:T(8,128)(2,1)S(1)} async-done(((bf16[32,48,128]{2,1,0:T(8,128)(2,1)}), bf16[32,48,128]{2,1,0:T(8,128)(2,1)S(1)}, u32[]{:S(2)}, u32[]{:S(2)}) %all-to-all-start.3) | async-done | bytes 393248 | tf_op jit(solution)/shard_map/all_to_all | solution.py:575
  91.0 0.7 shard_map.122
  91.7 17.5 %all_to_all.32.in_ref = bf16[32,96,128]{2,1,0:T(8,128)(2,1)S(1)} all-to-all(bf16[32,96,128]{2,1,0:T(8,128)(2,1)S(1)} %get-tuple-element.29), channel_id=1, replica_groups=mesh['grp'=4,'ffn'=32] {'ffn'}, dimensions={0} | all-to-all | bytes 1572864 | tf_op jit(solution)/shard_map/all_to_all | solution.py:575
  109.2 6.0 %shard_map.123 = bf16[32,96,128]{2,1,0:T(8,128)(2,1)S(1)} custom-call(bf16[32,96,128]{2,1,0:T(8,128)(2,1)S(1)} %all_to_all.32.in_ref, f32[1,5120]{1,0:T(1,128)S(1)} %bitcast.16, bf16[2,432,5120]{2,1,0:T(8,128)(2,1)} %bitcast.17, bf16[432,5120]{1,0:T(8,128)(2,1)} %down_hbm.1), custom_call_target="tpu_custom_call" | custom-call | tf_op jit(solution)/shard_map/pallas_call | solution.py:560
  115.2 17.9 %all_to_all.33.in_ref = bf16[32,96,128]{2,1,0:T(8,128)(2,1)S(1)} all-to-all(bf16[32,96,128]{2,1,0:T(8,128)(2,1)S(1)} %shard_map.123), channel_id=1, replica_groups=mesh['grp'=4,'ffn'=32] {'ffn'}, dimensions={0} | all-to-all | bytes 1572864 | tf_op jit(solution)/shard_map/all_to_all | solution.py:575
  133.1 0.8 shard_map.124
  (25 shorter events, 1.0 us)
Async XLA Ops:
  0.0 20.3 %copy-start.3 = (s32[32]{0:T(128)S(1)}, s32[32]{0:T(128)}, u32[]{:S(2)}) copy-start(s32[32]{0:T(128)} %param.22) | copy-start | bytes 388
  0.0 20.2 %copy-start.4 = (s32[2]{0:T(128)S(1)}, s32[2]{0:T(128)}, u32[]{:S(2)}) copy-start(s32[2]{0:T(128)} %param.21) | copy-start | bytes 28
  3.2 28.5 %all-to-all-start = ((bf16[32,152,128]{2,1,0:T(8,128)(2,1)}), bf16[32,152,128]{2,1,0:T(8,128)(2,1)S(1)}, u32[]{:S(2)}, u32[]{:S(2)}) async-start(bf16[32,152,128]{2,1,0:T(8,128)(2,1)} %shard_map.118), calls=%async_computation | async-start | bytes 2490368 | tf_op jit(solution)/shard_map/all_to_all | solution.py:575
  15.2 8.0 %collective-permute-start = (bf16[160,640]{1,0:T(8,128)(2,1)}, bf16[160,640]{1,0:T(8,128)(2,1)S(1)}, u32[]{:S(2)}, u32[]{:S(2)}) collective-permute-start(bf16[160,640]{1,0:T(8,128)(2,1)} %bitcast.12), channel_id=1, source_target_pairs={{0,32},{32,64},{64,96},{96,0},{1,33},{33,65},{65,97},{97,1},{2,34}... | collective-permute-start | bytes 614408 | tf_op jit(solution)/shard_map/ppermute | solution.py:697
  16.5 12.2 %collective-permute-start.1 = (bf16[160,640]{1,0:T(8,128)(2,1)}, bf16[160,640]{1,0:T(8,128)(2,1)S(1)}, u32[]{:S(2)}, u32[]{:S(2)}) collective-permute-start(bf16[160,640]{1,0:T(8,128)(2,1)} %bitcast.13), channel_id=1, source_target_pairs={{0,64},{32,96},{64,0},{96,32},{1,65},{33,97},{65,1},{97,33},{2,66}... | collective-permute-start | bytes 614408 | tf_op jit(solution)/shard_map/ppermute | solution.py:697
  19.1 9.6 %collective-permute-start.2 = (bf16[160,640]{1,0:T(8,128)(2,1)}, bf16[160,640]{1,0:T(8,128)(2,1)S(1)}, u32[]{:S(2)}, u32[]{:S(2)}) collective-permute-start(bf16[160,640]{1,0:T(8,128)(2,1)} %bitcast.14), channel_id=1, source_target_pairs={{0,96},{32,0},{64,32},{96,64},{1,97},{33,1},{65,33},{97,65},{2,98}... | collective-permute-start | bytes 614408 | tf_op jit(solution)/shard_map/ppermute | solution.py:697
  47.2 33.4 %copy-start.2 = (bf16[288,160]{0,1:T(8,128)(2,1)S(1)}, bf16[288,160]{0,1:T(8,128)(2,1)}, u32[]{:S(2)}) copy-start(bf16[288,160]{0,1:T(8,128)(2,1)} %param.12) | copy-start | bytes 276484
  47.2 43.8 %copy-start = (bf16[640,160]{0,1:T(8,128)(2,1)S(1)}, bf16[640,160]{0,1:T(8,128)(2,1)}, u32[]{:S(2)}) copy-start(bf16[640,160]{0,1:T(8,128)(2,1)} %param.17) | copy-start | bytes 614404
  55.5 53.7 %copy-start.1 = (f32[5120]{0:T(1024)S(1)}, f32[5120]{0:T(1024)}, u32[]{:S(2)}) copy-start(f32[5120]{0:T(1024)} %param.18) | copy-start | bytes 61444
  75.8 15.2 %all-to-all-start.3 = ((bf16[32,48,128]{2,1,0:T(8,128)(2,1)}), bf16[32,48,128]{2,1,0:T(8,128)(2,1)S(1)}, u32[]{:S(2)}, u32[]{:S(2)}) async-start(bf16[32,48,128]{2,1,0:T(8,128)(2,1)} %shard_map.121), calls=%async_computation.3 | async-start | bytes 786432 | tf_op jit(solution)/shard_map/all_to_all | solution.py:575

commit v3 on v2

--- a/solution.py
+++ b/solution.py
@@ -33,6 +33,7 @@
 GROUP = 4
 CHUNKS = 4
 FCHUNK = 640
+AHEAD = 3
 
 vmem = pl.BlockSpec(memory_space=pltpu.VMEM)
 smem = pl.BlockSpec(memory_space=pltpu.SMEM)
@@ -58,7 +59,17 @@
     return high, middle, rest - middle
 
 
-def project_kernel(x_hbm, gain_hbm, w_hbm, out_ref, x_vmem, gain_ref, w_vmem, sems):
+def stat_block(stat):
+    row = rows_of((STATS, HD))
+    high, middle, low = split3(stat)
+    return jnp.where(
+        row == 0, high, jnp.where(row == 1, middle, jnp.where(row == 2, low, 0.0))
+    ).astype(BF16)
+
+
+def project_kernel(
+    p_ref, x_hbm, gain_hbm, w_hbm, out_ref, x_vmem, gain_ref, w_vmem, x_rows, sems
+):
     copies = [pltpu.make_async_copy(x_hbm, x_vmem, sems.at[3])]
     gain_copy = pltpu.make_async_copy(gain_hbm, gain_ref, sems.at[4])
     gain_copy.start()
@@ -68,31 +79,42 @@
         copy.start()
     copies[0].wait()
     gain_copy.wait()
-    x = jnp.transpose(x_vmem[...].astype(F32))
+    x_rows[...] = jnp.transpose(x_vmem[...].astype(F32))
+    half = TOKENS // ROWS // 2
+    x = jnp.concatenate(
+        [
+            x_rows[pl.ds(pl.multiple_of((2 * i + p_ref[0]) * ROWS, 16), ROWS), :]
+            for i in range(half)
+        ],
+        axis=0,
+    )
     scaled = (x * gain_ref[...]).astype(BF16)
     squares = jnp.sum(x * x, axis=1, keepdims=True)
-    blocks = TOKENS // ROWS
     diagonal = rows_of((ROWS, HD)) == lanes((ROWS, HD))
-    row = rows_of((STATS, HD))
-    for b in range(blocks):
-        part = jnp.broadcast_to(squares[b * ROWS : (b + 1) * ROWS], (ROWS, HD))
+    for i in range(half):
+        part = jnp.broadcast_to(squares[i * ROWS : (i + 1) * ROWS], (ROWS, HD))
         stat = jnp.sum(jnp.where(diagonal, part, 0.0), axis=0, keepdims=True)
-        high, middle, low = split3(stat)
-        block = jnp.where(
-            row == 0, high, jnp.where(row == 1, middle, jnp.where(row == 2, low, 0.0))
-        ).astype(BF16)
+        block = stat_block(stat)
         for h in range(GH):
-            out_ref[h * blocks + b, 3 * ROWS :, :] = block
+            out_ref[h * half + i, 3 * ROWS :, :] = block
     for k in range(3):
         copies[1 + k].wait()
         product = jnp.dot(scaled, w_vmem[k], preferred_element_type=F32).astype(BF16)
         for h in range(GH):
-            for b in range(blocks):
-                out_ref[h * blocks + b, k * ROWS : (k + 1) * ROWS, :] = product[
-                    b * ROWS : (b + 1) * ROWS, h * HD : (h + 1) * HD
+            for i in range(half):
+                out_ref[h * half + i, k * ROWS : (k + 1) * ROWS, :] = product[
+                    i * ROWS : (i + 1) * ROWS, h * HD : (h + 1) * HD
                 ]
-    for target in range(GH * blocks, out_ref.shape[0]):
+    for target in range(GH * half, out_ref.shape[0]):
         out_ref[target] = jnp.zeros(out_ref.shape[1:], BF16)
+
+
+def add_kernel(left_ref, right_ref, out_ref):
+    for i in range(out_ref.shape[0]):
+        total = left_ref[i].astype(F32) + right_ref[i].astype(F32)
+        stat = jnp.sum(total[3 * ROWS :], axis=0, keepdims=True)
+        out_ref[i, : 3 * ROWS, :] = total[: 3 * ROWS].astype(BF16)
+        out_ref[i, 3 * ROWS :, :] = stat_block(stat)
 
 
 def rotate_kernel(in_ref, cos_ref, sin_ref, out_ref, own_ref):
@@ -166,6 +188,7 @@
 
     n_pre = [lists[k, pages] for k in range(PRE)]
     n_dec = lists[PRE, pages]
+    pairs = [lists[k, pages + 1 + CHUNKS] for k in range(PRE)]
 
     f = f_ref[0]
     blocks = TOKENS // ROWS
@@ -198,9 +221,6 @@
             unit = request * GH + own_head
             peak[unit] = jnp.maximum(peak[unit], own_scores(request)[0])
 
-    for copy in copies[:CHUNKS]:
-        copy.wait()
-
     def pair(request, i):
         last = n_pre[request] - 1
         first_page = lists[request, 2 * i]
@@ -211,10 +231,21 @@
         return jnp.concatenate([ref[p, :, h * HD : (h + 1) * HD] for p in pages_of], axis=0)
 
     wide_lane = lanes((SPAN, 2 * PAGE))
-    pairs = [(n + 1) >> 1 for n in n_pre]
-    for request in range(PRE):
-
-        def first_pass(i, _, request=request):
+    def in_chunks(which, one_pass):
+        def chunk(c, _):
+            part = pl.ds(c * step, step)
+            source, target = ((key_hbm, keys), (value_hbm, values))[which]
+            pltpu.make_async_copy(source.at[part], target.at[part], sems.at[which, c]).wait()
+            for request in range(PRE):
+                lower = lists[request, pages + 1 + c]
+                upper = lists[request, pages + 2 + c]
+                lax.fori_loop(lower, upper, one_pass(request), 0)
+            return 0
+
+        lax.fori_loop(0, CHUNKS, chunk, 0)
+
+    def first_pass(request):
+        def one_pair(i, _):
             both = pair(request, i)
             left = left_ref[both[0]]
             other = jnp.where(2 * i + 1 < n_pre[request], left_ref[both[1]], 0) + PAGE
@@ -229,24 +260,22 @@
                 )
             return 0
 
-        lax.fori_loop(0, pairs[request], first_pass, 0)
+        return one_pair
+
+    in_chunks(0, first_pass)
 
     for unit in range(PRE * GH):
         peak[unit] = jnp.broadcast_to(
             jnp.max(peak[unit], axis=1, keepdims=True), (SPAN, SPAN)
         )
 
-    for copy in copies[CHUNKS:]:
-        copy.wait()
-
     def weigh(unit, weights, value):
         ones = jnp.ones((value.shape[0], HD), BF16)
         both = jnp.concatenate([value, ones], axis=1)
         summed[unit] += jnp.dot(weights.astype(BF16), both, preferred_element_type=F32)
 
-    for request in range(PRE):
-
-        def second_pass(i, _, request=request):
+    def second_pass(request):
+        def one_pair(i, _):
             both = pair(request, i)
             for h in range(GH):
                 unit = request * GH + h
@@ -256,7 +285,9 @@
                 weigh(unit, weights, joined(values, both, h))
             return 0
 
-        lax.fori_loop(0, pairs[request], second_pass, 0)
+        return one_pair
+
+    in_chunks(1, second_pass)
 
     @pl.when(has_own)
     def _():
@@ -499,11 +530,10 @@
     return result
 
 
-def ffn_kernel(
-    in_ref, gain_ref, gate_hbm, down_hbm, out_ref, rows, normed, gates, down, hidden, sems
-):
+def ffn_kernel(f_ref, mine_ref, theirs_ref, gain_ref, gate_hbm, down_hbm, *refs):
+    ahead, (out_ref, rows, normed, gates, down, hidden, sems) = refs[:AHEAD], refs[AHEAD:]
     copies = []
-    for c in range(D // FCHUNK):
+    for c in range(AHEAD, D // FCHUNK):
         part = pl.ds(c * FCHUNK, FCHUNK)
         copies.append(
             pltpu.make_async_copy(gate_hbm.at[:, :, part], gates.at[:, :, part], sems.at[c])
@@ -511,9 +541,17 @@
     copies.append(pltpu.make_async_copy(down_hbm, down, sems.at[D // FCHUNK]))
     for copy in copies:
         copy.start()
-    for s in range(0, in_ref.shape[0], 4):
-        tiles = tiles_of([in_ref[s + j].astype(F32) for j in range(4)])
-        for k, tile in enumerate(tiles):
+    odd = lax.rem(f_ref[0], 2) == 1
+    for s in range(0, 2 * mine_ref.shape[0], 4):
+        messages = []
+        for j in range(4):
+            place = (s + j) // 2
+            mine = mine_ref[place].astype(F32)
+            theirs = theirs_ref[place].astype(F32)
+            messages.append(
+                jnp.where(odd, mine, theirs) if j % 2 else jnp.where(odd, theirs, mine)
+            )
+        for k, tile in enumerate(tiles_of(messages)):
             at = s * COLS + k * HD
             rows[:, at : at + HD] = tile
     full = rows[...]
@@ -522,15 +560,19 @@
     gate = jnp.zeros((QUARTER, down.shape[0]), F32)
     up = jnp.zeros((QUARTER, down.shape[0]), F32)
     for c in range(D // FCHUNK):
-        copies[c].wait()
         part = pl.ds(c * FCHUNK, FCHUNK)
         block = normed[:, part]
-        gate = gate + turned_dot(block, gates[0, :, part])
-        up = up + turned_dot(block, gates[1, :, part])
+        if c < AHEAD:
+            both = ahead[c][0], ahead[c][1]
+        else:
+            copies[c - AHEAD].wait()
+            both = gates[0, :, part], gates[1, :, part]
+        gate = gate + turned_dot(block, both[0])
+        up = up + turned_dot(block, both[1])
     hidden[...] = (gate / (1.0 + jnp.exp(-gate)) * up).astype(BF16)
     copies[-1].wait()
     wide = 4 * COLS
-    for s in range(in_ref.shape[0] // 4):
+    for s in range(out_ref.shape[0] // 4):
         product = jnp.dot(
             hidden[...], down[:, s * wide : (s + 1) * wide], preferred_element_type=F32
         )
@@ -544,6 +586,29 @@
         total = total + in_ref[s].astype(F32)
     total = turned_lanes(total, lax.rem(4 - lax.rem(f_ref[0], 4), 4))
     out_ref[...] = (own_ref[...].astype(F32) + unpacked(total)).astype(BF16)
+
+
+def fetch_kernel(in_ref, *refs):
+    *targets, sems = refs
+    copies = [
+        pltpu.make_async_copy(in_ref.at[:, :, pl.ds(c * FCHUNK, FCHUNK)], target, sems.at[c])
+        for c, target in enumerate(targets)
+    ]
+    for copy in copies:
+        copy.start()
+    for copy in copies:
+        copy.wait()
+
+
+def fetched(gate_up):
+    out = tuple(shape(*gate_up.shape[:2], FCHUNK) for _ in range(AHEAD))
+    return call(
+        fetch_kernel,
+        out,
+        [hbm],
+        [pltpu.SemaphoreType.DMA((AHEAD,))],
+        out_specs=(vmem,) * AHEAD,
+    )(gate_up)
 
 
 def call(kernel, out, specs, scratch=(), out_specs=None):
@@ -615,12 +680,12 @@
     )(lists, lefts, tokens, f1, fresh, own_block, key_cache, value_cache)
 
 
-def run_ffn(rows, gain, gate_up, down):
+def run_ffn(f1, mine, theirs, gain, gate_up, down, ahead):
     hidden_units = down.shape[0]
     return call(
         ffn_kernel,
-        shape(rows.shape[0], MSG, HD),
-        [vmem] * 2 + [hbm] * 2,
+        shape(2 * mine.shape[0], MSG, HD),
+        [smem] + [vmem] * 3 + [hbm] * 2 + [vmem] * AHEAD,
         [
             pltpu.VMEM((QUARTER, D), F32),
             pltpu.VMEM((QUARTER, D), BF16),
@@ -629,7 +694,7 @@
             pltpu.VMEM((QUARTER, hidden_units), BF16),
             pltpu.SemaphoreType.DMA((D // FCHUNK + 1,)),
         ],
-    )(rows, gain, gate_up, down)
+    )(f1, mine, theirs, gain, gate_up, down, *ahead)
 
 
 def shards(
@@ -654,19 +719,30 @@
     g1 = g.astype(jnp.int32).reshape(1)
     pages = key_cache.shape[0]
 
-    cosine, sine = tables(f, span_offsets, decode_lengths)
-    partial = call(
-        project_kernel,
-        shape(ffn, 3 * ROWS + STATS, HD),
-        [hbm, hbm, hbm],
-        [
-            pltpu.VMEM((COLS, TOKENS), BF16),
-            pltpu.VMEM((1, COLS), F32),
-            pltpu.VMEM(qkv_weight.shape, BF16),
-            pltpu.SemaphoreType.DMA((5,)),
-        ],
-    )(layer_input.T, norm_gain.reshape(1, -1), qkv_weight)
-    page_table, partial = lax.optimization_barrier((page_table, partial))
+    parity = [[2 * i + c for i in range(ffn // 2)] for c in range(2)]
+    neighbour = [(i, i ^ 1) for i in range(ffn)]
+
+    def projected(which):
+        return call(
+            project_kernel,
+            shape(ffn // 2, 3 * ROWS + STATS, HD),
+            [smem, hbm, hbm, hbm],
+            [
+                pltpu.VMEM((COLS, TOKENS), BF16),
+                pltpu.VMEM((1, COLS), F32),
+                pltpu.VMEM(qkv_weight.shape, BF16),
+                pltpu.VMEM((TOKENS, COLS), F32),
+                pltpu.SemaphoreType.DMA((5,)),
+            ],
+        )(which, layer_input.T, norm_gain.reshape(1, -1), qkv_weight)
+
+    core = lax.rem(f1, 2)
+    sent = projected(1 - core)
+    core, sent, page_table = lax.optimization_barrier((core, sent, page_table))
+    received = lax.ppermute(sent, "ffn", neighbour)
+    partial = call(add_kernel, shape(*sent.shape), [vmem] * 2)(projected(core), received)
+    span_rows, partial = lax.optimization_barrier((span_offsets, partial))
+    cosine, sine = tables(f, span_rows, decode_lengths)
     local_ids = f * pages + jnp.arange(pages, dtype=jnp.int32)
     requests = PRE + DEC
     numbers = jnp.arange(requests * MAXP, dtype=jnp.int32).reshape(requests, MAXP) + 1
@@ -688,32 +764,44 @@
     lists = jnp.sum(
         jnp.where(place[:, None, :] == order[None, :, None], order[None, None, :], 0), axis=2
     )
-    counts = jnp.sum(of_kind.astype(jnp.int32), axis=1, keepdims=True)
-    lists = jnp.concatenate([lists, counts], axis=1)
+    bound = jnp.arange(CHUNKS + 1, dtype=jnp.int32) * (pages // CHUNKS)
+    here = of_kind[:, None, :] & (order[None, None, :] < bound[None, :, None])
+    counts = jnp.sum(here.astype(jnp.int32), axis=2)
+    last = jnp.arange(CHUNKS + 1) == CHUNKS
+    lists = jnp.concatenate(
+        [lists, counts[:, CHUNKS:], (counts + last[None].astype(jnp.int32)) >> 1], axis=1
+    )
     tokens = jnp.clip(owners - PRE, 0, DEC - 1)
 
-    turned_weight, lists = lax.optimization_barrier((out_weight.T, lists))
-    out_weights = [turned_weight] + [
-        lax.ppermute(turned_weight, "grp", [(i, (i + s) % grp) for i in range(grp)])
-        for s in range(1, grp)
-    ]
-    partial, *out_weights = lax.optimization_barrier((swap(partial, "ffn"), *out_weights))
+    turned_weight, cosine = lax.optimization_barrier((out_weight.T, cosine))
+    def passed(weight, amount):
+        return lax.ppermute(weight, "grp", [(i, (i + amount) % grp) for i in range(grp)])
+
+    near = [passed(turned_weight, 1), passed(turned_weight, grp - 1)]
+    partial = lax.all_to_all(partial, "ffn", 0, 0, axis_index_groups=parity)
+    partial, *near = lax.optimization_barrier((partial, *near))
     fresh, own_block = call(
         rotate_kernel,
         (shape(ffn, ROWS, HD), shape(2, ROWS, HD)),
         [vmem] * 3,
         out_specs=(vmem, vmem),
     )(partial, cosine, sine)
+    middle = []
+    for _ in range(2, grp - 1):
+        last, own_block = lax.optimization_barrier((middle[-1] if middle else near[0], own_block))
+        middle.append(passed(last, 1))
     fresh = swap(fresh, "ffn").reshape(ffn * ROWS, HD)
+    fresh, *middle = lax.optimization_barrier((fresh, *middle))
     message = run_attention(
         lists, lefts, tokens, f1, fresh, own_block, key_cache, value_cache, grp, ffn
     )
     message = swap(message, ("grp", "ffn"))
     heads = call(merge_kernel, shape(ffn, ROWS, HD), [vmem])(message)
     heads = swap(heads, "ffn")
+    out_weights = [turned_weight, near[0], *middle, near[1]]
     own, rows = call(
         output_kernel,
-        (shape(QUARTER, COLS), shape(ffn, MSG, HD)),
+        (shape(QUARTER, COLS), shape(ffn // 2, MSG, HD)),
         [smem] * 2 + [vmem] * (2 + grp),
         [
             pltpu.VMEM((GH * (QUARTER // FEW), ROWS + 16, HD), F32),
@@ -722,10 +810,12 @@
         ],
         out_specs=(vmem, vmem),
     )(g1, f1, heads, layer_input, *out_weights)
-    rows = swap(rows, "ffn")
-
+    gate_up, rows = lax.optimization_barrier((jnp.swapaxes(gate_up_weight, 1, 2), rows))
+    mine = lax.all_to_all(rows, "ffn", 0, 0, axis_index_groups=parity)
+    ahead = fetched(gate_up)
+    theirs = lax.ppermute(mine, "ffn", neighbour)
     down_terms = run_ffn(
-        rows, ffn_gain.reshape(1, -1), jnp.swapaxes(gate_up_weight, 1, 2), down_weight
+        f1, mine, theirs, ffn_gain.reshape(1, -1), gate_up, down_weight, ahead
     )
     down_terms = swap(down_terms, "ffn")
     return call(finish_kernel, shape(QUARTER, COLS), [smem] + [vmem] * 2)(f1, down_terms, own)

time: 135 us -> 131 us (0.970)
  blocking collectives: 69.4 us -> 48 us
  waiting for transfers between devices: 21.4 us -> 28.2 us
  starting transfers between devices: 19.2 us -> 25.9 us
  Pallas kernels: 20.8 us -> 23.6 us
    all_to_all x4 -> x2, blocking collectives: 69.4 us -> 36 us  [swap(): return lax.all_to_all(value, axis, 0, 0)]
    all_to_all x0 -> x1, blocking collectives: none -> 12.1 us  [shards(): mine = lax.all_to_all(rows, 'ffn', 0, 0, axis_index_groups=parity)]
    all_to_all x0 -> x1, starting transfers between devices: none -> 7.69 us  [shards(): partial = lax.all_to_all(partial, 'ffn', 0, 0, axis_index_groups=parity)]
    ppermute x3 -> x5, waiting for transfers between devices: 8.16 us -> 14.7 us  [the longest x3 14.7 us: passed(): lax.ppermute(weight, 'grp', [(i, (i + amount) % grp) for i in range(grp)])]
    pallas_call x7 -> x10, Pallas kernels: 20.8 us -> 23.6 us  [placed(): function(*[pltpu.with_memory_space_constraint(a, pltpu.HBM) if spec is hb...]
    all_to_all x2, starting transfers between devices: 14.2 us -> 12.4 us  [swap(): return lax.all_to_all(value, axis, 0, 0)]
    ppermute x3 -> x5, starting transfers between devices: 4.99 us -> 5.81 us  [the longest x3 2.88 us: passed(): lax.ppermute(weight, 'grp', [(i, (i + amount) % grp) for i in range(grp)])]
  transfers between devices with their start and end apart: 5 -> 8, of which waited for: 4 -> 6; matrix products, arithmetic and copies ran while one was open for 2% -> 2% of each run, Pallas kernels for 0% -> 3%
where the time goes in v3:
time: 131 us; the launch traced here: 129 us
  blocking collectives  48 us (37%)
  waiting for transfers between devices  28.2 us (22%)
  starting transfers between devices  25.9 us (20%)
  Pallas kernels  23.6 us (18%)
  other arithmetic  2.95 us (2%)
    all_to_all x2, blocking collectives, swap(): return lax.all_to_all(value, axis, 0, 0)  36 us
    pallas_call x10, Pallas kernels, placed(): function(*[pltpu.with_memory_space_constraint(a, pltpu.HBM) if spec is hb...  23.6 us
    ppermute x3, waiting for transfers between devices, passed(): lax.ppermute(weight, 'grp', [(i, (i + amount) % grp) for i in range(grp)])  14.7 us
    all_to_all x2, waiting for transfers between devices, swap(): return lax.all_to_all(value, axis, 0, 0)  12.8 us
    all_to_all x2, starting transfers between devices, swap(): return lax.all_to_all(value, axis, 0, 0)  12.4 us
    all_to_all x1, blocking collectives, shards(): mine = lax.all_to_all(rows, 'ffn', 0, 0, axis_index_groups=parity)  12.1 us
    all_to_all x1, starting transfers between devices, shards(): partial = lax.all_to_all(partial, 'ffn', 0, 0, axis_index_groups=parity)  7.69 us
    ppermute x3, starting transfers between devices, passed(): lax.ppermute(weight, 'grp', [(i, (i + amount) % grp) for i in range(grp)])  2.88 us
  transfers between devices with their start and end apart: 8, of which 6 were waited for; matrix products, arithmetic and copies ran while one was open for 2% of the time, Pallas kernels for 3%

profile of v3, /device:TPU:1, one launch (start us, length us, event | category | flops | bytes accessed | tf_op | source)
XLA Modules:
  0.0 129.3 jit_solution(146831357188246137)
XLA Ops:
  0.0 1.9 %shard_map.118 = bf16[16,152,128]{2,1,0:T(8,128)(2,1)S(1)} custom-call(s32[1]{0:T(128)S(6)} %sub.21.p_ref, bf16[160,288]{1,0:T(8,128)(2,1)} %bitcast.17, f32[1,160]{1,0:T(1,128)} %bitcast.19, bf16[3,160,640]{2,1,0:T(8,128)(2,1)} %w_hbm.3), custom_call_target="tpu_custom_call" | custom-call | tf_op jit(solution)/shard_map/pallas_call | solution.py:625
  1.9 1.5 %collective-permute-start = (bf16[16,152,128]{2,1,0:T(8,128)(2,1)S(1)}, bf16[16,152,128]{2,1,0:T(8,128)(2,1)S(1)}, u32[]{:S(2)}, u32[]{:S(2)}) collective-permute-start(bf16[16,152,128]{2,1,0:T(8,128)(2,1)S(1)} %shard_map.118), channel_id=1, source_target_pairs={{0,1},{1,0},{2,3},{3,2},{4,5},{5,4},{6,7},{7,6},{8,9},{9,8},{10,11... | collective-permute-start | bytes 1867784 | tf_op jit(solution)/shard_map/ppermute | solution.py:742
  3.5 1.0 select_reduce_fusion
  5.8 1.9 %shard_map.119.left_ref = bf16[16,152,128]{2,1,0:T(8,128)(2,1)S(1)} custom-call(s32[1]{0:T(128)S(6)} %rem.32.p_ref, bf16[160,288]{1,0:T(8,128)(2,1)} %bitcast.18, f32[1,160]{1,0:T(1,128)} %bitcast.20, bf16[3,160,640]{2,1,0:T(8,128)(2,1)} %w_hbm.3), custom_call_target="tpu_custom_call" | custom-call | tf_op jit(solution)/shard_map/pallas_call | solution.py:625
  7.9 1.0 shard_map.120
  9.0 7.7 %all-to-all-start = ((bf16[16,152,128]{2,1,0:T(8,128)(2,1)}), bf16[16,152,128]{2,1,0:T(8,128)(2,1)S(1)}, u32[]{:S(2)}, u32[]{:S(2)}) async-start(bf16[16,152,128]{2,1,0:T(8,128)(2,1)} %shard_map.120), calls=%async_computation | async-start | bytes 1245184 | tf_op jit(solution)/shard_map/all_to_all | solution.py:781
  17.0 2.8 %collective-permute-start.2 = (bf16[160,640]{1,0:T(8,128)(2,1)S(1)}, bf16[160,640]{1,0:T(8,128)(2,1)S(1)}, u32[]{:S(2)}, u32[]{:S(2)}) collective-permute-start(bf16[160,640]{1,0:T(8,128)(2,1)S(1)} %bitcast.11), channel_id=1, source_target_pairs={{0,96},{32,0},{64,32},{96,64},{1,97},{33,1},{65,33},{97,65},{2,98}... | collective-permute-start | bytes 614408 | tf_op jit(solution)/shard_map/ppermute | solution.py:778
  19.8 4.2 %collective-permute-done.2.refs_3_ = bf16[160,640]{1,0:T(8,128)(2,1)S(1)} collective-permute-done((bf16[160,640]{1,0:T(8,128)(2,1)S(1)}, bf16[160,640]{1,0:T(8,128)(2,1)S(1)}, u32[]{:S(2)}, u32[]{:S(2)}) %collective-permute-start.2) | collective-permute-done | bytes 204832 | tf_op jit(solution)/shard_map/ppermute | solution.py:778
  24.0 3.1 %collective-permute-done.1.refs_1_ = bf16[160,640]{1,0:T(8,128)(2,1)S(1)} collective-permute-done((bf16[160,640]{1,0:T(8,128)(2,1)S(1)}, bf16[160,640]{1,0:T(8,128)(2,1)S(1)}, u32[]{:S(2)}, u32[]{:S(2)}) %collective-permute-start.1) | collective-permute-done | bytes 204832 | tf_op jit(solution)/shard_map/ppermute | solution.py:778
  27.8 0.9 shard_map.121
  28.7 7.7 %all-to-all-start.1 = ((bf16[32,48,128]{2,1,0:T(8,128)(2,1)}), bf16[32,48,128]{2,1,0:T(8,128)(2,1)S(1)}, u32[]{:S(2)}, u32[]{:S(2)}) async-start(bf16[32,48,128]{2,1,0:T(8,128)(2,1)} %get-tuple-element.36), calls=%async_computation.1 | async-start | bytes 786432 | tf_op jit(solution)/shard_map/all_to_all | solution.py:640
  36.8 7.4 %collective-permute-done.3.refs_2_ = bf16[160,640]{1,0:T(8,128)(2,1)S(1)} collective-permute-done((bf16[160,640]{1,0:T(8,128)(2,1)S(1)}, bf16[160,640]{1,0:T(8,128)(2,1)S(1)}, u32[]{:S(2)}, u32[]{:S(2)}) %collective-permute-start.3) | collective-permute-done | bytes 204832 | tf_op jit(solution)/shard_map/ppermute | solution.py:778
  44.2 2.6 %all-to-all-done.1 = bf16[32,48,128]{2,1,0:T(8,128)(2,1)S(1)} async-done(((bf16[32,48,128]{2,1,0:T(8,128)(2,1)}), bf16[32,48,128]{2,1,0:T(8,128)(2,1)S(1)}, u32[]{:S(2)}, u32[]{:S(2)}) %all-to-all-start.1) | async-done | bytes 393248 | tf_op jit(solution)/shard_map/all_to_all | solution.py:640
  46.8 7.7 %shard_map.122 = bf16[128,16,128]{2,1,0:T(8,128)(2,1)S(1)} custom-call(s32[3,34]{1,0:T(4,128)S(1)} %pad_add_fusion.lists, s32[28]{0:T(128)S(1)} %get-tuple-element.53.left_ref, s32[28]{0:T(128)S(1)} %get-tuple-element.55.token_ref, s32[1]{0:T(128)} %bitcast.f_ref, bf16[1536,128]{1,0:T(8,128)(2,1)S(1)} %bitcast.10, ...), custom_call_target="tpu_custom_call" | custom-call | tf_op jit(solution)/shard_map/pallas_call | solution.py:625
  54.5 18.1 %all_to_all.30.in_ref = bf16[128,16,128]{2,1,0:T(8,128)(2,1)S(1)} all-to-all(bf16[128,16,128]{2,1,0:T(8,128)(2,1)S(1)} %shard_map.122), channel_id=1, replica_groups=mesh['grp'=4,'ffn'=32] {'grp','ffn'}, dimensions={0} | all-to-all | bytes 1048576 | tf_op jit(solution)/shard_map/all_to_all | solution.py:640
  72.6 1.5 %shard_map.123 = bf16[32,48,128]{2,1,0:T(8,128)(2,1)} custom-call(bf16[128,16,128]{2,1,0:T(8,128)(2,1)S(1)} %all_to_all.30.in_ref), custom_call_target="tpu_custom_call" | custom-call | tf_op jit(solution)/shard_map/pallas_call | solution.py:625
  74.1 4.7 %all-to-all-start.3 = ((bf16[32,48,128]{2,1,0:T(8,128)(2,1)}), bf16[32,48,128]{2,1,0:T(8,128)(2,1)S(1)}, u32[]{:S(2)}, u32[]{:S(2)}) async-start(bf16[32,48,128]{2,1,0:T(8,128)(2,1)} %shard_map.123), calls=%async_computation.3 | async-start | bytes 786432 | tf_op jit(solution)/shard_map/all_to_all | solution.py:640
  79.0 10.3 %all-to-all-done.3.in_ref = bf16[32,48,128]{2,1,0:T(8,128)(2,1)S(1)} async-done(((bf16[32,48,128]{2,1,0:T(8,128)(2,1)}), bf16[32,48,128]{2,1,0:T(8,128)(2,1)S(1)}, u32[]{:S(2)}, u32[]{:S(2)}) %all-to-all-start.3) | async-done | bytes 393248 | tf_op jit(solution)/shard_map/all_to_all | solution.py:640
  89.9 12.1 %all_to_all.31.mine_ref = bf16[16,96,128]{2,1,0:T(8,128)(2,1)S(1)} all-to-all(bf16[16,96,128]{2,1,0:T(8,128)(2,1)S(1)} %get-tuple-element.45), channel_id=1, replica_groups={{0,2,4,6,8,10,12,14,16,18,20,22,24,26,28,30},{1,3,5,7,9,11,13,15,17,19,..., dimensions={0} | all-to-all | bytes 786432 | tf_op jit(solution)/shard_map/all_to_all | solution.py:814
  102.0 1.4 %collective-permute-start.4 = (bf16[16,96,128]{2,1,0:T(8,128)(2,1)S(1)}, bf16[16,96,128]{2,1,0:T(8,128)(2,1)S(1)}, u32[]{:S(2)}, u32[]{:S(2)}) collective-permute-start(bf16[16,96,128]{2,1,0:T(8,128)(2,1)S(1)} %all_to_all.31.mine_ref), channel_id=1, source_target_pairs={{0,1},{1,0},{2,3},{3,2},{4,5},{5,4},{6,7},{7,6},{8,9},{9,8},{10,11... | collective-permute-start | bytes 1179656 | tf_op jit(solution)/shard_map/ppermute | solution.py:816
  103.4 1.9 %shard_map.125 = (bf16[2,432,640]{2,1,0:T(8,128)(2,1)S(1)}, bf16[2,432,640]{2,1,0:T(8,128)(2,1)S(1)}, bf16[2,432,640]{2,1,0:T(8,128)(2,1)S(1)}) custom-call(bf16[2,432,5120]{2,1,0:T(8,128)(2,1)} %bitcast.15), custom_call_target="tpu_custom_call" | custom-call | tf_op jit(solution)/shard_map/pallas_call | solution.py:625
  105.4 5.1 %shard_map.126 = bf16[32,96,128]{2,1,0:T(8,128)(2,1)S(1)} custom-call(s32[1]{0:T(128)} %bitcast.f_ref, bf16[16,96,128]{2,1,0:T(8,128)(2,1)S(1)} %all_to_all.31.mine_ref, bf16[16,96,128]{2,1,0:T(8,128)(2,1)S(1)} %collective-permute-done.4.theirs_ref, f32[1,5120]{1,0:T(1,128)S(1)} %bitcast.14, bf16[2,432,5120]{2,1,0:T(8,128)(2,1)} %bitcast.16, ...), custom_call_target="tpu_custom_call" | custom-call | tf_op jit(solution)/shard_map/pallas_call | solution.py:625
  110.5 17.9 %all_to_all.32.in_ref = bf16[32,96,128]{2,1,0:T(8,128)(2,1)S(1)} all-to-all(bf16[32,96,128]{2,1,0:T(8,128)(2,1)S(1)} %shard_map.126), channel_id=1, replica_groups=mesh['grp'=4,'ffn'=32] {'ffn'}, dimensions={0} | all-to-all | bytes 1572864 | tf_op jit(solution)/shard_map/all_to_all | solution.py:640
  128.4 0.8 shard_map.127
  (40 shorter events, 3.8 us)
Async XLA Ops:
  0.0 16.7 %copy-start.3 = (s32[32]{0:T(128)S(1)}, s32[32]{0:T(128)}, u32[]{:S(2)}) copy-start(s32[32]{0:T(128)} %param.22) | copy-start | bytes 388
  0.0 8.9 %copy-start.4 = (s32[2]{0:T(128)S(1)}, s32[2]{0:T(128)}, u32[]{:S(2)}) copy-start(s32[2]{0:T(128)} %param.21) | copy-start | bytes 28
  0.0 17.0 %copy-start = (bf16[640,160]{0,1:T(8,128)(2,1)S(1)}, bf16[640,160]{0,1:T(8,128)(2,1)}, u32[]{:S(2)}) copy-start(bf16[640,160]{0,1:T(8,128)(2,1)} %param.17) | copy-start | bytes 614404
  1.9 6.0 %collective-permute-start = (bf16[16,152,128]{2,1,0:T(8,128)(2,1)S(1)}, bf16[16,152,128]{2,1,0:T(8,128)(2,1)S(1)}, u32[]{:S(2)}, u32[]{:S(2)}) collective-permute-start(bf16[16,152,128]{2,1,0:T(8,128)(2,1)S(1)} %shard_map.118), channel_id=1, source_target_pairs={{0,1},{1,0},{2,3},{3,2},{4,5},{5,4},{6,7},{7,6},{8,9},{9,8},{10,11... | collective-permute-start | bytes 1867784 | tf_op jit(solution)/shard_map/ppermute | solution.py:742
  9.0 18.8 %all-to-all-start = ((bf16[16,152,128]{2,1,0:T(8,128)(2,1)}), bf16[16,152,128]{2,1,0:T(8,128)(2,1)S(1)}, u32[]{:S(2)}, u32[]{:S(2)}) async-start(bf16[16,152,128]{2,1,0:T(8,128)(2,1)} %shard_map.120), calls=%async_computation | async-start | bytes 1245184 | tf_op jit(solution)/shard_map/all_to_all | solution.py:781
  17.0 7.0 %collective-permute-start.2 = (bf16[160,640]{1,0:T(8,128)(2,1)S(1)}, bf16[160,640]{1,0:T(8,128)(2,1)S(1)}, u32[]{:S(2)}, u32[]{:S(2)}) collective-permute-start(bf16[160,640]{1,0:T(8,128)(2,1)S(1)} %bitcast.11), channel_id=1, source_target_pairs={{0,96},{32,0},{64,32},{96,64},{1,97},{33,1},{65,33},{97,65},{2,98}... | collective-permute-start | bytes 614408 | tf_op jit(solution)/shard_map/ppermute | solution.py:778
  19.8 7.3 %collective-permute-start.1 = (bf16[160,640]{1,0:T(8,128)(2,1)S(1)}, bf16[160,640]{1,0:T(8,128)(2,1)S(1)}, u32[]{:S(2)}, u32[]{:S(2)}) collective-permute-start(bf16[160,640]{1,0:T(8,128)(2,1)S(1)} %bitcast.12), channel_id=1, source_target_pairs={{0,32},{32,64},{64,96},{96,0},{1,33},{33,65},{65,97},{97,1},{2,34}... | collective-permute-start | bytes 614408 | tf_op jit(solution)/shard_map/ppermute | solution.py:778
  28.7 18.0 %all-to-all-start.1 = ((bf16[32,48,128]{2,1,0:T(8,128)(2,1)}), bf16[32,48,128]{2,1,0:T(8,128)(2,1)S(1)}, u32[]{:S(2)}, u32[]{:S(2)}) async-start(bf16[32,48,128]{2,1,0:T(8,128)(2,1)} %get-tuple-element.36), calls=%async_computation.1 | async-start | bytes 786432 | tf_op jit(solution)/shard_map/all_to_all | solution.py:640
  36.5 7.7 %collective-permute-start.3 = (bf16[160,640]{1,0:T(8,128)(2,1)S(1)}, bf16[160,640]{1,0:T(8,128)(2,1)S(1)}, u32[]{:S(2)}, u32[]{:S(2)}) collective-permute-start(bf16[160,640]{1,0:T(8,128)(2,1)S(1)} %collective-permute-done.1.refs_1_), channel_id=1, source_target_pairs={{0,32},{32,64},{64,96},{96,0},{1,33},{33,65},{65,97},{97,1},{2,34}... | collective-permute-start | bytes 614408 | tf_op jit(solution)/shard_map/ppermute | solution.py:778
  46.8 32.1 %copy-start.2 = (bf16[288,160]{0,1:T(8,128)(2,1)S(1)}, bf16[288,160]{0,1:T(8,128)(2,1)}, u32[]{:S(2)}) copy-start(bf16[288,160]{0,1:T(8,128)(2,1)} %param.12) | copy-start | bytes 276484
  74.1 15.2 %all-to-all-start.3 = ((bf16[32,48,128]{2,1,0:T(8,128)(2,1)}), bf16[32,48,128]{2,1,0:T(8,128)(2,1)S(1)}, u32[]{:S(2)}, u32[]{:S(2)}) async-start(bf16[32,48,128]{2,1,0:T(8,128)(2,1)} %shard_map.123), calls=%async_computation.3 | async-start | bytes 786432 | tf_op jit(solution)/shard_map/all_to_all | solution.py:640
  102.0 3.4 %copy-start.1 = (f32[5120]{0:T(1024)S(1)}, f32[5120]{0:T(1024)}, u32[]{:S(2)}) copy-start(f32[5120]{0:T(1024)} %param.18) | copy-start | bytes 61444
  102.0 3.4 %collective-permute-start.4 = (bf16[16,96,128]{2,1,0:T(8,128)(2,1)S(1)}, bf16[16,96,128]{2,1,0:T(8,128)(2,1)S(1)}, u32[]{:S(2)}, u32[]{:S(2)}) collective-permute-start(bf16[16,96,128]{2,1,0:T(8,128)(2,1)S(1)} %all_to_all.31.mine_ref), channel_id=1, source_target_pairs={{0,1},{1,0},{2,3},{3,2},{4,5},{5,4},{6,7},{7,6},{8,9},{9,8},{10,11... | collective-permute-start | bytes 1179656 | tf_op jit(solution)/shard_map/ppermute | solution.py:816

commit v4 on v3

--- a/solution.py
+++ b/solution.py
@@ -531,7 +531,8 @@
 
 
 def ffn_kernel(f_ref, mine_ref, theirs_ref, gain_ref, gate_hbm, down_hbm, *refs):
-    ahead, (out_ref, rows, normed, gates, down, hidden, sems) = refs[:AHEAD], refs[AHEAD:]
+    ahead, refs = refs[:AHEAD], refs[AHEAD:]
+    keep_ref, send_ref, rows, normed, gates, down, hidden, sems = refs
     copies = []
     for c in range(AHEAD, D // FCHUNK):
         part = pl.ds(c * FCHUNK, FCHUNK)
@@ -572,12 +573,20 @@
     hidden[...] = (gate / (1.0 + jnp.exp(-gate)) * up).astype(BF16)
     copies[-1].wait()
     wide = 4 * COLS
-    for s in range(out_ref.shape[0] // 4):
+    for s in range(keep_ref.shape[0] // 2):
         product = jnp.dot(
             hidden[...], down[:, s * wide : (s + 1) * wide], preferred_element_type=F32
         )
-        for j, message in enumerate(messages_of(product)):
-            out_ref[4 * s + j] = message
+        messages = messages_of(product)
+        for j in range(2):
+            even, uneven = messages[2 * j], messages[2 * j + 1]
+            keep_ref[2 * s + j] = jnp.where(odd, uneven, even)
+            send_ref[2 * s + j] = jnp.where(odd, even, uneven)
+
+
+def join_kernel(left_ref, right_ref, out_ref):
+    for i in range(out_ref.shape[0]):
+        out_ref[i] = (left_ref[i].astype(F32) + right_ref[i].astype(F32)).astype(BF16)
 
 
 def finish_kernel(f_ref, in_ref, own_ref, out_ref):
@@ -684,7 +693,7 @@
     hidden_units = down.shape[0]
     return call(
         ffn_kernel,
-        shape(2 * mine.shape[0], MSG, HD),
+        (shape(*mine.shape), shape(*mine.shape)),
         [smem] + [vmem] * 3 + [hbm] * 2 + [vmem] * AHEAD,
         [
             pltpu.VMEM((QUARTER, D), F32),
@@ -694,6 +703,7 @@
             pltpu.VMEM((QUARTER, hidden_units), BF16),
             pltpu.SemaphoreType.DMA((D // FCHUNK + 1,)),
         ],
+        out_specs=(vmem, vmem),
     )(f1, mine, theirs, gain, gate_up, down, *ahead)
 
 
@@ -814,10 +824,12 @@
     mine = lax.all_to_all(rows, "ffn", 0, 0, axis_index_groups=parity)
     ahead = fetched(gate_up)
     theirs = lax.ppermute(mine, "ffn", neighbour)
-    down_terms = run_ffn(
+    kept, sent = run_ffn(
         f1, mine, theirs, ffn_gain.reshape(1, -1), gate_up, down_weight, ahead
     )
-    down_terms = swap(down_terms, "ffn")
+    received = lax.ppermute(sent, "ffn", neighbour)
+    down_terms = call(join_kernel, shape(*kept.shape), [vmem] * 2)(kept, received)
+    down_terms = lax.all_to_all(down_terms, "ffn", 0, 0, axis_index_groups=parity)
     return call(finish_kernel, shape(QUARTER, COLS), [smem] + [vmem] * 2)(f1, down_terms, own)
 
 

time: 131 us -> 128 us (0.977)
  blocking collectives: 48 us -> 42.6 us
  waiting for transfers between devices: 28.2 us -> 29.9 us
    all_to_all x2 -> x1, blocking collectives: 36 us -> 18 us  [swap(): return lax.all_to_all(value, axis, 0, 0)]
    all_to_all x0 -> x1, blocking collectives: none -> 12.5 us  [shards(): lax.all_to_all(down_terms, 'ffn', 0, 0, axis_index_groups=parity)]
    ppermute x1 -> x2, waiting for transfers between devices: 0.01 us -> 1.71 us  [shards(): received = lax.ppermute(sent, 'ffn', neighbour)]
    pallas_call x10 -> x11, Pallas kernels: 23.6 us -> 24.7 us  [placed(): function(*[pltpu.with_memory_space_constraint(a, pltpu.HBM) if spec is hb...]
  transfers between devices with their start and end apart: 8 -> 9, of which waited for: 6 -> 7; matrix products, arithmetic and copies ran while one was open for 2% -> 2% of each run, Pallas kernels for 3% -> 3%
where the time goes in v4:
time: 128 us; the launch traced here: 127 us
  blocking collectives  42.6 us (33%)
  waiting for transfers between devices  29.9 us (23%)
  starting transfers between devices  26 us (20%)
  Pallas kernels  24.7 us (19%)
  other arithmetic  2.95 us (2%)
    pallas_call x11, Pallas kernels, placed(): function(*[pltpu.with_memory_space_constraint(a, pltpu.HBM) if spec is hb...  24.7 us
    all_to_all x1, blocking collectives, swap(): return lax.all_to_all(value, axis, 0, 0)  18 us
    ppermute x3, waiting for transfers between devices, passed(): lax.ppermute(weight, 'grp', [(i, (i + amount) % grp) for i in range(grp)])  14.7 us
    all_to_all x2, waiting for transfers between devices, swap(): return lax.all_to_all(value, axis, 0, 0)  12.8 us
    all_to_all x1, blocking collectives, shards(): lax.all_to_all(down_terms, 'ffn', 0, 0, axis_index_groups=parity)  12.5 us
    all_to_all x2, starting transfers between devices, swap(): return lax.all_to_all(value, axis, 0, 0)  12.4 us
    all_to_all x1, blocking collectives, shards(): mine = lax.all_to_all(rows, 'ffn', 0, 0, axis_index_groups=parity)  12.1 us
    all_to_all x1, starting transfers between devices, shards(): partial = lax.all_to_all(partial, 'ffn', 0, 0, axis_index_groups=parity)  7.69 us
  transfers between devices with their start and end apart: 9, of which 7 were waited for; matrix products, arithmetic and copies ran while one was open for 2% of the time, Pallas kernels for 3%

profile of v4, /device:TPU:1, one launch (start us, length us, event | category | flops | bytes accessed | tf_op | source)
XLA Modules:
  0.0 126.8 jit_solution(4470230109861128271)
XLA Ops:
  0.0 1.9 %shard_map.118 = bf16[16,152,128]{2,1,0:T(8,128)(2,1)S(1)} custom-call(s32[1]{0:T(128)S(6)} %sub.21.p_ref, bf16[160,288]{1,0:T(8,128)(2,1)} %bitcast.17, f32[1,160]{1,0:T(1,128)} %bitcast.19, bf16[3,160,640]{2,1,0:T(8,128)(2,1)} %w_hbm.3), custom_call_target="tpu_custom_call" | custom-call | tf_op jit(solution)/shard_map/pallas_call | solution.py:634
  1.9 1.5 %collective-permute-start = (bf16[16,152,128]{2,1,0:T(8,128)(2,1)S(1)}, bf16[16,152,128]{2,1,0:T(8,128)(2,1)S(1)}, u32[]{:S(2)}, u32[]{:S(2)}) collective-permute-start(bf16[16,152,128]{2,1,0:T(8,128)(2,1)S(1)} %shard_map.118), channel_id=1, source_target_pairs={{0,1},{1,0},{2,3},{3,2},{4,5},{5,4},{6,7},{7,6},{8,9},{9,8},{10,11... | collective-permute-start | bytes 1867784 | tf_op jit(solution)/shard_map/ppermute | solution.py:752
  3.5 1.0 select_reduce_fusion
  5.8 1.9 %shard_map.119.left_ref = bf16[16,152,128]{2,1,0:T(8,128)(2,1)S(1)} custom-call(s32[1]{0:T(128)S(6)} %rem.32.p_ref, bf16[160,288]{1,0:T(8,128)(2,1)} %bitcast.18, f32[1,160]{1,0:T(1,128)} %bitcast.20, bf16[3,160,640]{2,1,0:T(8,128)(2,1)} %w_hbm.3), custom_call_target="tpu_custom_call" | custom-call | tf_op jit(solution)/shard_map/pallas_call | solution.py:634
  7.9 1.0 shard_map.120
  9.0 7.7 %all-to-all-start = ((bf16[16,152,128]{2,1,0:T(8,128)(2,1)}), bf16[16,152,128]{2,1,0:T(8,128)(2,1)S(1)}, u32[]{:S(2)}, u32[]{:S(2)}) async-start(bf16[16,152,128]{2,1,0:T(8,128)(2,1)} %shard_map.120), calls=%async_computation | async-start | bytes 1245184 | tf_op jit(solution)/shard_map/all_to_all | solution.py:791
  17.0 2.8 %collective-permute-start.2 = (bf16[160,640]{1,0:T(8,128)(2,1)S(1)}, bf16[160,640]{1,0:T(8,128)(2,1)S(1)}, u32[]{:S(2)}, u32[]{:S(2)}) collective-permute-start(bf16[160,640]{1,0:T(8,128)(2,1)S(1)} %bitcast.11), channel_id=1, source_target_pairs={{0,96},{32,0},{64,32},{96,64},{1,97},{33,1},{65,33},{97,65},{2,98}... | collective-permute-start | bytes 614408 | tf_op jit(solution)/shard_map/ppermute | solution.py:788
  19.8 4.2 %collective-permute-done.2.refs_3_ = bf16[160,640]{1,0:T(8,128)(2,1)S(1)} collective-permute-done((bf16[160,640]{1,0:T(8,128)(2,1)S(1)}, bf16[160,640]{1,0:T(8,128)(2,1)S(1)}, u32[]{:S(2)}, u32[]{:S(2)}) %collective-permute-start.2) | collective-permute-done | bytes 204832 | tf_op jit(solution)/shard_map/ppermute | solution.py:788
  24.0 3.1 %collective-permute-done.1.refs_1_ = bf16[160,640]{1,0:T(8,128)(2,1)S(1)} collective-permute-done((bf16[160,640]{1,0:T(8,128)(2,1)S(1)}, bf16[160,640]{1,0:T(8,128)(2,1)S(1)}, u32[]{:S(2)}, u32[]{:S(2)}) %collective-permute-start.1) | collective-permute-done | bytes 204832 | tf_op jit(solution)/shard_map/ppermute | solution.py:788
  27.8 0.9 shard_map.121
  28.7 7.7 %all-to-all-start.1 = ((bf16[32,48,128]{2,1,0:T(8,128)(2,1)}), bf16[32,48,128]{2,1,0:T(8,128)(2,1)S(1)}, u32[]{:S(2)}, u32[]{:S(2)}) async-start(bf16[32,48,128]{2,1,0:T(8,128)(2,1)} %get-tuple-element.38), calls=%async_computation.1 | async-start | bytes 786432 | tf_op jit(solution)/shard_map/all_to_all | solution.py:649
  36.8 7.4 %collective-permute-done.3.refs_2_ = bf16[160,640]{1,0:T(8,128)(2,1)S(1)} collective-permute-done((bf16[160,640]{1,0:T(8,128)(2,1)S(1)}, bf16[160,640]{1,0:T(8,128)(2,1)S(1)}, u32[]{:S(2)}, u32[]{:S(2)}) %collective-permute-start.3) | collective-permute-done | bytes 204832 | tf_op jit(solution)/shard_map/ppermute | solution.py:788
  44.2 2.6 %all-to-all-done.1 = bf16[32,48,128]{2,1,0:T(8,128)(2,1)S(1)} async-done(((bf16[32,48,128]{2,1,0:T(8,128)(2,1)}), bf16[32,48,128]{2,1,0:T(8,128)(2,1)S(1)}, u32[]{:S(2)}, u32[]{:S(2)}) %all-to-all-start.1) | async-done | bytes 393248 | tf_op jit(solution)/shard_map/all_to_all | solution.py:649
  46.7 8.7 %shard_map.122 = bf16[128,16,128]{2,1,0:T(8,128)(2,1)S(1)} custom-call(s32[3,34]{1,0:T(4,128)S(1)} %pad_add_fusion.lists, s32[28]{0:T(128)S(1)} %get-tuple-element.57.left_ref, s32[28]{0:T(128)S(1)} %get-tuple-element.59.token_ref, s32[1]{0:T(128)} %bitcast.f_ref, bf16[1536,128]{1,0:T(8,128)(2,1)S(1)} %bitcast.10, ...), custom_call_target="tpu_custom_call" | custom-call | tf_op jit(solution)/shard_map/pallas_call | solution.py:634
  55.4 18.0 %all_to_all.30.in_ref = bf16[128,16,128]{2,1,0:T(8,128)(2,1)S(1)} all-to-all(bf16[128,16,128]{2,1,0:T(8,128)(2,1)S(1)} %shard_map.122), channel_id=1, replica_groups=mesh['grp'=4,'ffn'=32] {'grp','ffn'}, dimensions={0} | all-to-all | bytes 1048576 | tf_op jit(solution)/shard_map/all_to_all | solution.py:649
  73.5 1.5 %shard_map.123 = bf16[32,48,128]{2,1,0:T(8,128)(2,1)} custom-call(bf16[128,16,128]{2,1,0:T(8,128)(2,1)S(1)} %all_to_all.30.in_ref), custom_call_target="tpu_custom_call" | custom-call | tf_op jit(solution)/shard_map/pallas_call | solution.py:634
  75.0 4.7 %all-to-all-start.3 = ((bf16[32,48,128]{2,1,0:T(8,128)(2,1)}), bf16[32,48,128]{2,1,0:T(8,128)(2,1)S(1)}, u32[]{:S(2)}, u32[]{:S(2)}) async-start(bf16[32,48,128]{2,1,0:T(8,128)(2,1)} %shard_map.123), calls=%async_computation.3 | async-start | bytes 786432 | tf_op jit(solution)/shard_map/all_to_all | solution.py:649
  79.8 10.3 %all-to-all-done.3.in_ref = bf16[32,48,128]{2,1,0:T(8,128)(2,1)S(1)} async-done(((bf16[32,48,128]{2,1,0:T(8,128)(2,1)}), bf16[32,48,128]{2,1,0:T(8,128)(2,1)S(1)}, u32[]{:S(2)}, u32[]{:S(2)}) %all-to-all-start.3) | async-done | bytes 393248 | tf_op jit(solution)/shard_map/all_to_all | solution.py:649
  90.8 12.1 %all_to_all.31.mine_ref = bf16[16,96,128]{2,1,0:T(8,128)(2,1)S(1)} all-to-all(bf16[16,96,128]{2,1,0:T(8,128)(2,1)S(1)} %get-tuple-element.47), channel_id=1, replica_groups={{0,2,4,6,8,10,12,14,16,18,20,22,24,26,28,30},{1,3,5,7,9,11,13,15,17,19,..., dimensions={0} | all-to-all | bytes 786432 | tf_op jit(solution)/shard_map/all_to_all | solution.py:824
  102.9 1.4 %collective-permute-start.4 = (bf16[16,96,128]{2,1,0:T(8,128)(2,1)S(1)}, bf16[16,96,128]{2,1,0:T(8,128)(2,1)S(1)}, u32[]{:S(2)}, u32[]{:S(2)}) collective-permute-start(bf16[16,96,128]{2,1,0:T(8,128)(2,1)S(1)} %all_to_all.31.mine_ref), channel_id=1, source_target_pairs={{0,1},{1,0},{2,3},{3,2},{4,5},{5,4},{6,7},{7,6},{8,9},{9,8},{10,11... | collective-permute-start | bytes 1179656 | tf_op jit(solution)/shard_map/ppermute | solution.py:826
  104.3 1.9 %shard_map.125 = (bf16[2,432,640]{2,1,0:T(8,128)(2,1)S(1)}, bf16[2,432,640]{2,1,0:T(8,128)(2,1)S(1)}, bf16[2,432,640]{2,1,0:T(8,128)(2,1)S(1)}) custom-call(bf16[2,432,5120]{2,1,0:T(8,128)(2,1)} %bitcast.15), custom_call_target="tpu_custom_call" | custom-call | tf_op jit(solution)/shard_map/pallas_call | solution.py:634
  106.3 5.3 %shard_map.126 = (bf16[16,96,128]{2,1,0:T(8,128)(2,1)S(1)}, bf16[16,96,128]{2,1,0:T(8,128)(2,1)S(1)}) custom-call(s32[1]{0:T(128)} %bitcast.f_ref, bf16[16,96,128]{2,1,0:T(8,128)(2,1)S(1)} %all_to_all.31.mine_ref, bf16[16,96,128]{2,1,0:T(8,128)(2,1)S(1)} %collective-permute-done.4.theirs_ref, f32[1,5120]{1,0:T(1,128)S(1)} %bitcast.14, ...), custom_call_target="tpu_custom_call" | custom-call | tf_op jit(solution)/shard_map/pallas_call | solution.py:634
  111.7 1.7 %collective-permute-done.5.right_ref = bf16[16,96,128]{2,1,0:T(8,128)(2,1)S(1)} collective-permute-done((bf16[16,96,128]{2,1,0:T(8,128)(2,1)S(1)}, bf16[16,96,128]{2,1,0:T(8,128)(2,1)S(1)}, u32[]{:S(2)}, u32[]{:S(2)}) %collective-permute-start.5) | collective-permute-done | bytes 393248 | tf_op jit(solution)/shard_map/ppermute | solution.py:830
  113.5 12.5 %all_to_all.32.in_ref = bf16[16,96,128]{2,1,0:T(8,128)(2,1)S(1)} all-to-all(bf16[16,96,128]{2,1,0:T(8,128)(2,1)S(1)} %shard_map.127), channel_id=1, replica_groups={{0,2,4,6,8,10,12,14,16,18,20,22,24,26,28,30},{1,3,5,7,9,11,13,15,17,19,..., dimensions={0} | all-to-all | bytes 786432 | tf_op jit(solution)/shard_map/all_to_all | solution.py:832
  (43 shorter events, 4.7 us)
Async XLA Ops:
  0.0 16.7 %copy-start.3 = (s32[32]{0:T(128)S(1)}, s32[32]{0:T(128)}, u32[]{:S(2)}) copy-start(s32[32]{0:T(128)} %param.22) | copy-start | bytes 388
  0.0 8.9 %copy-start.4 = (s32[2]{0:T(128)S(1)}, s32[2]{0:T(128)}, u32[]{:S(2)}) copy-start(s32[2]{0:T(128)} %param.21) | copy-start | bytes 28
  0.0 17.0 %copy-start = (bf16[640,160]{0,1:T(8,128)(2,1)S(1)}, bf16[640,160]{0,1:T(8,128)(2,1)}, u32[]{:S(2)}) copy-start(bf16[640,160]{0,1:T(8,128)(2,1)} %param.17) | copy-start | bytes 614404
  1.9 6.0 %collective-permute-start = (bf16[16,152,128]{2,1,0:T(8,128)(2,1)S(1)}, bf16[16,152,128]{2,1,0:T(8,128)(2,1)S(1)}, u32[]{:S(2)}, u32[]{:S(2)}) collective-permute-start(bf16[16,152,128]{2,1,0:T(8,128)(2,1)S(1)} %shard_map.118), channel_id=1, source_target_pairs={{0,1},{1,0},{2,3},{3,2},{4,5},{5,4},{6,7},{7,6},{8,9},{9,8},{10,11... | collective-permute-start | bytes 1867784 | tf_op jit(solution)/shard_map/ppermute | solution.py:752
  9.0 18.8 %all-to-all-start = ((bf16[16,152,128]{2,1,0:T(8,128)(2,1)}), bf16[16,152,128]{2,1,0:T(8,128)(2,1)S(1)}, u32[]{:S(2)}, u32[]{:S(2)}) async-start(bf16[16,152,128]{2,1,0:T(8,128)(2,1)} %shard_map.120), calls=%async_computation | async-start | bytes 1245184 | tf_op jit(solution)/shard_map/all_to_all | solution.py:791
  17.0 7.0 %collective-permute-start.2 = (bf16[160,640]{1,0:T(8,128)(2,1)S(1)}, bf16[160,640]{1,0:T(8,128)(2,1)S(1)}, u32[]{:S(2)}, u32[]{:S(2)}) collective-permute-start(bf16[160,640]{1,0:T(8,128)(2,1)S(1)} %bitcast.11), channel_id=1, source_target_pairs={{0,96},{32,0},{64,32},{96,64},{1,97},{33,1},{65,33},{97,65},{2,98}... | collective-permute-start | bytes 614408 | tf_op jit(solution)/shard_map/ppermute | solution.py:788
  19.8 7.3 %collective-permute-start.1 = (bf16[160,640]{1,0:T(8,128)(2,1)S(1)}, bf16[160,640]{1,0:T(8,128)(2,1)S(1)}, u32[]{:S(2)}, u32[]{:S(2)}) collective-permute-start(bf16[160,640]{1,0:T(8,128)(2,1)S(1)} %bitcast.12), channel_id=1, source_target_pairs={{0,32},{32,64},{64,96},{96,0},{1,33},{33,65},{65,97},{97,1},{2,34}... | collective-permute-start | bytes 614408 | tf_op jit(solution)/shard_map/ppermute | solution.py:788
  28.7 18.0 %all-to-all-start.1 = ((bf16[32,48,128]{2,1,0:T(8,128)(2,1)}), bf16[32,48,128]{2,1,0:T(8,128)(2,1)S(1)}, u32[]{:S(2)}, u32[]{:S(2)}) async-start(bf16[32,48,128]{2,1,0:T(8,128)(2,1)} %get-tuple-element.38), calls=%async_computation.1 | async-start | bytes 786432 | tf_op jit(solution)/shard_map/all_to_all | solution.py:649
  36.4 7.7 %collective-permute-start.3 = (bf16[160,640]{1,0:T(8,128)(2,1)S(1)}, bf16[160,640]{1,0:T(8,128)(2,1)S(1)}, u32[]{:S(2)}, u32[]{:S(2)}) collective-permute-start(bf16[160,640]{1,0:T(8,128)(2,1)S(1)} %collective-permute-done.1.refs_1_), channel_id=1, source_target_pairs={{0,32},{32,64},{64,96},{96,0},{1,33},{33,65},{65,97},{97,1},{2,34}... | collective-permute-start | bytes 614408 | tf_op jit(solution)/shard_map/ppermute | solution.py:788
  46.7 33.0 %copy-start.2 = (bf16[288,160]{0,1:T(8,128)(2,1)S(1)}, bf16[288,160]{0,1:T(8,128)(2,1)}, u32[]{:S(2)}) copy-start(bf16[288,160]{0,1:T(8,128)(2,1)} %param.12) | copy-start | bytes 276484
  75.0 15.2 %all-to-all-start.3 = ((bf16[32,48,128]{2,1,0:T(8,128)(2,1)}), bf16[32,48,128]{2,1,0:T(8,128)(2,1)S(1)}, u32[]{:S(2)}, u32[]{:S(2)}) async-start(bf16[32,48,128]{2,1,0:T(8,128)(2,1)} %shard_map.123), calls=%async_computation.3 | async-start | bytes 786432 | tf_op jit(solution)/shard_map/all_to_all | solution.py:649
  102.9 3.4 %copy-start.1 = (f32[5120]{0:T(1024)S(1)}, f32[5120]{0:T(1024)}, u32[]{:S(2)}) copy-start(f32[5120]{0:T(1024)} %param.18) | copy-start | bytes 61444
  102.9 3.4 %collective-permute-start.4 = (bf16[16,96,128]{2,1,0:T(8,128)(2,1)S(1)}, bf16[16,96,128]{2,1,0:T(8,128)(2,1)S(1)}, u32[]{:S(2)}, u32[]{:S(2)}) collective-permute-start(bf16[16,96,128]{2,1,0:T(8,128)(2,1)S(1)} %all_to_all.31.mine_ref), channel_id=1, source_target_pairs={{0,1},{1,0},{2,3},{3,2},{4,5},{5,4},{6,7},{7,6},{8,9},{9,8},{10,11... | collective-permute-start | bytes 1179656 | tf_op jit(solution)/shard_map/ppermute | solution.py:826
  111.6 1.8 %collective-permute-start.5 = (bf16[16,96,128]{2,1,0:T(8,128)(2,1)S(1)}, bf16[16,96,128]{2,1,0:T(8,128)(2,1)S(1)}, u32[]{:S(2)}, u32[]{:S(2)}) collective-permute-start(bf16[16,96,128]{2,1,0:T(8,128)(2,1)S(1)} %get-tuple-element.53), channel_id=1, source_target_pairs={{0,1},{1,0},{2,3},{3,2},{4,5},{5,4},{6,7},{7,6},{8,9},{9,8},{10,11... | collective-permute-start | bytes 1179656 | tf_op jit(solution)/shard_map/ppermute | solution.py:830

commit v5 on v4

--- a/solution.py
+++ b/solution.py
@@ -149,7 +149,8 @@
     own_ref,
     key_hbm,
     value_hbm,
-    out_ref,
+    keep_ref,
+    send_ref,
     keys,
     values,
     sems,
@@ -386,20 +387,54 @@
 
     row = rows_of((16, HD))
     diagonal = (row == lanes((16, HD))) & (row < FEW)
-    ffn = out_ref.shape[0] // (TOKENS // QUARTER)
+    odd = lax.rem(f, 2) == 1
+    half = keep_ref.shape[0] // (TOKENS // QUARTER)
+    per_head = QUARTER // FEW
+
+    def block_of(q, h, b):
+        part = pl.ds(q * QUARTER + b * FEW, 16)
+        stat = jnp.sum(jnp.where(diagonal, lse[h, part, :], 0.0), axis=0, keepdims=True)
+        return with_stat(jnp.where(row < FEW, final[h, part, :], 0.0), stat, row)
+
     for q in range(TOKENS // QUARTER):
         for h in range(GH):
-            for b in range(QUARTER // FEW):
-                part = pl.ds(q * QUARTER + b * FEW, 16)
-                stat = jnp.sum(jnp.where(diagonal, lse[h, part, :], 0.0), axis=0, keepdims=True)
-                high, middle, low = split3(stat)
-                block = jnp.where(row < FEW, final[h, part, :], 0.0)
-                block = jnp.where(row == FEW, high, block)
-                block = jnp.where(row == FEW + 1, middle, block)
-                block = jnp.where(row == FEW + 2, low, block)
-                out_ref[q * ffn + h * (QUARTER // FEW) + b] = block.astype(BF16)
-        for target in range(GH * (QUARTER // FEW), ffn):
-            out_ref[q * ffn + target] = jnp.zeros((16, HD), BF16)
+            for b in range(0, per_head, 2):
+                even, uneven = block_of(q, h, b), block_of(q, h, b + 1)
+                target = q * half + (h * per_head + b) // 2
+                keep_ref[target] = jnp.where(odd, uneven, even).astype(BF16)
+                send_ref[target] = jnp.where(odd, even, uneven).astype(BF16)
+        for target in range(GH * per_head // 2, half):
+            keep_ref[q * half + target] = jnp.zeros((16, HD), BF16)
+            send_ref[q * half + target] = jnp.zeros((16, HD), BF16)
+
+
+def with_stat(block, stat, row):
+    high, middle, low = split3(stat)
+    block = jnp.where(row == FEW, high, block)
+    block = jnp.where(row == FEW + 1, middle, block)
+    return jnp.where(row == FEW + 2, low, block)
+
+
+def stat_of(block, row):
+    return jnp.sum(jnp.where(row >= FEW, block.astype(F32), 0.0), axis=0, keepdims=True)
+
+
+def pair_kernel(left_ref, right_ref, out_ref):
+    blocks = out_ref.shape[0]
+    row = rows_of((16, HD))
+    left = jnp.concatenate([stat_of(left_ref[i], row) for i in range(blocks)], axis=0)
+    right = jnp.concatenate([stat_of(right_ref[i], row) for i in range(blocks)], axis=0)
+    top = jnp.maximum(left, right)
+    left = jnp.exp2(left - top)
+    right = jnp.exp2(right - top)
+    total = left + right
+    stats = top + jnp.log2(total)
+    turned = jnp.transpose(jnp.concatenate([left / total, right / total], axis=0))
+    for i in range(blocks):
+        block = turned[:16, i : i + 1] * left_ref[i].astype(F32)
+        block = block + turned[:16, blocks + i : blocks + i + 1] * right_ref[i].astype(F32)
+        block = jnp.where(row < FEW, block, 0.0)
+        out_ref[i] = with_stat(block, stats[i : i + 1], row).astype(BF16)
 
 
 def merge_kernel(in_ref, out_ref):
@@ -421,7 +456,8 @@
         )
         weights = jnp.exp2(stats - jnp.max(stats, axis=0, keepdims=True))
         all_weights.append(weights / jnp.sum(weights, axis=0, keepdims=True))
-    turned = jnp.transpose(jnp.concatenate(all_weights, axis=0))
+    filler = jnp.zeros((HD - groups * sources, HD), F32)
+    turned = jnp.transpose(jnp.concatenate(all_weights + [filler], axis=0))
     pieces = []
     for g in range(groups):
         total = jnp.zeros((16, HD), F32)
@@ -430,16 +466,19 @@
             total = total + turned[:16, source : source + 1] * in_ref[source].astype(F32)
         pieces.append(total[:FEW])
     result = jnp.concatenate(pieces, axis=0).astype(BF16)
-    for s in range(sources):
+    for s in range(out_ref.shape[0]):
         out_ref[s] = result
 
 
-def output_kernel(g_ref, f_ref, in_ref, x_ref, *refs):
+def output_kernel(g_ref, f_ref, mine_ref, theirs_ref, x_ref, *refs):
     *w_refs, own_ref, out_ref, spread, heads, product = refs
     blocks = QUARTER // FEW
     groups = len(w_refs)
+    odd = lax.rem(f_ref[0], 2) == 1
     for source in range(GH * blocks):
-        spread[source, :ROWS, :] = in_ref[source].astype(F32)
+        pair = mine_ref[source // 2].astype(F32), theirs_ref[source // 2].astype(F32)
+        first, second = pair if source % 2 else pair[::-1]
+        spread[source, :ROWS, :] = jnp.where(odd, first, second)
         spread[source, ROWS:, :] = jnp.zeros((16, HD), F32)
     for g in range(groups):
         for h in range(GH):
@@ -670,7 +709,7 @@
     units = PRE * GH
     return call(
         attention_kernel,
-        shape(grp * ffn, 16, HD),
+        (shape(grp * ffn // 2, 16, HD), shape(grp * ffn // 2, 16, HD)),
         [smem] * 4 + [vmem] * 2 + [hbm] * 2,
         [
             pltpu.VMEM((pages, PAGE, GH * HD), BF16),
@@ -686,6 +725,7 @@
             pltpu.VMEM((GH, TOKENS + 16, HD), F32),
             pltpu.VMEM((GH, TOKENS + 16, HD), F32),
         ],
+        out_specs=(vmem, vmem),
     )(lists, lefts, tokens, f1, fresh, own_block, key_cache, value_cache)
 
 
@@ -787,7 +827,7 @@
     def passed(weight, amount):
         return lax.ppermute(weight, "grp", [(i, (i + amount) % grp) for i in range(grp)])
 
-    near = [passed(turned_weight, 1), passed(turned_weight, grp - 1)]
+    near = [passed(turned_weight, 1)]
     partial = lax.all_to_all(partial, "ffn", 0, 0, axis_index_groups=parity)
     partial, *near = lax.optimization_barrier((partial, *near))
     fresh, own_block = call(
@@ -802,24 +842,29 @@
         middle.append(passed(last, 1))
     fresh = swap(fresh, "ffn").reshape(ffn * ROWS, HD)
     fresh, *middle = lax.optimization_barrier((fresh, *middle))
-    message = run_attention(
+    kept, sent = run_attention(
         lists, lefts, tokens, f1, fresh, own_block, key_cache, value_cache, grp, ffn
     )
-    message = swap(message, ("grp", "ffn"))
-    heads = call(merge_kernel, shape(ffn, ROWS, HD), [vmem])(message)
-    heads = swap(heads, "ffn")
-    out_weights = [turned_weight, near[0], *middle, near[1]]
+    received = lax.ppermute(sent, "ffn", neighbour)
+    message = call(pair_kernel, shape(*kept.shape), [vmem] * 2)(kept, received)
+    cores = [[g * ffn + i for g in range(grp) for i in group] for group in parity]
+    message = lax.all_to_all(message, ("grp", "ffn"), 0, 0, axis_index_groups=cores)
+    heads = call(merge_kernel, shape(ffn // 2, ROWS, HD), [vmem])(message)
+    heads = lax.all_to_all(heads, "ffn", 0, 0, axis_index_groups=parity)
+    others = lax.ppermute(heads, "ffn", neighbour)
+    far = passed(out_weight.T, grp - 1)
+    out_weights = [turned_weight, near[0], *middle, far]
     own, rows = call(
         output_kernel,
         (shape(QUARTER, COLS), shape(ffn // 2, MSG, HD)),
-        [smem] * 2 + [vmem] * (2 + grp),
+        [smem] * 2 + [vmem] * (3 + grp),
         [
             pltpu.VMEM((GH * (QUARTER // FEW), ROWS + 16, HD), F32),
             pltpu.VMEM((grp, 16 * (QUARTER // FEW), GH * HD), BF16),
             pltpu.VMEM((QUARTER, COLS), F32),
         ],
         out_specs=(vmem, vmem),
-    )(g1, f1, heads, layer_input, *out_weights)
+    )(g1, f1, heads, others, layer_input, *out_weights)
     gate_up, rows = lax.optimization_barrier((jnp.swapaxes(gate_up_weight, 1, 2), rows))
     mine = lax.all_to_all(rows, "ffn", 0, 0, axis_index_groups=parity)
     ahead = fetched(gate_up)

time: 128 us -> 126 us (0.984)
    all_to_all x2 -> x1, waiting for transfers between devices: 12.8 us -> 2.45 us  [swap(): return lax.all_to_all(value, axis, 0, 0)]
    all_to_all x0 -> x1, waiting for transfers between devices: none -> 6.36 us  [shards(): heads = lax.all_to_all(heads, 'ffn', 0, 0, axis_index_groups=parity)]
    all_to_all x2 -> x1, starting transfers between devices: 12.4 us -> 6.14 us  [swap(): return lax.all_to_all(value, axis, 0, 0)]
    all_to_all x0 -> x1, starting transfers between devices: none -> 3.52 us  [shards(): heads = lax.all_to_all(heads, 'ffn', 0, 0, axis_index_groups=parity)]
    ppermute x0 -> x1, starting transfers between devices: none -> 2.76 us  [shards(): others = lax.ppermute(heads, 'ffn', neighbour)]
    all_to_all x1, waiting for transfers between devices: 0.73 us -> 3 us  [shards(): partial = lax.all_to_all(partial, 'ffn', 0, 0, axis_index_groups=parity)]
    ppermute x3, waiting for transfers between devices: 14.7 us -> 12.7 us  [passed(): lax.ppermute(weight, 'grp', [(i, (i + amount) % grp) for i in range(grp)])]
    ppermute x2 -> x3, waiting for transfers between devices: 1.71 us -> 3.23 us  [shards(): received = lax.ppermute(sent, 'ffn', neighbour)]
  transfers between devices with their start and end apart: 9 -> 11, of which waited for: 7 -> 8; matrix products, arithmetic and copies ran while one was open for 2% -> 3% of each run, Pallas kernels for 3% -> 3%
where the time goes in v5:
time: 126 us
  blocking collectives  42.7 us (34%)
  waiting for transfers between devices  28.7 us (23%)
  starting transfers between devices  26.6 us (21%)
  Pallas kernels  24.3 us (19%)
  other arithmetic  2.95 us (2%)
    pallas_call x12, Pallas kernels, placed(): function(*[pltpu.with_memory_space_constraint(a, pltpu.HBM) if spec is hb...  24.3 us
    all_to_all x1, blocking collectives, shards(): lax.all_to_all(message, ('grp', 'ffn'), 0, 0, axis_index_groups=cores)  17.7 us
    ppermute x3, waiting for transfers between devices, passed(): lax.ppermute(weight, 'grp', [(i, (i + amount) % grp) for i in range(grp)])  12.7 us
    all_to_all x1, blocking collectives, shards(): lax.all_to_all(down_terms, 'ffn', 0, 0, axis_index_groups=parity)  12.5 us
    all_to_all x1, blocking collectives, shards(): mine = lax.all_to_all(rows, 'ffn', 0, 0, axis_index_groups=parity)  12.5 us
    all_to_all x1, starting transfers between devices, shards(): partial = lax.all_to_all(partial, 'ffn', 0, 0, axis_index_groups=parity)  7.69 us
    all_to_all x1, waiting for transfers between devices, shards(): heads = lax.all_to_all(heads, 'ffn', 0, 0, axis_index_groups=parity)  6.36 us
    all_to_all x1, starting transfers between devices, swap(): return lax.all_to_all(value, axis, 0, 0)  6.14 us
  transfers between devices with their start and end apart: 11, of which 8 were waited for; matrix products, arithmetic and copies ran while one was open for 3% of the time, Pallas kernels for 3%

profile of v5, /device:TPU:1, one launch (start us, length us, event | category | flops | bytes accessed | tf_op | source)
XLA Modules:
  0.0 125.8 jit_solution(9536429777126704132)
XLA Ops:
  0.0 1.9 %shard_map.118 = bf16[16,152,128]{2,1,0:T(8,128)(2,1)S(1)} custom-call(s32[1]{0:T(128)S(6)} %sub.21.p_ref, bf16[160,288]{1,0:T(8,128)(2,1)} %bitcast.17, f32[1,160]{1,0:T(1,128)} %bitcast.19, bf16[3,160,640]{2,1,0:T(8,128)(2,1)} %w_hbm.3), custom_call_target="tpu_custom_call" | custom-call | tf_op jit(solution)/shard_map/pallas_call | solution.py:673
  1.9 1.5 %collective-permute-start = (bf16[16,152,128]{2,1,0:T(8,128)(2,1)S(1)}, bf16[16,152,128]{2,1,0:T(8,128)(2,1)S(1)}, u32[]{:S(2)}, u32[]{:S(2)}) collective-permute-start(bf16[16,152,128]{2,1,0:T(8,128)(2,1)S(1)} %shard_map.118), channel_id=1, source_target_pairs={{0,1},{1,0},{2,3},{3,2},{4,5},{5,4},{6,7},{7,6},{8,9},{9,8},{10,11... | collective-permute-start | bytes 1867784 | tf_op jit(solution)/shard_map/ppermute | solution.py:792
  5.8 1.9 %shard_map.119.left_ref = bf16[16,152,128]{2,1,0:T(8,128)(2,1)S(1)} custom-call(s32[1]{0:T(128)S(6)} %rem.32.p_ref, bf16[160,288]{1,0:T(8,128)(2,1)} %bitcast.18, f32[1,160]{1,0:T(1,128)} %bitcast.20, bf16[3,160,640]{2,1,0:T(8,128)(2,1)} %w_hbm.3), custom_call_target="tpu_custom_call" | custom-call | tf_op jit(solution)/shard_map/pallas_call | solution.py:673
  9.0 7.7 %all-to-all-start = ((bf16[16,152,128]{2,1,0:T(8,128)(2,1)}), bf16[16,152,128]{2,1,0:T(8,128)(2,1)S(1)}, u32[]{:S(2)}, u32[]{:S(2)}) async-start(bf16[16,152,128]{2,1,0:T(8,128)(2,1)} %shard_map.120), calls=%async_computation | async-start | bytes 1245184 | tf_op jit(solution)/shard_map/all_to_all | solution.py:831
  17.0 1.4 %collective-permute-start.1 = (bf16[160,640]{1,0:T(8,128)(2,1)S(1)}, bf16[160,640]{1,0:T(8,128)(2,1)S(1)}, u32[]{:S(2)}, u32[]{:S(2)}) collective-permute-start(bf16[160,640]{1,0:T(8,128)(2,1)S(1)} %bitcast.11), channel_id=1, source_target_pairs={{0,32},{32,64},{64,96},{96,0},{1,33},{33,65},{65,97},{97,1},{2,34}... | collective-permute-start | bytes 614408 | tf_op jit(solution)/shard_map/ppermute | solution.py:828
  18.4 6.4 %collective-permute-done.1.refs_1_ = bf16[160,640]{1,0:T(8,128)(2,1)S(1)} collective-permute-done((bf16[160,640]{1,0:T(8,128)(2,1)S(1)}, bf16[160,640]{1,0:T(8,128)(2,1)S(1)}, u32[]{:S(2)}, u32[]{:S(2)}) %collective-permute-start.1) | collective-permute-done | bytes 204832 | tf_op jit(solution)/shard_map/ppermute | solution.py:828
  24.8 3.0 %all-to-all-done.in_ref = bf16[16,152,128]{2,1,0:T(8,128)(2,1)S(1)} async-done(((bf16[16,152,128]{2,1,0:T(8,128)(2,1)}), bf16[16,152,128]{2,1,0:T(8,128)(2,1)S(1)}, u32[]{:S(2)}, u32[]{:S(2)}) %all-to-all-start) | async-done | bytes 622624 | tf_op jit(solution)/shard_map/all_to_all | solution.py:831
  28.7 6.1 %all-to-all-start.1 = ((bf16[32,48,128]{2,1,0:T(8,128)(2,1)}), bf16[32,48,128]{2,1,0:T(8,128)(2,1)S(1)}, u32[]{:S(2)}, u32[]{:S(2)}) async-start(bf16[32,48,128]{2,1,0:T(8,128)(2,1)} %get-tuple-element.39), calls=%async_computation.1 | async-start | bytes 786432 | tf_op jit(solution)/shard_map/all_to_all | solution.py:688
  34.9 1.4 %collective-permute-start.2 = (bf16[160,640]{1,0:T(8,128)(2,1)S(1)}, bf16[160,640]{1,0:T(8,128)(2,1)S(1)}, u32[]{:S(2)}, u32[]{:S(2)}) collective-permute-start(bf16[160,640]{1,0:T(8,128)(2,1)S(1)} %collective-permute-done.1.refs_1_), channel_id=1, source_target_pairs={{0,32},{32,64},{64,96},{96,0},{1,33},{33,65},{65,97},{97,1},{2,34}... | collective-permute-start | bytes 614408 | tf_op jit(solution)/shard_map/ppermute | solution.py:828
  36.5 6.3 %collective-permute-done.2.refs_2_ = bf16[160,640]{1,0:T(8,128)(2,1)S(1)} collective-permute-done((bf16[160,640]{1,0:T(8,128)(2,1)S(1)}, bf16[160,640]{1,0:T(8,128)(2,1)S(1)}, u32[]{:S(2)}, u32[]{:S(2)}) %collective-permute-start.2) | collective-permute-done | bytes 204832 | tf_op jit(solution)/shard_map/ppermute | solution.py:828
  42.8 2.5 %all-to-all-done.1 = bf16[32,48,128]{2,1,0:T(8,128)(2,1)S(1)} async-done(((bf16[32,48,128]{2,1,0:T(8,128)(2,1)}), bf16[32,48,128]{2,1,0:T(8,128)(2,1)S(1)}, u32[]{:S(2)}, u32[]{:S(2)}) %all-to-all-start.1) | async-done | bytes 393248 | tf_op jit(solution)/shard_map/all_to_all | solution.py:688
  45.2 7.7 %shard_map.122 = (bf16[64,16,128]{2,1,0:T(8,128)(2,1)S(1)}, bf16[64,16,128]{2,1,0:T(8,128)(2,1)S(1)}) custom-call(s32[3,34]{1,0:T(4,128)S(1)} %pad_add_fusion.lists, s32[28]{0:T(128)S(1)} %get-tuple-element.59.left_ref, s32[28]{0:T(128)S(1)} %get-tuple-element.61.token_ref, s32[1]{0:T(128)} %bitcast.f_ref, bf16[1536,128]{1,0:T(8,128)(2,1)S(1)} %bitcast.10, ...), custom_call_target="tpu_custom_call" | custom-call | tf_op jit(solution)/shard_map/pallas_call | solution.py:673
  53.1 1.5 %collective-permute-done.3.right_ref = bf16[64,16,128]{2,1,0:T(8,128)(2,1)S(1)} collective-permute-done((bf16[64,16,128]{2,1,0:T(8,128)(2,1)S(1)}, bf16[64,16,128]{2,1,0:T(8,128)(2,1)S(1)}, u32[]{:S(2)}, u32[]{:S(2)}) %collective-permute-start.3) | collective-permute-done | bytes 262176 | tf_op jit(solution)/shard_map/ppermute | solution.py:848
  55.3 17.7 %all_to_all.30.in_ref = bf16[64,16,128]{2,1,0:T(8,128)(2,1)S(1)} all-to-all(bf16[64,16,128]{2,1,0:T(8,128)(2,1)S(1)} %shard_map.123), channel_id=1, replica_groups={{0,2,4,6,8,10,12,14,16,18,20,22,24,26,28,30,32,34,36,38,40,42,44,46,48,..., dimensions={0} | all-to-all | bytes 524288 | tf_op jit(solution)/shard_map/all_to_all | solution.py:851
  73.0 1.2 shard_map.124
  74.2 3.5 %all-to-all-start.3 = ((bf16[16,48,128]{2,1,0:T(8,128)(2,1)}), bf16[16,48,128]{2,1,0:T(8,128)(2,1)S(1)}, u32[]{:S(2)}, u32[]{:S(2)}) async-start(bf16[16,48,128]{2,1,0:T(8,128)(2,1)} %shard_map.124), calls=%async_computation.3 | async-start | bytes 393216 | tf_op jit(solution)/shard_map/all_to_all | solution.py:853
  78.3 6.4 %all-to-all-done.3.mine_ref = bf16[16,48,128]{2,1,0:T(8,128)(2,1)S(1)} async-done(((bf16[16,48,128]{2,1,0:T(8,128)(2,1)}), bf16[16,48,128]{2,1,0:T(8,128)(2,1)S(1)}, u32[]{:S(2)}, u32[]{:S(2)}) %all-to-all-start.3) | async-done | bytes 196640 | tf_op jit(solution)/shard_map/all_to_all | solution.py:853
  84.6 2.8 %collective-permute-start.4 = (bf16[16,48,128]{2,1,0:T(8,128)(2,1)S(1)}, bf16[16,48,128]{2,1,0:T(8,128)(2,1)S(1)}, u32[]{:S(2)}, u32[]{:S(2)}) collective-permute-start(bf16[16,48,128]{2,1,0:T(8,128)(2,1)S(1)} %all-to-all-done.3.mine_ref), channel_id=1, source_target_pairs={{0,1},{1,0},{2,3},{3,2},{4,5},{5,4},{6,7},{7,6},{8,9},{9,8},{10,11... | collective-permute-start | bytes 589832 | tf_op jit(solution)/shard_map/ppermute | solution.py:854
  89.2 12.5 %all_to_all.31.mine_ref = bf16[16,96,128]{2,1,0:T(8,128)(2,1)S(1)} all-to-all(bf16[16,96,128]{2,1,0:T(8,128)(2,1)S(1)} %get-tuple-element.49), channel_id=1, replica_groups={{0,2,4,6,8,10,12,14,16,18,20,22,24,26,28,30},{1,3,5,7,9,11,13,15,17,19,..., dimensions={0} | all-to-all | bytes 786432 | tf_op jit(solution)/shard_map/all_to_all | solution.py:869
  101.7 1.5 %collective-permute-start.6 = (bf16[16,96,128]{2,1,0:T(8,128)(2,1)S(1)}, bf16[16,96,128]{2,1,0:T(8,128)(2,1)S(1)}, u32[]{:S(2)}, u32[]{:S(2)}) collective-permute-start(bf16[16,96,128]{2,1,0:T(8,128)(2,1)S(1)} %all_to_all.31.mine_ref), channel_id=1, source_target_pairs={{0,1},{1,0},{2,3},{3,2},{4,5},{5,4},{6,7},{7,6},{8,9},{9,8},{10,11... | collective-permute-start | bytes 1179656 | tf_op jit(solution)/shard_map/ppermute | solution.py:871
  103.2 1.9 %shard_map.126 = (bf16[2,432,640]{2,1,0:T(8,128)(2,1)S(1)}, bf16[2,432,640]{2,1,0:T(8,128)(2,1)S(1)}, bf16[2,432,640]{2,1,0:T(8,128)(2,1)S(1)}) custom-call(bf16[2,432,5120]{2,1,0:T(8,128)(2,1)} %bitcast.15), custom_call_target="tpu_custom_call" | custom-call | tf_op jit(solution)/shard_map/pallas_call | solution.py:673
  105.2 5.4 %shard_map.127 = (bf16[16,96,128]{2,1,0:T(8,128)(2,1)S(1)}, bf16[16,96,128]{2,1,0:T(8,128)(2,1)S(1)}) custom-call(s32[1]{0:T(128)} %bitcast.f_ref, bf16[16,96,128]{2,1,0:T(8,128)(2,1)S(1)} %all_to_all.31.mine_ref, bf16[16,96,128]{2,1,0:T(8,128)(2,1)S(1)} %collective-permute-done.6.theirs_ref, f32[1,5120]{1,0:T(1,128)S(1)} %bitcast.14, ...), custom_call_target="tpu_custom_call" | custom-call | tf_op jit(solution)/shard_map/pallas_call | solution.py:673
  110.6 1.7 %collective-permute-done.7.right_ref = bf16[16,96,128]{2,1,0:T(8,128)(2,1)S(1)} collective-permute-done((bf16[16,96,128]{2,1,0:T(8,128)(2,1)S(1)}, bf16[16,96,128]{2,1,0:T(8,128)(2,1)S(1)}, u32[]{:S(2)}, u32[]{:S(2)}) %collective-permute-start.7) | collective-permute-done | bytes 393248 | tf_op jit(solution)/shard_map/ppermute | solution.py:875
  112.4 12.5 %all_to_all.32.in_ref = bf16[16,96,128]{2,1,0:T(8,128)(2,1)S(1)} all-to-all(bf16[16,96,128]{2,1,0:T(8,128)(2,1)S(1)} %shard_map.128), channel_id=1, replica_groups={{0,2,4,6,8,10,12,14,16,18,20,22,24,26,28,30},{1,3,5,7,9,11,13,15,17,19,..., dimensions={0} | all-to-all | bytes 786432 | tf_op jit(solution)/shard_map/all_to_all | solution.py:877
  (48 shorter events, 9.2 us)
Async XLA Ops:
  0.0 16.7 %copy-start.3 = (s32[32]{0:T(128)S(1)}, s32[32]{0:T(128)}, u32[]{:S(2)}) copy-start(s32[32]{0:T(128)} %param.22) | copy-start | bytes 388
  0.0 8.9 %copy-start.4 = (s32[2]{0:T(128)S(1)}, s32[2]{0:T(128)}, u32[]{:S(2)}) copy-start(s32[2]{0:T(128)} %param.21) | copy-start | bytes 28
  0.0 17.0 %copy-start = (bf16[640,160]{0,1:T(8,128)(2,1)S(1)}, bf16[640,160]{0,1:T(8,128)(2,1)}, u32[]{:S(2)}) copy-start(bf16[640,160]{0,1:T(8,128)(2,1)} %param.17) | copy-start | bytes 614404
  1.9 6.0 %collective-permute-start = (bf16[16,152,128]{2,1,0:T(8,128)(2,1)S(1)}, bf16[16,152,128]{2,1,0:T(8,128)(2,1)S(1)}, u32[]{:S(2)}, u32[]{:S(2)}) collective-permute-start(bf16[16,152,128]{2,1,0:T(8,128)(2,1)S(1)} %shard_map.118), channel_id=1, source_target_pairs={{0,1},{1,0},{2,3},{3,2},{4,5},{5,4},{6,7},{7,6},{8,9},{9,8},{10,11... | collective-permute-start | bytes 1867784 | tf_op jit(solution)/shard_map/ppermute | solution.py:792
  9.0 18.8 %all-to-all-start = ((bf16[16,152,128]{2,1,0:T(8,128)(2,1)}), bf16[16,152,128]{2,1,0:T(8,128)(2,1)S(1)}, u32[]{:S(2)}, u32[]{:S(2)}) async-start(bf16[16,152,128]{2,1,0:T(8,128)(2,1)} %shard_map.120), calls=%async_computation | async-start | bytes 1245184 | tf_op jit(solution)/shard_map/all_to_all | solution.py:831
  17.0 7.8 %collective-permute-start.1 = (bf16[160,640]{1,0:T(8,128)(2,1)S(1)}, bf16[160,640]{1,0:T(8,128)(2,1)S(1)}, u32[]{:S(2)}, u32[]{:S(2)}) collective-permute-start(bf16[160,640]{1,0:T(8,128)(2,1)S(1)} %bitcast.11), channel_id=1, source_target_pairs={{0,32},{32,64},{64,96},{96,0},{1,33},{33,65},{65,97},{97,1},{2,34}... | collective-permute-start | bytes 614408 | tf_op jit(solution)/shard_map/ppermute | solution.py:828
  28.7 16.5 %all-to-all-start.1 = ((bf16[32,48,128]{2,1,0:T(8,128)(2,1)}), bf16[32,48,128]{2,1,0:T(8,128)(2,1)S(1)}, u32[]{:S(2)}, u32[]{:S(2)}) async-start(bf16[32,48,128]{2,1,0:T(8,128)(2,1)} %get-tuple-element.39), calls=%async_computation.1 | async-start | bytes 786432 | tf_op jit(solution)/shard_map/all_to_all | solution.py:688
  34.9 7.8 %collective-permute-start.2 = (bf16[160,640]{1,0:T(8,128)(2,1)S(1)}, bf16[160,640]{1,0:T(8,128)(2,1)S(1)}, u32[]{:S(2)}, u32[]{:S(2)}) collective-permute-start(bf16[160,640]{1,0:T(8,128)(2,1)S(1)} %collective-permute-done.1.refs_1_), channel_id=1, source_target_pairs={{0,32},{32,64},{64,96},{96,0},{1,33},{33,65},{65,97},{97,1},{2,34}... | collective-permute-start | bytes 614408 | tf_op jit(solution)/shard_map/ppermute | solution.py:828
  45.2 42.2 %copy-start.2 = (bf16[288,160]{0,1:T(8,128)(2,1)S(1)}, bf16[288,160]{0,1:T(8,128)(2,1)}, u32[]{:S(2)}) copy-start(bf16[288,160]{0,1:T(8,128)(2,1)} %param.12) | copy-start | bytes 276484
  53.0 1.6 %collective-permute-start.3 = (bf16[64,16,128]{2,1,0:T(8,128)(2,1)S(1)}, bf16[64,16,128]{2,1,0:T(8,128)(2,1)S(1)}, u32[]{:S(2)}, u32[]{:S(2)}) collective-permute-start(bf16[64,16,128]{2,1,0:T(8,128)(2,1)S(1)} %get-tuple-element.46), channel_id=1, source_target_pairs={{0,1},{1,0},{2,3},{3,2},{4,5},{5,4},{6,7},{7,6},{8,9},{9,8},{10,11... | collective-permute-start | bytes 786440 | tf_op jit(solution)/shard_map/ppermute | solution.py:848
  74.2 10.4 %all-to-all-start.3 = ((bf16[16,48,128]{2,1,0:T(8,128)(2,1)}), bf16[16,48,128]{2,1,0:T(8,128)(2,1)S(1)}, u32[]{:S(2)}, u32[]{:S(2)}) async-start(bf16[16,48,128]{2,1,0:T(8,128)(2,1)} %shard_map.124), calls=%async_computation.3 | async-start | bytes 393216 | tf_op jit(solution)/shard_map/all_to_all | solution.py:853
  77.7 9.8 %collective-permute-start.5 = (bf16[160,640]{1,0:T(8,128)(2,1)S(1)}, bf16[160,640]{1,0:T(8,128)(2,1)S(1)}, u32[]{:S(2)}, u32[]{:S(2)}) collective-permute-start(bf16[160,640]{1,0:T(8,128)(2,1)S(1)} %bitcast.12), channel_id=1, source_target_pairs={{0,96},{32,0},{64,32},{96,64},{1,97},{33,1},{65,33},{97,65},{2,98}... | collective-permute-start | bytes 614408 | tf_op jit(solution)/shard_map/ppermute | solution.py:828
  84.6 3.8 %collective-permute-start.4 = (bf16[16,48,128]{2,1,0:T(8,128)(2,1)S(1)}, bf16[16,48,128]{2,1,0:T(8,128)(2,1)S(1)}, u32[]{:S(2)}, u32[]{:S(2)}) collective-permute-start(bf16[16,48,128]{2,1,0:T(8,128)(2,1)S(1)} %all-to-all-done.3.mine_ref), channel_id=1, source_target_pairs={{0,1},{1,0},{2,3},{3,2},{4,5},{5,4},{6,7},{7,6},{8,9},{9,8},{10,11... | collective-permute-start | bytes 589832 | tf_op jit(solution)/shard_map/ppermute | solution.py:854
  101.7 3.5 %copy-start.1 = (f32[5120]{0:T(1024)S(1)}, f32[5120]{0:T(1024)}, u32[]{:S(2)}) copy-start(f32[5120]{0:T(1024)} %param.18) | copy-start | bytes 61444
  101.7 3.5 %collective-permute-start.6 = (bf16[16,96,128]{2,1,0:T(8,128)(2,1)S(1)}, bf16[16,96,128]{2,1,0:T(8,128)(2,1)S(1)}, u32[]{:S(2)}, u32[]{:S(2)}) collective-permute-start(bf16[16,96,128]{2,1,0:T(8,128)(2,1)S(1)} %all_to_all.31.mine_ref), channel_id=1, source_target_pairs={{0,1},{1,0},{2,3},{3,2},{4,5},{5,4},{6,7},{7,6},{8,9},{9,8},{10,11... | collective-permute-start | bytes 1179656 | tf_op jit(solution)/shard_map/ppermute | solution.py:871
  110.5 1.8 %collective-permute-start.7 = (bf16[16,96,128]{2,1,0:T(8,128)(2,1)S(1)}, bf16[16,96,128]{2,1,0:T(8,128)(2,1)S(1)}, u32[]{:S(2)}, u32[]{:S(2)}) collective-permute-start(bf16[16,96,128]{2,1,0:T(8,128)(2,1)S(1)} %get-tuple-element.55), channel_id=1, source_target_pairs={{0,1},{1,0},{2,3},{3,2},{4,5},{5,4},{6,7},{7,6},{8,9},{9,8},{10,11... | collective-permute-start | bytes 1179656 | tf_op jit(solution)/shard_map/ppermute | solution.py:875

commit v6 on v5

--- a/solution.py
+++ b/solution.py
@@ -788,10 +788,10 @@
 
     core = lax.rem(f1, 2)
     sent = projected(1 - core)
-    core, sent, page_table = lax.optimization_barrier((core, sent, page_table))
+    core, sent = lax.optimization_barrier((core, sent))
     received = lax.ppermute(sent, "ffn", neighbour)
     partial = call(add_kernel, shape(*sent.shape), [vmem] * 2)(projected(core), received)
-    span_rows, partial = lax.optimization_barrier((span_offsets, partial))
+    span_rows, page_table, partial = lax.optimization_barrier((span_offsets, page_table, partial))
     cosine, sine = tables(f, span_rows, decode_lengths)
     local_ids = f * pages + jnp.arange(pages, dtype=jnp.int32)
     requests = PRE + DEC
@@ -823,7 +823,7 @@
     )
     tokens = jnp.clip(owners - PRE, 0, DEC - 1)
 
-    turned_weight, cosine = lax.optimization_barrier((out_weight.T, cosine))
+    turned_weight, cosine, lists = lax.optimization_barrier((out_weight.T, cosine, lists))
     def passed(weight, amount):
         return lax.ppermute(weight, "grp", [(i, (i + amount) % grp) for i in range(grp)])
 

time: 126 us -> 126 us (level)
  transfers between devices with their start and end apart: 11 -> 11, of which waited for: 8 -> 8; matrix products, arithmetic and copies ran while one was open for 3% -> 1% of each run, Pallas kernels for 3% -> 3%
where the time goes in v6:
time: 126 us; the launch traced here: 125 us
  blocking collectives  42.1 us (33%)
  waiting for transfers between devices  28.4 us (23%)
  starting transfers between devices  27.1 us (22%)
  Pallas kernels  24.8 us (20%)
  other arithmetic  2.22 us (2%)
    pallas_call x12, Pallas kernels, placed(): function(*[pltpu.with_memory_space_constraint(a, pltpu.HBM) if spec is hb...  24.8 us
    all_to_all x1, blocking collectives, shards(): lax.all_to_all(message, ('grp', 'ffn'), 0, 0, axis_index_groups=cores)  17.1 us
    ppermute x3, waiting for transfers between devices, passed(): lax.ppermute(weight, 'grp', [(i, (i + amount) % grp) for i in range(grp)])  12.9 us
    all_to_all x1, blocking collectives, shards(): lax.all_to_all(down_terms, 'ffn', 0, 0, axis_index_groups=parity)  12.5 us
    all_to_all x1, blocking collectives, shards(): mine = lax.all_to_all(rows, 'ffn', 0, 0, axis_index_groups=parity)  12.5 us
    all_to_all x1, starting transfers between devices, shards(): partial = lax.all_to_all(partial, 'ffn', 0, 0, axis_index_groups=parity)  7.71 us
    all_to_all x1, waiting for transfers between devices, shards(): heads = lax.all_to_all(heads, 'ffn', 0, 0, axis_index_groups=parity)  6.36 us
    all_to_all x1, starting transfers between devices, swap(): return lax.all_to_all(value, axis, 0, 0)  6.12 us
  transfers between devices with their start and end apart: 11, of which 8 were waited for; matrix products, arithmetic and copies ran while one was open for 1% of the time, Pallas kernels for 3%

profile of v6, /device:TPU:1, one launch (start us, length us, event | category | flops | bytes accessed | tf_op | source)
XLA Modules:
  0.0 125.2 jit_solution(7824398014901543815)
XLA Ops:
  0.0 1.9 %shard_map.118 = bf16[16,152,128]{2,1,0:T(8,128)(2,1)S(1)} custom-call(s32[1]{0:T(128)S(6)} %sub.21.p_ref, bf16[160,288]{1,0:T(8,128)(2,1)} %bitcast.17, f32[1,160]{1,0:T(1,128)} %bitcast.19, bf16[3,160,640]{2,1,0:T(8,128)(2,1)} %w_hbm.3), custom_call_target="tpu_custom_call" | custom-call | tf_op jit(solution)/shard_map/pallas_call | solution.py:673
  1.9 1.5 %collective-permute-start = (bf16[16,152,128]{2,1,0:T(8,128)(2,1)S(1)}, bf16[16,152,128]{2,1,0:T(8,128)(2,1)S(1)}, u32[]{:S(2)}, u32[]{:S(2)}) collective-permute-start(bf16[16,152,128]{2,1,0:T(8,128)(2,1)S(1)} %shard_map.118), channel_id=1, source_target_pairs={{0,1},{1,0},{2,3},{3,2},{4,5},{5,4},{6,7},{7,6},{8,9},{9,8},{10,11... | collective-permute-start | bytes 1867784 | tf_op jit(solution)/shard_map/ppermute | solution.py:792
  3.4 1.9 %shard_map.119.left_ref = bf16[16,152,128]{2,1,0:T(8,128)(2,1)S(1)} custom-call(s32[1]{0:T(128)S(6)} %rem.32.p_ref, bf16[160,288]{1,0:T(8,128)(2,1)} %bitcast.18, f32[1,160]{1,0:T(1,128)} %bitcast.20, bf16[3,160,640]{2,1,0:T(8,128)(2,1)} %w_hbm.3), custom_call_target="tpu_custom_call" | custom-call | tf_op jit(solution)/shard_map/pallas_call | solution.py:673
  8.4 7.7 %all-to-all-start = ((bf16[16,152,128]{2,1,0:T(8,128)(2,1)}), bf16[16,152,128]{2,1,0:T(8,128)(2,1)S(1)}, u32[]{:S(2)}, u32[]{:S(2)}) async-start(bf16[16,152,128]{2,1,0:T(8,128)(2,1)} %shard_map.120), calls=%async_computation | async-start | bytes 1245184 | tf_op jit(solution)/shard_map/all_to_all | solution.py:831
  16.5 1.4 %collective-permute-start.1 = (bf16[160,640]{1,0:T(8,128)(2,1)S(1)}, bf16[160,640]{1,0:T(8,128)(2,1)S(1)}, u32[]{:S(2)}, u32[]{:S(2)}) collective-permute-start(bf16[160,640]{1,0:T(8,128)(2,1)S(1)} %bitcast.11), channel_id=1, source_target_pairs={{0,32},{32,64},{64,96},{96,0},{1,33},{33,65},{65,97},{97,1},{2,34}... | collective-permute-start | bytes 614408 | tf_op jit(solution)/shard_map/ppermute | solution.py:828
  17.9 6.4 %collective-permute-done.1.refs_1_ = bf16[160,640]{1,0:T(8,128)(2,1)S(1)} collective-permute-done((bf16[160,640]{1,0:T(8,128)(2,1)S(1)}, bf16[160,640]{1,0:T(8,128)(2,1)S(1)}, u32[]{:S(2)}, u32[]{:S(2)}) %collective-permute-start.1) | collective-permute-done | bytes 204832 | tf_op jit(solution)/shard_map/ppermute | solution.py:828
  24.3 2.9 %all-to-all-done.in_ref = bf16[16,152,128]{2,1,0:T(8,128)(2,1)S(1)} async-done(((bf16[16,152,128]{2,1,0:T(8,128)(2,1)}), bf16[16,152,128]{2,1,0:T(8,128)(2,1)S(1)}, u32[]{:S(2)}, u32[]{:S(2)}) %all-to-all-start) | async-done | bytes 622624 | tf_op jit(solution)/shard_map/all_to_all | solution.py:831
  28.1 6.1 %all-to-all-start.1 = ((bf16[32,48,128]{2,1,0:T(8,128)(2,1)}), bf16[32,48,128]{2,1,0:T(8,128)(2,1)S(1)}, u32[]{:S(2)}, u32[]{:S(2)}) async-start(bf16[32,48,128]{2,1,0:T(8,128)(2,1)} %get-tuple-element.41), calls=%async_computation.1 | async-start | bytes 786432 | tf_op jit(solution)/shard_map/all_to_all | solution.py:688
  34.2 1.4 %collective-permute-start.2 = (bf16[160,640]{1,0:T(8,128)(2,1)S(1)}, bf16[160,640]{1,0:T(8,128)(2,1)S(1)}, u32[]{:S(2)}, u32[]{:S(2)}) collective-permute-start(bf16[160,640]{1,0:T(8,128)(2,1)S(1)} %collective-permute-done.1.refs_1_), channel_id=1, source_target_pairs={{0,32},{32,64},{64,96},{96,0},{1,33},{33,65},{65,97},{97,1},{2,34}... | collective-permute-start | bytes 614408 | tf_op jit(solution)/shard_map/ppermute | solution.py:828
  35.6 6.5 %collective-permute-done.2.refs_2_ = bf16[160,640]{1,0:T(8,128)(2,1)S(1)} collective-permute-done((bf16[160,640]{1,0:T(8,128)(2,1)S(1)}, bf16[160,640]{1,0:T(8,128)(2,1)S(1)}, u32[]{:S(2)}, u32[]{:S(2)}) %collective-permute-start.2) | collective-permute-done | bytes 204832 | tf_op jit(solution)/shard_map/ppermute | solution.py:828
  42.0 2.5 %all-to-all-done.1 = bf16[32,48,128]{2,1,0:T(8,128)(2,1)S(1)} async-done(((bf16[32,48,128]{2,1,0:T(8,128)(2,1)}), bf16[32,48,128]{2,1,0:T(8,128)(2,1)S(1)}, u32[]{:S(2)}, u32[]{:S(2)}) %all-to-all-start.1) | async-done | bytes 393248 | tf_op jit(solution)/shard_map/all_to_all | solution.py:688
  44.6 8.2 %shard_map.122 = (bf16[64,16,128]{2,1,0:T(8,128)(2,1)S(1)}, bf16[64,16,128]{2,1,0:T(8,128)(2,1)S(1)}) custom-call(s32[3,34]{1,0:T(4,128)S(1)} %pad_add_fusion.1.lists, s32[28]{0:T(128)S(1)} %get-tuple-element.61.left_ref, s32[28]{0:T(128)S(1)} %get-tuple-element.63.token_ref, s32[1]{0:T(128)} %bitcast.f_ref, bf16[1536,128]{1,0:T(8,128)(2,1)S(1)} %bitcast.10, ...), custom_call_target="tpu_custom_call" | custom-call | tf_op jit(solution)/shard_map/pallas_call | solution.py:673
  53.5 1.2 collective-permute-done.3.right_ref
  55.4 17.1 %all_to_all.30.in_ref = bf16[64,16,128]{2,1,0:T(8,128)(2,1)S(1)} all-to-all(bf16[64,16,128]{2,1,0:T(8,128)(2,1)S(1)} %shard_map.123), channel_id=1, replica_groups={{0,2,4,6,8,10,12,14,16,18,20,22,24,26,28,30,32,34,36,38,40,42,44,46,48,..., dimensions={0} | all-to-all | bytes 524288 | tf_op jit(solution)/shard_map/all_to_all | solution.py:851
  72.5 1.2 shard_map.124
  73.7 3.5 %all-to-all-start.3 = ((bf16[16,48,128]{2,1,0:T(8,128)(2,1)}), bf16[16,48,128]{2,1,0:T(8,128)(2,1)S(1)}, u32[]{:S(2)}, u32[]{:S(2)}) async-start(bf16[16,48,128]{2,1,0:T(8,128)(2,1)} %shard_map.124), calls=%async_computation.3 | async-start | bytes 393216 | tf_op jit(solution)/shard_map/all_to_all | solution.py:853
  77.7 6.4 %all-to-all-done.3.mine_ref = bf16[16,48,128]{2,1,0:T(8,128)(2,1)S(1)} async-done(((bf16[16,48,128]{2,1,0:T(8,128)(2,1)}), bf16[16,48,128]{2,1,0:T(8,128)(2,1)S(1)}, u32[]{:S(2)}, u32[]{:S(2)}) %all-to-all-start.3) | async-done | bytes 196640 | tf_op jit(solution)/shard_map/all_to_all | solution.py:853
  84.1 2.8 %collective-permute-start.4 = (bf16[16,48,128]{2,1,0:T(8,128)(2,1)S(1)}, bf16[16,48,128]{2,1,0:T(8,128)(2,1)S(1)}, u32[]{:S(2)}, u32[]{:S(2)}) collective-permute-start(bf16[16,48,128]{2,1,0:T(8,128)(2,1)S(1)} %all-to-all-done.3.mine_ref), channel_id=1, source_target_pairs={{0,1},{1,0},{2,3},{3,2},{4,5},{5,4},{6,7},{7,6},{8,9},{9,8},{10,11... | collective-permute-start | bytes 589832 | tf_op jit(solution)/shard_map/ppermute | solution.py:854
  88.7 12.5 %all_to_all.31.mine_ref = bf16[16,96,128]{2,1,0:T(8,128)(2,1)S(1)} all-to-all(bf16[16,96,128]{2,1,0:T(8,128)(2,1)S(1)} %get-tuple-element.51), channel_id=1, replica_groups={{0,2,4,6,8,10,12,14,16,18,20,22,24,26,28,30},{1,3,5,7,9,11,13,15,17,19,..., dimensions={0} | all-to-all | bytes 786432 | tf_op jit(solution)/shard_map/all_to_all | solution.py:869
  101.1 1.5 %collective-permute-start.6 = (bf16[16,96,128]{2,1,0:T(8,128)(2,1)S(1)}, bf16[16,96,128]{2,1,0:T(8,128)(2,1)S(1)}, u32[]{:S(2)}, u32[]{:S(2)}) collective-permute-start(bf16[16,96,128]{2,1,0:T(8,128)(2,1)S(1)} %all_to_all.31.mine_ref), channel_id=1, source_target_pairs={{0,1},{1,0},{2,3},{3,2},{4,5},{5,4},{6,7},{7,6},{8,9},{9,8},{10,11... | collective-permute-start | bytes 1179656 | tf_op jit(solution)/shard_map/ppermute | solution.py:871
  102.7 1.9 %shard_map.126 = (bf16[2,432,640]{2,1,0:T(8,128)(2,1)S(1)}, bf16[2,432,640]{2,1,0:T(8,128)(2,1)S(1)}, bf16[2,432,640]{2,1,0:T(8,128)(2,1)S(1)}) custom-call(bf16[2,432,5120]{2,1,0:T(8,128)(2,1)} %bitcast.15), custom_call_target="tpu_custom_call" | custom-call | tf_op jit(solution)/shard_map/pallas_call | solution.py:673
  104.6 5.4 %shard_map.127 = (bf16[16,96,128]{2,1,0:T(8,128)(2,1)S(1)}, bf16[16,96,128]{2,1,0:T(8,128)(2,1)S(1)}) custom-call(s32[1]{0:T(128)} %bitcast.f_ref, bf16[16,96,128]{2,1,0:T(8,128)(2,1)S(1)} %all_to_all.31.mine_ref, bf16[16,96,128]{2,1,0:T(8,128)(2,1)S(1)} %collective-permute-done.6.theirs_ref, f32[1,5120]{1,0:T(1,128)S(1)} %bitcast.14, ...), custom_call_target="tpu_custom_call" | custom-call | tf_op jit(solution)/shard_map/pallas_call | solution.py:673
  110.1 1.7 %collective-permute-done.7.right_ref = bf16[16,96,128]{2,1,0:T(8,128)(2,1)S(1)} collective-permute-done((bf16[16,96,128]{2,1,0:T(8,128)(2,1)S(1)}, bf16[16,96,128]{2,1,0:T(8,128)(2,1)S(1)}, u32[]{:S(2)}, u32[]{:S(2)}) %collective-permute-start.7) | collective-permute-done | bytes 393248 | tf_op jit(solution)/shard_map/ppermute | solution.py:875
  111.9 12.5 %all_to_all.32.in_ref = bf16[16,96,128]{2,1,0:T(8,128)(2,1)S(1)} all-to-all(bf16[16,96,128]{2,1,0:T(8,128)(2,1)S(1)} %shard_map.128), channel_id=1, replica_groups={{0,2,4,6,8,10,12,14,16,18,20,22,24,26,28,30},{1,3,5,7,9,11,13,15,17,19,..., dimensions={0} | all-to-all | bytes 786432 | tf_op jit(solution)/shard_map/all_to_all | solution.py:877
  (50 shorter events, 9.1 us)
Async XLA Ops:
  0.0 8.1 %copy-start.4 = (s32[32]{0:T(128)S(1)}, s32[32]{0:T(128)}, u32[]{:S(2)}) copy-start(s32[32]{0:T(128)} %param.22) | copy-start | bytes 388
  0.0 8.0 %copy-start.5 = (s32[2]{0:T(128)S(1)}, s32[2]{0:T(128)}, u32[]{:S(2)}) copy-start(s32[2]{0:T(128)} %param.21) | copy-start | bytes 28
  0.0 7.2 %copy-start.3 = (s32[34,128]{1,0:T(8,128)S(1)}, s32[34,128]{1,0:T(8,128)}, u32[]{:S(2)}) copy-start(s32[34,128]{1,0:T(8,128)} %param.23) | copy-start | bytes 52228
  0.0 16.5 %copy-start = (bf16[640,160]{0,1:T(8,128)(2,1)S(1)}, bf16[640,160]{0,1:T(8,128)(2,1)}, u32[]{:S(2)}) copy-start(bf16[640,160]{0,1:T(8,128)(2,1)} %param.17) | copy-start | bytes 614404
  1.9 4.2 %collective-permute-start = (bf16[16,152,128]{2,1,0:T(8,128)(2,1)S(1)}, bf16[16,152,128]{2,1,0:T(8,128)(2,1)S(1)}, u32[]{:S(2)}, u32[]{:S(2)}) collective-permute-start(bf16[16,152,128]{2,1,0:T(8,128)(2,1)S(1)} %shard_map.118), channel_id=1, source_target_pairs={{0,1},{1,0},{2,3},{3,2},{4,5},{5,4},{6,7},{7,6},{8,9},{9,8},{10,11... | collective-permute-start | bytes 1867784 | tf_op jit(solution)/shard_map/ppermute | solution.py:792
  8.4 18.8 %all-to-all-start = ((bf16[16,152,128]{2,1,0:T(8,128)(2,1)}), bf16[16,152,128]{2,1,0:T(8,128)(2,1)S(1)}, u32[]{:S(2)}, u32[]{:S(2)}) async-start(bf16[16,152,128]{2,1,0:T(8,128)(2,1)} %shard_map.120), calls=%async_computation | async-start | bytes 1245184 | tf_op jit(solution)/shard_map/all_to_all | solution.py:831
  16.5 7.7 %collective-permute-start.1 = (bf16[160,640]{1,0:T(8,128)(2,1)S(1)}, bf16[160,640]{1,0:T(8,128)(2,1)S(1)}, u32[]{:S(2)}, u32[]{:S(2)}) collective-permute-start(bf16[160,640]{1,0:T(8,128)(2,1)S(1)} %bitcast.11), channel_id=1, source_target_pairs={{0,32},{32,64},{64,96},{96,0},{1,33},{33,65},{65,97},{97,1},{2,34}... | collective-permute-start | bytes 614408 | tf_op jit(solution)/shard_map/ppermute | solution.py:828
  28.1 16.5 %all-to-all-start.1 = ((bf16[32,48,128]{2,1,0:T(8,128)(2,1)}), bf16[32,48,128]{2,1,0:T(8,128)(2,1)S(1)}, u32[]{:S(2)}, u32[]{:S(2)}) async-start(bf16[32,48,128]{2,1,0:T(8,128)(2,1)} %get-tuple-element.41), calls=%async_computation.1 | async-start | bytes 786432 | tf_op jit(solution)/shard_map/all_to_all | solution.py:688
  34.2 7.8 %collective-permute-start.2 = (bf16[160,640]{1,0:T(8,128)(2,1)S(1)}, bf16[160,640]{1,0:T(8,128)(2,1)S(1)}, u32[]{:S(2)}, u32[]{:S(2)}) collective-permute-start(bf16[160,640]{1,0:T(8,128)(2,1)S(1)} %collective-permute-done.1.refs_1_), channel_id=1, source_target_pairs={{0,32},{32,64},{64,96},{96,0},{1,33},{33,65},{65,97},{97,1},{2,34}... | collective-permute-start | bytes 614408 | tf_op jit(solution)/shard_map/ppermute | solution.py:828
  44.6 42.3 %copy-start.2 = (bf16[288,160]{0,1:T(8,128)(2,1)S(1)}, bf16[288,160]{0,1:T(8,128)(2,1)}, u32[]{:S(2)}) copy-start(bf16[288,160]{0,1:T(8,128)(2,1)} %param.12) | copy-start | bytes 276484
  52.8 1.8 %collective-permute-start.3 = (bf16[64,16,128]{2,1,0:T(8,128)(2,1)S(1)}, bf16[64,16,128]{2,1,0:T(8,128)(2,1)S(1)}, u32[]{:S(2)}, u32[]{:S(2)}) collective-permute-start(bf16[64,16,128]{2,1,0:T(8,128)(2,1)S(1)} %get-tuple-element.48), channel_id=1, source_target_pairs={{0,1},{1,0},{2,3},{3,2},{4,5},{5,4},{6,7},{7,6},{8,9},{9,8},{10,11... | collective-permute-start | bytes 786440 | tf_op jit(solution)/shard_map/ppermute | solution.py:848
  73.7 10.4 %all-to-all-start.3 = ((bf16[16,48,128]{2,1,0:T(8,128)(2,1)}), bf16[16,48,128]{2,1,0:T(8,128)(2,1)S(1)}, u32[]{:S(2)}, u32[]{:S(2)}) async-start(bf16[16,48,128]{2,1,0:T(8,128)(2,1)} %shard_map.124), calls=%async_computation.3 | async-start | bytes 393216 | tf_op jit(solution)/shard_map/all_to_all | solution.py:853
  77.2 9.8 %collective-permute-start.5 = (bf16[160,640]{1,0:T(8,128)(2,1)S(1)}, bf16[160,640]{1,0:T(8,128)(2,1)S(1)}, u32[]{:S(2)}, u32[]{:S(2)}) collective-permute-start(bf16[160,640]{1,0:T(8,128)(2,1)S(1)} %bitcast.12), channel_id=1, source_target_pairs={{0,96},{32,0},{64,32},{96,64},{1,97},{33,1},{65,33},{97,65},{2,98}... | collective-permute-start | bytes 614408 | tf_op jit(solution)/shard_map/ppermute | solution.py:828
  84.1 3.8 %collective-permute-start.4 = (bf16[16,48,128]{2,1,0:T(8,128)(2,1)S(1)}, bf16[16,48,128]{2,1,0:T(8,128)(2,1)S(1)}, u32[]{:S(2)}, u32[]{:S(2)}) collective-permute-start(bf16[16,48,128]{2,1,0:T(8,128)(2,1)S(1)} %all-to-all-done.3.mine_ref), channel_id=1, source_target_pairs={{0,1},{1,0},{2,3},{3,2},{4,5},{5,4},{6,7},{7,6},{8,9},{9,8},{10,11... | collective-permute-start | bytes 589832 | tf_op jit(solution)/shard_map/ppermute | solution.py:854
  101.1 3.5 %copy-start.1 = (f32[5120]{0:T(1024)S(1)}, f32[5120]{0:T(1024)}, u32[]{:S(2)}) copy-start(f32[5120]{0:T(1024)} %param.18) | copy-start | bytes 61444
  101.1 3.5 %collective-permute-start.6 = (bf16[16,96,128]{2,1,0:T(8,128)(2,1)S(1)}, bf16[16,96,128]{2,1,0:T(8,128)(2,1)S(1)}, u32[]{:S(2)}, u32[]{:S(2)}) collective-permute-start(bf16[16,96,128]{2,1,0:T(8,128)(2,1)S(1)} %all_to_all.31.mine_ref), channel_id=1, source_target_pairs={{0,1},{1,0},{2,3},{3,2},{4,5},{5,4},{6,7},{7,6},{8,9},{9,8},{10,11... | collective-permute-start | bytes 1179656 | tf_op jit(solution)/shard_map/ppermute | solution.py:871
  110.0 1.8 %collective-permute-start.7 = (bf16[16,96,128]{2,1,0:T(8,128)(2,1)S(1)}, bf16[16,96,128]{2,1,0:T(8,128)(2,1)S(1)}, u32[]{:S(2)}, u32[]{:S(2)}) collective-permute-start(bf16[16,96,128]{2,1,0:T(8,128)(2,1)S(1)} %get-tuple-element.57), channel_id=1, source_target_pairs={{0,1},{1,0},{2,3},{3,2},{4,5},{5,4},{6,7},{7,6},{8,9},{9,8},{10,11... | collective-permute-start | bytes 1179656 | tf_op jit(solution)/shard_map/ppermute | solution.py:875
